TPU v7x, 512 devices: a whole 4x8x8 slice. The times are simulated.
512 devices in a mesh: seq: 128 (over y, x_lo, z), ch: 4 (over x_hi, core).
Axes of the slice: x: 4 (x_hi: 2, x_lo: 2; x = x_hi * 2 + x_lo), y: 8, z: 8, core: 2. Of those that a mesh axis runs over, the one named last changes fastest.
Arguments:
- signal_x: bfloat16 [64, 65536], P('ch', 'seq'), may hold values from -6 to 6
- gate_q: bfloat16 [64, 65536], P('ch', 'seq'), may hold values from -6 to 6
- gate_k: bfloat16 [64, 65536], P('ch', 'seq'), may hold values from -6 to 6
- skip_gain: float32 [64], P('ch'), may hold values from 0.5 to 1.5
- residue: float32 [16], replicated, may hold values from -1.5 to 1.5
- memory: float32 [16], replicated, may hold values from 30 to 262144
- cotangent: bfloat16 [64, 65536], P('ch', 'seq'), may hold values from -6 to 6
Outputs:
- output: bfloat16 [64, 65536], P('ch', 'seq')
- grad_x: bfloat16 [64, 65536], P('ch', 'seq')
- grad_q: bfloat16 [64, 65536], P('ch', 'seq')
- grad_k: bfloat16 [64, 65536], P('ch', 'seq')
- grad_skip: float32 [64], P('ch')
- grad_residue: float32 [16], replicated
- grad_memory: float32 [16], replicated
All inputs are finite; a program needn't handle non-finite values.
Results may differ from a plain program's by a relative error of at most 0.002.
Values sent between devices are 32-bit elements; how exact they have to be, the bound alone decides.
A program may use at most 64 MiB of HBM per device.

v0:
```python
import math

import jax
import jax.numpy as jnp
from jax import lax
from jax.sharding import PartitionSpec as P

HIGH_PREC = lax.Precision.HIGHEST


def partner_2(shard, axis, stride):
    return lax.ppermute(shard, axis, [(i, i ^ 1 << stride) for i in range(lax.axis_size(axis))])


def cmul(left_op, right_op):
    return jnp.stack(
        [
            left_op[0] * right_op[0] - left_op[1] * right_op[1],
            left_op[0] * right_op[1] + left_op[1] * right_op[0],
        ]
    )


def dft_pair(order_len, orient):
    indices = jnp.arange(order_len, dtype=jnp.int32)
    products = indices[:, None] * indices[None, :] % order_len
    angles = products.astype(jnp.float32) * (2.0 * math.pi / order_len)
    return (jnp.cos(angles), orient * jnp.sin(angles))


def apply_matrix(signal_data, matrix_pair, pattern):
    with_cos = jnp.einsum(pattern, signal_data, matrix_pair[0], precision=HIGH_PREC)
    with_sin = jnp.einsum(pattern, signal_data, matrix_pair[1], precision=HIGH_PREC)
    return jnp.stack([with_cos[0] - with_sin[1], with_sin[0] + with_cos[1]])


def split_factor(local_len):
    chosen = 1
    factor = 1
    while factor * factor <= local_len:
        if local_len % factor == 0:
            chosen = factor
        factor = factor + 1
    return chosen


def inner_twiddle(outer_len, inner_len, orient):
    local_len = outer_len * inner_len
    rows_idx = jnp.arange(outer_len, dtype=jnp.int32)
    cols_idx = jnp.arange(inner_len, dtype=jnp.int32)
    products = rows_idx[:, None] * cols_idx[None, :] % local_len
    angles = products.astype(jnp.float32) * (2.0 * math.pi / local_len)
    return jnp.stack([jnp.cos(angles), orient * jnp.sin(angles)])[:, None, None]


def local_forward(signal_data):
    local_len = signal_data.shape[-1]
    outer_len = split_factor(local_len)
    inner_len = local_len // outer_len
    shaped = signal_data.reshape(signal_data.shape[:3] + (outer_len, inner_len))
    shaped = apply_matrix(shaped, dft_pair(outer_len, -1.0), "zsxab,ak->zsxkb")
    shaped = cmul(shaped, inner_twiddle(outer_len, inner_len, -1.0))
    shaped = apply_matrix(shaped, dft_pair(inner_len, -1.0), "zsxkb,bc->zsxkc")
    return shaped.reshape(signal_data.shape)


def local_inverse(signal_data):
    local_len = signal_data.shape[-1]
    outer_len = split_factor(local_len)
    inner_len = local_len // outer_len
    shaped = signal_data.reshape(signal_data.shape[:3] + (outer_len, inner_len))
    shaped = apply_matrix(shaped, dft_pair(inner_len, 1.0), "zsxkc,cb->zsxkb")
    shaped = cmul(shaped, inner_twiddle(outer_len, inner_len, 1.0))
    shaped = apply_matrix(shaped, dft_pair(outer_len, 1.0), "zsxkb,kj->zsxjb")
    return shaped.reshape(signal_data.shape)


def global_twiddle(freq_block, local_len, full_len, orient):
    slot_ids = jnp.arange(2, dtype=jnp.int32)
    freq_ids = 2 * freq_block + slot_ids
    products = freq_ids[:, None] * jnp.arange(local_len, dtype=jnp.int32)[None, :]
    angles = products.astype(jnp.float32) * (2.0 * math.pi / full_len)
    return jnp.stack([jnp.cos(angles), orient * jnp.sin(angles)])[:, None]


def bit_reverse(seq_index, sections):
    reversed_idx = jnp.zeros((), jnp.int32)
    for bit_level in range(sections):
        reversed_idx = reversed_idx | (seq_index >> bit_level & 1) << sections - 1 - bit_level
    return reversed_idx


def level_weight(seq_index, bit_level, orient):
    offset = seq_index & (1 << bit_level) - 1
    angles = offset.astype(jnp.float32) * (2.0 * math.pi / 2 ** (bit_level + 1))
    is_upper = seq_index >> bit_level & 1
    return (jnp.stack([jnp.cos(angles), orient * jnp.sin(angles)]), is_upper)


def forward_partners(signal_data, sections):
    seq_index = lax.axis_index("seq")
    for bit_level in range(sections - 1, -1, -1):
        partner = partner_2(signal_data, "seq", bit_level)
        weight, is_upper = level_weight(seq_index, bit_level, -1.0)
        summed = signal_data + partner
        differ = cmul(partner - signal_data, weight)
        signal_data = jnp.where(is_upper == 1, differ, summed)
    return signal_data


def inverse_partners(signal_data, sections):
    seq_index = lax.axis_index("seq")
    for bit_level in range(sections):
        partner = partner_2(signal_data, "seq", bit_level)
        weight, is_upper = level_weight(seq_index, bit_level, 1.0)
        lower_new = signal_data + cmul(partner, weight)
        upper_new = partner - cmul(signal_data, weight)
        signal_data = jnp.where(is_upper == 1, upper_new, lower_new)
    return signal_data


def forward_transform(signals, sections):
    seq_index = lax.axis_index("seq")
    devices = lax.axis_size("seq")
    local_len = signals.shape[-1]
    full_len = 2 * devices * local_len
    angles = seq_index.astype(jnp.float32) * (math.pi / devices)
    weight = jnp.stack([jnp.cos(angles), -jnp.sin(angles)])
    signal_data = jnp.stack([signals, cmul(signals, weight)], axis=2)
    signal_data = forward_partners(signal_data, sections)
    freq_block = bit_reverse(seq_index, sections)
    signal_data = cmul(signal_data, global_twiddle(freq_block, local_len, full_len, -1.0))
    return local_forward(signal_data)


def inverse_transform(spectra, sections):
    seq_index = lax.axis_index("seq")
    devices = lax.axis_size("seq")
    local_len = spectra.shape[-1]
    full_len = 2 * devices * local_len
    signal_data = local_inverse(spectra)
    freq_block = bit_reverse(seq_index, sections)
    signal_data = cmul(signal_data, global_twiddle(freq_block, local_len, full_len, 1.0))
    signal_data = inverse_partners(signal_data, sections)
    angles = seq_index.astype(jnp.float32) * (math.pi / devices)
    weight = jnp.stack([jnp.cos(angles), jnp.sin(angles)])
    result = signal_data[:, :, 0] + cmul(signal_data[:, :, 1], weight)
    return result / full_len


def per_device(signal_x, gate_q, gate_k, skip_gain, residue, memory, cotangent):
    channels, local_len = signal_x.shape
    devices = lax.axis_size("seq")
    sections = devices.bit_length() - 1
    seq_index = lax.axis_index("seq")
    positions = (seq_index * local_len + jnp.arange(local_len, dtype=jnp.int32)).astype(jnp.float32)
    weights = jnp.sqrt(2.0 / memory)[:, None] * jnp.exp(-positions[None, :] / memory[:, None])
    filter_taps = jnp.sum(residue[:, None] * weights, axis=0)
    x_float = signal_x.astype(jnp.float32)
    q_float = gate_q.astype(jnp.float32)
    k_float = gate_k.astype(jnp.float32)
    d_float = cotangent.astype(jnp.float32)
    values = x_float * k_float
    grad_mixed = d_float * q_float
    value_sig = jnp.stack([values, jnp.zeros_like(values)])
    grad_sig = jnp.stack([grad_mixed, jnp.zeros_like(grad_mixed)])
    sig_count = value_sig.shape[1]
    taps_sig = jnp.stack([filter_taps, jnp.zeros_like(filter_taps)])[:, None]
    spectra = forward_transform(jnp.concatenate([value_sig, taps_sig], axis=1), sections)
    value_spec = spectra[:, :sig_count]
    taps_spec = spectra[:, sig_count:]
    conv_sig = inverse_transform(cmul(value_spec, taps_spec), sections)
    grad_spec = forward_transform(grad_sig, sections)
    conj_sign = jnp.array([1.0, -1.0], jnp.float32).reshape(2, 1, 1, 1)
    back_spec = cmul(taps_spec * conj_sign, grad_spec)
    cross_spec = jnp.sum(cmul(value_spec * conj_sign, grad_spec), axis=1, keepdims=True)
    back_sig = inverse_transform(jnp.concatenate([back_spec, cross_spec], axis=1), sections)
    grad_taps = back_sig[0, sig_count]
    conv_out = conv_sig[0]
    corr_out = back_sig[0, :sig_count]
    mixed_out = conv_out + skip_gain[:, None] * values
    output = (q_float * mixed_out).astype(jnp.bfloat16)
    grad_values = skip_gain[:, None] * grad_mixed + corr_out
    grad_x = (grad_values * k_float).astype(jnp.bfloat16)
    grad_q = (d_float * mixed_out).astype(jnp.bfloat16)
    grad_k = (grad_values * x_float).astype(jnp.bfloat16)
    weighted = weights * grad_taps[None, :]
    part_residue = jnp.sum(weighted, axis=1)
    part_memory = residue * jnp.sum(weighted * (positions[None, :] / memory[:, None] - 0.5), axis=1)
    part_skip = jnp.sum(grad_mixed * values, axis=1)
    all_channels = channels * lax.axis_size("ch")
    seq_total = devices * local_len
    sum_residue, sum_memory = lax.psum((part_residue, part_memory), ("seq", "ch"))
    sum_skip = lax.psum(part_skip, "seq")
    norm_scale = 1.0 / math.sqrt(all_channels * seq_total)
    grad_skip = sum_skip / math.sqrt(seq_total)
    grad_residue = sum_residue * norm_scale
    grad_memory = sum_memory * norm_scale
    return (output, grad_x, grad_q, grad_k, grad_skip, grad_residue, grad_memory)


def solution(mesh):
    return jax.shard_map(
        per_device,
        mesh=mesh,
        in_specs=(
            P("ch", "seq"),
            P("ch", "seq"),
            P("ch", "seq"),
            P("ch"),
            P(),
            P(),
            P("ch", "seq"),
        ),
        out_specs=(
            P("ch", "seq"),
            P("ch", "seq"),
            P("ch", "seq"),
            P("ch", "seq"),
            P("ch"),
            P(),
            P(),
        ),
        check_vma=False,
    )
```

profile of v0, /device:TPU:4, one launch (start us, length us, event | category | flops | bytes accessed | tf_op | source)
XLA Modules:
  0.0 616.5 jit_solution(16483242981298394517)
XLA Ops:
  0.8 0.6 copy-done.6
  2.3 7.7 %collective-permute-start = (f32[2,17,2,512]{3,1,2,0:T(8,128)S(1)}, f32[2,17,2,512]{3,1,2,0:T(8,128)S(1)}, u32[]{:S(2)}, u32[]{:S(2)}) collective-permute-start(f32[2,17,2,512]{3,1,2,0:T(8,128)S(1)} %pad_maximum_fusion.13), channel_id=1, source_target_pairs={{0,256},{4,260},{8,264},{12,268},{16,272},{20,276},{24,280},{28,28... | collective-permute-start | bytes 417800 | tf_op jit(solution)/shard_map/ppermute | solution.py:12
  10.1 2.0 collective-permute-start.14
  13.4 10.8 %collective-permute-done.14 = f32[2,16,2,512]{3,1,0,2:T(8,128)S(1)} collective-permute-done((f32[2,16,2,512]{3,1,0,2:T(8,128)S(1)}, f32[2,16,2,512]{3,1,0,2:T(8,128)S(1)}, u32[]{:S(2)}, u32[]{:S(2)}) %collective-permute-start.14) | collective-permute-done | bytes 131104 | tf_op jit(solution)/shard_map/ppermute | solution.py:12
  24.4 4.9 collective-permute-start.15
  29.4 1.9 collective-permute-start.1
  31.4 7.9 %collective-permute-done.15 = f32[2,16,2,512]{3,1,0,2:T(8,128)S(1)} collective-permute-done((f32[2,16,2,512]{3,1,0,2:T(8,128)S(1)}, f32[2,16,2,512]{3,1,0,2:T(8,128)S(1)}, u32[]{:S(2)}, u32[]{:S(2)}) %collective-permute-start.15) | collective-permute-done | bytes 131104 | tf_op jit(solution)/shard_map/ppermute | solution.py:12
  39.4 1.9 collective-permute-start.16
  41.3 1.8 collective-permute-done.1
  43.3 2.1 collective-permute-start.2
  45.5 0.8 collective-permute-done.16
  46.3 3.1 collective-permute-start.17
  49.4 2.4 collective-permute-done.2
  51.9 3.1 collective-permute-start.3
  55.1 10.9 %collective-permute-start.18 = (f32[2,16,2,512]{3,1,0,2:T(8,128)S(1)}, f32[2,16,2,512]{3,1,0,2:T(8,128)S(1)}, u32[]{:S(2)}, u32[]{:S(2)}) collective-permute-start(f32[2,16,2,512]{3,1,0,2:T(8,128)S(1)} %maximum_select_fusion.10), channel_id=1, source_target_pairs={{0,16},{4,20},{8,24},{12,28},{16,0},{20,4},{24,8},{28,12},{32,48},... | collective-permute-start | bytes 393224 | tf_op jit(solution)/shard_map/ppermute | solution.py:12
  66.2 4.3 collective-permute-start.4
  70.8 7.4 %collective-permute-start.19 = (f32[2,16,2,512]{3,1,0,2:T(8,128)S(1)}, f32[2,16,2,512]{3,1,0,2:T(8,128)S(1)}, u32[]{:S(2)}, u32[]{:S(2)}) collective-permute-start(f32[2,16,2,512]{3,1,0,2:T(8,128)S(1)} %maximum_select_fusion.11), channel_id=1, source_target_pairs={{0,8},{4,12},{8,0},{12,4},{16,24},{20,28},{24,16},{28,20},{32,40},... | collective-permute-start | bytes 393224 | tf_op jit(solution)/shard_map/ppermute | solution.py:12
  78.2 3.5 collective-permute-done.4
  81.8 4.0 collective-permute-start.5
  85.8 3.4 collective-permute-done.19
  89.3 2.0 collective-permute-start.20
  91.3 4.3 collective-permute-done.5
  95.7 2.1 collective-permute-start.6
  98.9 0.6 convolution_bitcast_fusion.4
  99.5 0.6 convolution_bitcast_fusion.5
  100.1 4.2 collective-permute-done.6
  105.0 0.6 convolution_bitcast_fusion.2
  105.6 0.6 convolution_bitcast_fusion.3
  106.4 1.1 fusion
  107.5 1.1 fusion.2
  109.6 0.6 fusion.46
  110.2 0.6 fusion.52
  111.1 0.6 fusion.4
  111.7 0.6 fusion.5
  112.4 0.6 copy-done.4
  114.1 0.7 fusion.7
  114.8 0.7 fusion.6
  115.6 0.9 convolution_bitcast_fusion.1
  116.5 0.6 convolution_bitcast_fusion
  118.9 2.2 collective-permute-start.21
  121.6 3.6 collective-permute-start.7
  125.2 4.2 collective-permute-done.7
  129.5 2.8 collective-permute-start.8
  132.5 3.9 collective-permute-start.22
  136.4 9.4 %collective-permute-done.8 = f32[2,16,2,512]{3,1,0,2:T(8,128)S(1)} collective-permute-done((f32[2,16,2,512]{3,1,0,2:T(8,128)S(1)}, f32[2,16,2,512]{3,1,0,2:T(8,128)S(1)}, u32[]{:S(2)}, u32[]{:S(2)}) %collective-permute-start.8) | collective-permute-done | bytes 131104 | tf_op jit(solution)/shard_map/ppermute | solution.py:12
  145.9 4.5 collective-permute-start.9
  150.6 5.6 collective-permute-start.23
  156.3 1.6 collective-permute-done.9
  157.9 7.1 %collective-permute-start.10 = (f32[2,16,2,512]{3,1,0,2:T(8,128)S(1)}, f32[2,16,2,512]{3,1,0,2:T(8,128)S(1)}, u32[]{:S(2)}, u32[]{:S(2)}) collective-permute-start(f32[2,16,2,512]{3,1,0,2:T(8,128)S(1)} %fusion.17), channel_id=1, source_target_pairs={{0,32},{4,36},{8,40},{12,44},{16,48},{20,52},{24,56},{28,60},{32,0... | collective-permute-start | bytes 393224 | tf_op jit(solution)/shard_map/ppermute | solution.py:12
  165.1 0.7 collective-permute-done.23
  165.9 3.3 collective-permute-start.24
  169.3 3.7 collective-permute-start.11
  173.6 3.3 collective-permute-start.25
  177.0 4.4 collective-permute-start.12
  181.9 4.4 collective-permute-start.26
  186.4 2.8 collective-permute-done.12
  189.2 4.3 collective-permute-start.13
  193.5 4.0 collective-permute-done.26
  197.6 4.7 collective-permute-start.27
  202.5 10.7 %collective-permute-done.27 = f32[2,17,2,512]{3,1,2,0:T(8,128)S(1)} collective-permute-done((f32[2,17,2,512]{3,1,2,0:T(8,128)S(1)}, f32[2,17,2,512]{3,1,2,0:T(8,128)S(1)}, u32[]{:S(2)}, u32[]{:S(2)}) %collective-permute-start.27) | collective-permute-done | bytes 139296 | tf_op jit(solution)/shard_map/ppermute | solution.py:12
  213.6 93.2 %all-reduce.3 = (f32[16]{0:T(128)S(1)}, f32[16]{0:T(128)S(1)}) all-reduce(f32[16]{0:T(128)S(1)} %get-tuple-element.8, f32[16]{0:T(128)S(1)} %mul.2458), channel_id=1, replica_groups=mesh['seq'=128,'ch'=4] {'seq','ch'}, use_global_device_ids=true, to_apply=%region_5.6 | all-reduce | flops 32 | bytes 256 | tf_op jit(solution)/shard_map/psum | solution.py:193
  307.9 0.8 fusion.29
  308.7 0.6 fusion.28
  309.3 306.7 %psum.21 = f32[16]{0:T(128)S(1)} all-reduce(f32[16]{0:T(128)S(1)} %get-tuple-element.130), channel_id=1, replica_groups=mesh['seq'=128,'ch'=4] {'seq'}, use_global_device_ids=true, to_apply=%region_3.4 | all-reduce | flops 16 | bytes 128 | tf_op jit(solution)/shard_map/psum | solution.py:194
  (195 shorter events, 12.9 us)
Async XLA Ops:
  0.8 0.7 copy-start.6
  0.8 0.7 copy-start.7
  1.4 0.7 copy-start.2
  1.5 0.7 copy-start.1
  2.3 7.8 %copy-start = (bf16[16,512]{1,0:T(8,128)(2,1)S(1)}, bf16[16,512]{1,0:T(8,128)(2,1)}, u32[]{:S(2)}) copy-start(bf16[16,512]{1,0:T(8,128)(2,1)} %param.9) | copy-start | bytes 49156
  2.3 7.8 %copy-start.3 = (bf16[16,512]{1,0:T(8,128)(2,1)S(1)}, bf16[16,512]{1,0:T(8,128)(2,1)}, u32[]{:S(2)}) copy-start(bf16[16,512]{1,0:T(8,128)(2,1)} %param.14) | copy-start | bytes 49156
  2.3 27.0 %collective-permute-start = (f32[2,17,2,512]{3,1,2,0:T(8,128)S(1)}, f32[2,17,2,512]{3,1,2,0:T(8,128)S(1)}, u32[]{:S(2)}, u32[]{:S(2)}) collective-permute-start(f32[2,17,2,512]{3,1,2,0:T(8,128)S(1)} %pad_maximum_fusion.13), channel_id=1, source_target_pairs={{0,256},{4,260},{8,264},{12,268},{16,272},{20,276},{24,280},{28,28... | collective-permute-start | bytes 417800 | tf_op jit(solution)/shard_map/ppermute | solution.py:12
  10.1 14.1 %collective-permute-start.14 = (f32[2,16,2,512]{3,1,0,2:T(8,128)S(1)}, f32[2,16,2,512]{3,1,0,2:T(8,128)S(1)}, u32[]{:S(2)}, u32[]{:S(2)}) collective-permute-start(f32[2,16,2,512]{3,1,0,2:T(8,128)S(1)} %pad_maximum_fusion.16), channel_id=1, source_target_pairs={{0,256},{4,260},{8,264},{12,268},{16,272},{20,276},{24,280},{28,28... | collective-permute-start | bytes 393224 | tf_op jit(solution)/shard_map/ppermute | solution.py:12
  24.4 14.9 %collective-permute-start.15 = (f32[2,16,2,512]{3,1,0,2:T(8,128)S(1)}, f32[2,16,2,512]{3,1,0,2:T(8,128)S(1)}, u32[]{:S(2)}, u32[]{:S(2)}) collective-permute-start(f32[2,16,2,512]{3,1,0,2:T(8,128)S(1)} %maximum_select_fusion.7), channel_id=1, source_target_pairs={{0,128},{4,132},{8,136},{12,140},{16,144},{20,148},{24,152},{28,15... | collective-permute-start | bytes 393224 | tf_op jit(solution)/shard_map/ppermute | solution.py:12
  29.4 13.7 %collective-permute-start.1 = (f32[2,17,2,512]{3,1,2,0:T(8,128)S(1)}, f32[2,17,2,512]{3,1,2,0:T(8,128)S(1)}, u32[]{:S(2)}, u32[]{:S(2)}) collective-permute-start(f32[2,17,2,512]{3,1,2,0:T(8,128)S(1)} %maximum_select_fusion), channel_id=1, source_target_pairs={{0,128},{4,132},{8,136},{12,140},{16,144},{20,148},{24,152},{28,15... | collective-permute-start | bytes 417800 | tf_op jit(solution)/shard_map/ppermute | solution.py:12
  39.4 6.9 %collective-permute-start.16 = (f32[2,16,2,512]{3,1,0,2:T(8,128)S(1)}, f32[2,16,2,512]{3,1,0,2:T(8,128)S(1)}, u32[]{:S(2)}, u32[]{:S(2)}) collective-permute-start(f32[2,16,2,512]{3,1,0,2:T(8,128)S(1)} %maximum_select_fusion.8), channel_id=1, source_target_pairs={{0,64},{4,68},{8,72},{12,76},{16,80},{20,84},{24,88},{28,92},{32,9... | collective-permute-start | bytes 393224 | tf_op jit(solution)/shard_map/ppermute | solution.py:12
  43.3 8.5 %collective-permute-start.2 = (f32[2,17,2,512]{3,1,2,0:T(8,128)S(1)}, f32[2,17,2,512]{3,1,2,0:T(8,128)S(1)}, u32[]{:S(2)}, u32[]{:S(2)}) collective-permute-start(f32[2,17,2,512]{3,1,2,0:T(8,128)S(1)} %maximum_select_fusion.1), channel_id=1, source_target_pairs={{0,64},{4,68},{8,72},{12,76},{16,80},{20,84},{24,88},{28,92},{32,9... | collective-permute-start | bytes 417800 | tf_op jit(solution)/shard_map/ppermute | solution.py:12
  46.3 8.7 %collective-permute-start.17 = (f32[2,16,2,512]{3,1,0,2:T(8,128)S(1)}, f32[2,16,2,512]{3,1,0,2:T(8,128)S(1)}, u32[]{:S(2)}, u32[]{:S(2)}) collective-permute-start(f32[2,16,2,512]{3,1,0,2:T(8,128)S(1)} %maximum_select_fusion.9), channel_id=1, source_target_pairs={{0,32},{4,36},{8,40},{12,44},{16,48},{20,52},{24,56},{28,60},{32,0... | collective-permute-start | bytes 393224 | tf_op jit(solution)/shard_map/ppermute | solution.py:12
  51.9 14.1 %collective-permute-start.3 = (f32[2,17,2,512]{3,1,2,0:T(8,128)S(1)}, f32[2,17,2,512]{3,1,2,0:T(8,128)S(1)}, u32[]{:S(2)}, u32[]{:S(2)}) collective-permute-start(f32[2,17,2,512]{3,1,2,0:T(8,128)S(1)} %maximum_select_fusion.2), channel_id=1, source_target_pairs={{0,32},{4,36},{8,40},{12,44},{16,48},{20,52},{24,56},{28,60},{32,0... | collective-permute-start | bytes 417800 | tf_op jit(solution)/shard_map/ppermute | solution.py:12
  55.1 15.6 %collective-permute-start.18 = (f32[2,16,2,512]{3,1,0,2:T(8,128)S(1)}, f32[2,16,2,512]{3,1,0,2:T(8,128)S(1)}, u32[]{:S(2)}, u32[]{:S(2)}) collective-permute-start(f32[2,16,2,512]{3,1,0,2:T(8,128)S(1)} %maximum_select_fusion.10), channel_id=1, source_target_pairs={{0,16},{4,20},{8,24},{12,28},{16,0},{20,4},{24,8},{28,12},{32,48},... | collective-permute-start | bytes 393224 | tf_op jit(solution)/shard_map/ppermute | solution.py:12
  66.2 15.5 %collective-permute-start.4 = (f32[2,17,2,512]{3,1,2,0:T(8,128)S(1)}, f32[2,17,2,512]{3,1,2,0:T(8,128)S(1)}, u32[]{:S(2)}, u32[]{:S(2)}) collective-permute-start(f32[2,17,2,512]{3,1,2,0:T(8,128)S(1)} %maximum_select_fusion.3), channel_id=1, source_target_pairs={{0,16},{4,20},{8,24},{12,28},{16,0},{20,4},{24,8},{28,12},{32,48},... | collective-permute-start | bytes 417800 | tf_op jit(solution)/shard_map/ppermute | solution.py:12
  70.8 18.4 %collective-permute-start.19 = (f32[2,16,2,512]{3,1,0,2:T(8,128)S(1)}, f32[2,16,2,512]{3,1,0,2:T(8,128)S(1)}, u32[]{:S(2)}, u32[]{:S(2)}) collective-permute-start(f32[2,16,2,512]{3,1,0,2:T(8,128)S(1)} %maximum_select_fusion.11), channel_id=1, source_target_pairs={{0,8},{4,12},{8,0},{12,4},{16,24},{20,28},{24,16},{28,20},{32,40},... | collective-permute-start | bytes 393224 | tf_op jit(solution)/shard_map/ppermute | solution.py:12
  81.8 13.8 %collective-permute-start.5 = (f32[2,17,2,512]{3,1,2,0:T(8,128)S(1)}, f32[2,17,2,512]{3,1,2,0:T(8,128)S(1)}, u32[]{:S(2)}, u32[]{:S(2)}) collective-permute-start(f32[2,17,2,512]{3,1,2,0:T(8,128)S(1)} %maximum_select_fusion.4), channel_id=1, source_target_pairs={{0,8},{4,12},{8,0},{12,4},{16,24},{20,28},{24,16},{28,20},{32,40},... | collective-permute-start | bytes 417800 | tf_op jit(solution)/shard_map/ppermute | solution.py:12
  89.3 8.9 %collective-permute-start.20 = (f32[2,16,2,512]{3,1,0,2:T(8,128)S(1)}, f32[2,16,2,512]{3,1,0,2:T(8,128)S(1)}, u32[]{:S(2)}, u32[]{:S(2)}) collective-permute-start(f32[2,16,2,512]{3,1,0,2:T(8,128)S(1)} %maximum_select_fusion.12), channel_id=1, source_target_pairs={{0,4},{4,0},{8,12},{12,8},{16,20},{20,16},{24,28},{28,24},{32,36},... | collective-permute-start | bytes 393224 | tf_op jit(solution)/shard_map/ppermute | solution.py:12
  95.7 8.6 %collective-permute-start.6 = (f32[2,17,2,512]{3,1,2,0:T(8,128)S(1)}, f32[2,17,2,512]{3,1,2,0:T(8,128)S(1)}, u32[]{:S(2)}, u32[]{:S(2)}) collective-permute-start(f32[2,17,2,512]{3,1,2,0:T(8,128)S(1)} %maximum_select_fusion.5), channel_id=1, source_target_pairs={{0,4},{4,0},{8,12},{12,8},{16,20},{20,16},{24,28},{28,24},{32,36},... | collective-permute-start | bytes 417800 | tf_op jit(solution)/shard_map/ppermute | solution.py:12
  112.4 0.7 copy-start.4
  118.9 13.5 %collective-permute-start.21 = (f32[2,17,2,512]{3,1,2,0:T(8,128)S(1)}, f32[2,17,2,512]{3,1,2,0:T(8,128)S(1)}, u32[]{:S(2)}, u32[]{:S(2)}) collective-permute-start(f32[2,17,2,512]{3,1,2,0:T(8,128)S(1)} %pad_maximum_fusion.14), channel_id=1, source_target_pairs={{0,4},{4,0},{8,12},{12,8},{16,20},{20,16},{24,28},{28,24},{32,36},... | collective-permute-start | bytes 417800 | tf_op jit(solution)/shard_map/ppermute | solution.py:12
  121.6 7.9 %collective-permute-start.7 = (f32[2,16,2,512]{3,1,0,2:T(8,128)S(1)}, f32[2,16,2,512]{3,1,0,2:T(8,128)S(1)}, u32[]{:S(2)}, u32[]{:S(2)}) collective-permute-start(f32[2,16,2,512]{3,1,0,2:T(8,128)S(1)} %pad_maximum_fusion.15), channel_id=1, source_target_pairs={{0,4},{4,0},{8,12},{12,8},{16,20},{20,16},{24,28},{28,24},{32,36},... | collective-permute-start | bytes 393224 | tf_op jit(solution)/shard_map/ppermute | solution.py:12
  129.5 16.3 %collective-permute-start.8 = (f32[2,16,2,512]{3,1,0,2:T(8,128)S(1)}, f32[2,16,2,512]{3,1,0,2:T(8,128)S(1)}, u32[]{:S(2)}, u32[]{:S(2)}) collective-permute-start(f32[2,16,2,512]{3,1,0,2:T(8,128)S(1)} %fusion.15), channel_id=1, source_target_pairs={{0,8},{4,12},{8,0},{12,4},{16,24},{20,28},{24,16},{28,20},{32,40},... | collective-permute-start | bytes 393224 | tf_op jit(solution)/shard_map/ppermute | solution.py:12
  132.5 17.9 %collective-permute-start.22 = (f32[2,17,2,512]{3,1,2,0:T(8,128)S(1)}, f32[2,17,2,512]{3,1,2,0:T(8,128)S(1)}, u32[]{:S(2)}, u32[]{:S(2)}) collective-permute-start(f32[2,17,2,512]{3,1,2,0:T(8,128)S(1)} %fusion.8), channel_id=1, source_target_pairs={{0,8},{4,12},{8,0},{12,4},{16,24},{20,28},{24,16},{28,20},{32,40},... | collective-permute-start | bytes 417800 | tf_op jit(solution)/shard_map/ppermute | solution.py:12
  145.9 11.9 %collective-permute-start.9 = (f32[2,16,2,512]{3,1,0,2:T(8,128)S(1)}, f32[2,16,2,512]{3,1,0,2:T(8,128)S(1)}, u32[]{:S(2)}, u32[]{:S(2)}) collective-permute-start(f32[2,16,2,512]{3,1,0,2:T(8,128)S(1)} %fusion.16), channel_id=1, source_target_pairs={{0,16},{4,20},{8,24},{12,28},{16,0},{20,4},{24,8},{28,12},{32,48},... | collective-permute-start | bytes 393224 | tf_op jit(solution)/shard_map/ppermute | solution.py:12
  150.6 15.2 %collective-permute-start.23 = (f32[2,17,2,512]{3,1,2,0:T(8,128)S(1)}, f32[2,17,2,512]{3,1,2,0:T(8,128)S(1)}, u32[]{:S(2)}, u32[]{:S(2)}) collective-permute-start(f32[2,17,2,512]{3,1,2,0:T(8,128)S(1)} %fusion.9), channel_id=1, source_target_pairs={{0,16},{4,20},{8,24},{12,28},{16,0},{20,4},{24,8},{28,12},{32,48},... | collective-permute-start | bytes 417800 | tf_op jit(solution)/shard_map/ppermute | solution.py:12
  157.9 11.3 %collective-permute-start.10 = (f32[2,16,2,512]{3,1,0,2:T(8,128)S(1)}, f32[2,16,2,512]{3,1,0,2:T(8,128)S(1)}, u32[]{:S(2)}, u32[]{:S(2)}) collective-permute-start(f32[2,16,2,512]{3,1,0,2:T(8,128)S(1)} %fusion.17), channel_id=1, source_target_pairs={{0,32},{4,36},{8,40},{12,44},{16,48},{20,52},{24,56},{28,60},{32,0... | collective-permute-start | bytes 393224 | tf_op jit(solution)/shard_map/ppermute | solution.py:12
  165.9 7.6 %collective-permute-start.24 = (f32[2,17,2,512]{3,1,2,0:T(8,128)S(1)}, f32[2,17,2,512]{3,1,2,0:T(8,128)S(1)}, u32[]{:S(2)}, u32[]{:S(2)}) collective-permute-start(f32[2,17,2,512]{3,1,2,0:T(8,128)S(1)} %fusion.10), channel_id=1, source_target_pairs={{0,32},{4,36},{8,40},{12,44},{16,48},{20,52},{24,56},{28,60},{32,0... | collective-permute-start | bytes 417800 | tf_op jit(solution)/shard_map/ppermute | solution.py:12
  169.3 7.6 %collective-permute-start.11 = (f32[2,16,2,512]{3,1,0,2:T(8,128)S(1)}, f32[2,16,2,512]{3,1,0,2:T(8,128)S(1)}, u32[]{:S(2)}, u32[]{:S(2)}) collective-permute-start(f32[2,16,2,512]{3,1,0,2:T(8,128)S(1)} %fusion.18), channel_id=1, source_target_pairs={{0,64},{4,68},{8,72},{12,76},{16,80},{20,84},{24,88},{28,92},{32,9... | collective-permute-start | bytes 393224 | tf_op jit(solution)/shard_map/ppermute | solution.py:12
  173.6 8.2 %collective-permute-start.25 = (f32[2,17,2,512]{3,1,2,0:T(8,128)S(1)}, f32[2,17,2,512]{3,1,2,0:T(8,128)S(1)}, u32[]{:S(2)}, u32[]{:S(2)}) collective-permute-start(f32[2,17,2,512]{3,1,2,0:T(8,128)S(1)} %fusion.11), channel_id=1, source_target_pairs={{0,64},{4,68},{8,72},{12,76},{16,80},{20,84},{24,88},{28,92},{32,9... | collective-permute-start | bytes 417800 | tf_op jit(solution)/shard_map/ppermute | solution.py:12
  177.0 12.1 %collective-permute-start.12 = (f32[2,16,2,512]{3,1,0,2:T(8,128)S(1)}, f32[2,16,2,512]{3,1,0,2:T(8,128)S(1)}, u32[]{:S(2)}, u32[]{:S(2)}) collective-permute-start(f32[2,16,2,512]{3,1,0,2:T(8,128)S(1)} %fusion.19), channel_id=1, source_target_pairs={{0,128},{4,132},{8,136},{12,140},{16,144},{20,148},{24,152},{28,15... | collective-permute-start | bytes 393224 | tf_op jit(solution)/shard_map/ppermute | solution.py:12
  181.9 15.6 %collective-permute-start.26 = (f32[2,17,2,512]{3,1,2,0:T(8,128)S(1)}, f32[2,17,2,512]{3,1,2,0:T(8,128)S(1)}, u32[]{:S(2)}, u32[]{:S(2)}) collective-permute-start(f32[2,17,2,512]{3,1,2,0:T(8,128)S(1)} %fusion.12), channel_id=1, source_target_pairs={{0,128},{4,132},{8,136},{12,140},{16,144},{20,148},{24,152},{28,15... | collective-permute-start | bytes 417800 | tf_op jit(solution)/shard_map/ppermute | solution.py:12
  189.2 13.1 %collective-permute-start.13 = (f32[2,16,2,512]{3,1,0,2:T(8,128)S(1)}, f32[2,16,2,512]{3,1,0,2:T(8,128)S(1)}, u32[]{:S(2)}, u32[]{:S(2)}) collective-permute-start(f32[2,16,2,512]{3,1,0,2:T(8,128)S(1)} %fusion.20), channel_id=1, source_target_pairs={{0,256},{4,260},{8,264},{12,268},{16,272},{20,276},{24,280},{28,28... | collective-permute-start | bytes 393224 | tf_op jit(solution)/shard_map/ppermute | solution.py:12
  197.6 15.6 %collective-permute-start.27 = (f32[2,17,2,512]{3,1,2,0:T(8,128)S(1)}, f32[2,17,2,512]{3,1,2,0:T(8,128)S(1)}, u32[]{:S(2)}, u32[]{:S(2)}) collective-permute-start(f32[2,17,2,512]{3,1,2,0:T(8,128)S(1)} %fusion.13), channel_id=1, source_target_pairs={{0,256},{4,260},{8,264},{12,268},{16,272},{20,276},{24,280},{28,28... | collective-permute-start | bytes 417800 | tf_op jit(solution)/shard_map/ppermute | solution.py:12
  307.3 0.7 copy-start.5
where the time goes:
time: 618 us; the launch traced here: 617 us
  blocking collectives  400 us (65%)
  starting transfers between devices  115 us (19%)
  waiting for transfers between devices  73.9 us (12%)
  matrix products  11.2 us (2%)
  other arithmetic  7.95 us (1%)
    psum x1, blocking collectives, per_device(): sum_skip = lax.psum(part_skip, 'seq')  307 us
    ppermute x28, starting transfers between devices, partner_2(): lax.ppermute(shard, axis, [(i, i ^ 1 << stride) for i in range(lax.axis_s...  115 us
    psum x1, blocking collectives, per_device(): lax.psum((part_residue, part_memory), ('seq', 'ch'))  93.2 us
    ppermute x28, waiting for transfers between devices, partner_2(): lax.ppermute(shard, axis, [(i, i ^ 1 << stride) for i in range(lax.axis_s...  73.9 us
  transfers between devices with their start and end apart: 28, of which 20 were waited for; matrix products, arithmetic and copies ran while one was open for 1% of the time, Pallas kernels for 0%

commit v1 on v0

v1 whole, which is shorter than its diff:
```python
import math

import jax
import jax.numpy as jnp
from jax import lax
from jax.sharding import PartitionSpec as P

HIGH_PREC = lax.Precision.HIGHEST


def mm(pattern, left_op, right_op):
    return jnp.einsum(pattern, left_op, right_op, precision=HIGH_PREC)


def exchange(shard, axis, bit):
    size = lax.axis_size(axis)
    return lax.ppermute(shard, axis, [(i, i ^ (1 << bit)) for i in range(size)])


def decay(blocks, block_len, inv_m):
    return jnp.exp(-(blocks * block_len).astype(jnp.float32) * inv_m)


def state_scan(fwd, fwd_m, bwd, inv_m, block_len):
    seq_index = lax.axis_index("seq")
    sections = lax.axis_size("seq").bit_length() - 1
    pre = jnp.zeros_like(fwd)
    pre_m = jnp.zeros_like(fwd)
    post = jnp.zeros_like(bwd)
    for bit in range(sections):
        size = 1 << bit
        recv = exchange(jnp.stack([fwd, fwd_m, bwd]), "seq", bit)
        o_fwd, o_fwd_m, o_bwd = recv[0], recv[1], recv[2]
        rank = seq_index % size
        upper = (seq_index >> bit) & 1
        lag = decay(rank, block_len, inv_m)
        lead = decay(size - 1 - rank, block_len, inv_m)
        whole = jnp.exp(-float(size * block_len) * inv_m)
        shift = float(size * block_len)
        lag_len = (rank * block_len).astype(jnp.float32)
        pre = jnp.where(upper == 1, pre + lag * o_fwd, pre)
        pre_m = jnp.where(upper == 1, pre_m + lag * (o_fwd_m + lag_len * o_fwd), pre_m)
        post = jnp.where(upper == 1, post, post + lead * o_bwd)
        lo_f, lo_fm = jnp.where(upper == 1, o_fwd, fwd), jnp.where(upper == 1, o_fwd_m, fwd_m)
        hi_f, hi_fm = jnp.where(upper == 1, fwd, o_fwd), jnp.where(upper == 1, fwd_m, o_fwd_m)
        lo_b, hi_b = jnp.where(upper == 1, o_bwd, bwd), jnp.where(upper == 1, bwd, o_bwd)
        fwd = whole * lo_f + hi_f
        fwd_m = whole * (lo_fm + shift * lo_f) + hi_fm
        bwd = lo_b + whole * hi_b
    return pre, pre_m, post


def butterfly_sum(value, axis):
    sections = lax.axis_size(axis).bit_length() - 1
    for bit in range(sections):
        value = value + exchange(value, axis, bit)
    return value


def per_device(signal_x, gate_q, gate_k, skip_gain, residue, memory, cotangent):
    channels, block_len = signal_x.shape
    seq_total = lax.axis_size("seq") * block_len
    all_channels = channels * lax.axis_size("ch")
    inv_m = 1.0 / memory
    gain = jnp.sqrt(2.0 / memory)
    amp = residue * gain
    offs = jnp.arange(block_len, dtype=jnp.float32)[:, None]
    e_down = jnp.exp(-offs * inv_m)
    e_up = jnp.exp(offs * inv_m)
    e_tail = jnp.exp(-(block_len - 1 - offs) * inv_m)
    e_next = jnp.exp(-(offs + 1) * inv_m)
    e_in = jnp.exp(-(block_len - offs) * inv_m)
    lower = offs >= offs.T
    toeplitz = jnp.where(lower, mm("tn,sn->ts", e_down * amp, e_up), 0.0)

    x_float = signal_x.astype(jnp.float32)
    q_float = gate_q.astype(jnp.float32)
    k_float = gate_k.astype(jnp.float32)
    d_float = cotangent.astype(jnp.float32)
    values = x_float * k_float
    grad_mixed = d_float * q_float

    conv_local = mm("cs,ts->ct", values, toeplitz)
    corr_local = mm("ct,ts->cs", grad_mixed, toeplitz)
    fwd = mm("cs,sn->cn", values, e_tail)
    fwd_m = mm("cs,sn->cn", values, e_tail * (block_len - 1 - offs))
    bwd = mm("ct,tn->cn", grad_mixed, e_down)
    fold = mm("ct,tn->cn", grad_mixed, e_next)
    fold_m = mm("ct,tn->cn", grad_mixed, e_next * (offs + 1) * inv_m)
    pair = jnp.where(lower, mm("ct,cs->ts", grad_mixed, values), 0.0)
    near = mm("ts,sn->tn", pair, e_up)
    near_m = mm("ts,sn->tn", pair, e_up * offs * inv_m)
    local_res = jnp.sum(e_down * near, axis=0)
    local_mem = jnp.sum(e_down * ((offs * inv_m - 0.5) * near - near_m), axis=0)

    pre, pre_m, post = state_scan(fwd, fwd_m, bwd, inv_m, block_len)

    conv_out = conv_local + mm("cn,tn->ct", pre, e_next * amp)
    corr_out = corr_local + mm("cn,sn->cs", post, e_in * amp)
    cross_res = jnp.sum(pre * fold, axis=0)
    cross_mem = jnp.sum(pre * (fold_m - 0.5 * fold) + pre_m * inv_m * fold, axis=0)

    mixed_out = conv_out + skip_gain[:, None] * values
    output = (q_float * mixed_out).astype(jnp.bfloat16)
    grad_values = skip_gain[:, None] * grad_mixed + corr_out
    grad_x = (grad_values * k_float).astype(jnp.bfloat16)
    grad_q = (d_float * mixed_out).astype(jnp.bfloat16)
    grad_k = (grad_values * x_float).astype(jnp.bfloat16)

    part_skip = jnp.sum(grad_mixed * values, axis=1)
    part_res = gain * (local_res + cross_res)
    part_mem = residue * gain * (local_mem + cross_mem)
    seq_sums = butterfly_sum(jnp.concatenate([part_res, part_mem, part_skip]), "seq")
    order = memory.shape[0]
    both = butterfly_sum(seq_sums[: 2 * order], "ch")
    norm_scale = 1.0 / math.sqrt(all_channels * seq_total)
    grad_skip = seq_sums[2 * order :] / math.sqrt(seq_total)
    grad_residue = both[:order] * norm_scale
    grad_memory = both[order:] * norm_scale
    return (output, grad_x, grad_q, grad_k, grad_skip, grad_residue, grad_memory)


def solution(mesh):
    return jax.shard_map(
        per_device,
        mesh=mesh,
        in_specs=(
            P("ch", "seq"),
            P("ch", "seq"),
            P("ch", "seq"),
            P("ch"),
            P(),
            P(),
            P("ch", "seq"),
        ),
        out_specs=(
            P("ch", "seq"),
            P("ch", "seq"),
            P("ch", "seq"),
            P("ch", "seq"),
            P("ch"),
            P(),
            P(),
        ),
        check_vma=False,
    )
```

time: 618 us -> 122 us (0.20)
  the two profiles are of different devices: /device:TPU:4 before, /device:TPU:1 now
where the time goes in v1:
time: 122 us; the launch traced here: 121 us
  starting transfers between devices  91 us (75%)
  waiting for transfers between devices  17.4 us (14%)
  matrix products  8.51 us (7%)
  local copies, waits for them, and re-layouts  1.9 us (2%)
  other arithmetic  1.57 us (1%)
    ppermute x16, starting transfers between devices, exchange(): return lax.ppermute(shard, axis, [(i, i ^ 1 << bit) for i in range(size)])  91 us
    ppermute x16, waiting for transfers between devices, exchange(): return lax.ppermute(shard, axis, [(i, i ^ 1 << bit) for i in range(size)])  17.4 us
    dot_general x13, matrix products, mm(): return jnp.einsum(pattern, left_op, right_op, precision=HIGH_PREC)  8.51 us
  transfers between devices with their start and end apart: 16, of which 16 were waited for; matrix products, arithmetic and copies ran while one was open for 3% of the time, Pallas kernels for 0%

profile of v1, /device:TPU:1, one launch (start us, length us, event | category | flops | bytes accessed | tf_op | source)
XLA Modules:
  0.0 121.5 jit_solution(15463383904964921669)
XLA Ops:
  0.6 0.0 copy-start.4
  0.6 0.0 copy-start
  0.7 0.0 copy-start.1
  0.7 0.6 copy-done.4
  1.3 0.1 copy-done
  1.4 0.0 copy-done.1
  1.4 0.2 fusion.23
  1.6 0.0 copy-start.2
  1.6 0.0 copy-start.3
  1.6 0.2 fusion.21
  1.9 0.5 copy-done.2
  2.4 0.0 copy-done.3
  2.4 0.2 fusion.30
  2.6 4.8 %collective-permute-start = (f32[3,16,16]{2,1,0:T(8,128)S(1)}, f32[3,16,16]{2,1,0:T(8,128)S(1)}, u32[]{:S(2)}, u32[]{:S(2)}) collective-permute-start(f32[3,16,16]{2,1,0:T(8,128)S(1)} %pad_maximum_fusion), channel_id=1, source_target_pairs={{0,4},{4,0},{8,12},{12,8},{16,20},{20,16},{24,28},{28,24},{32,36},... | collective-permute-start | bytes 9224 | tf_op jit(solution)/shard_map/ppermute | solution.py:17
  7.6 1.1 collective-permute-done
  8.7 5.8 %collective-permute-start.1 = (f32[3,16,16]{2,1,0:T(8,128)S(1)}, f32[3,16,16]{2,1,0:T(8,128)S(1)}, u32[]{:S(2)}, u32[]{:S(2)}) collective-permute-start(f32[3,16,16]{2,1,0:T(8,128)S(1)} %pad_maximum_fusion.1), channel_id=1, source_target_pairs={{0,8},{4,12},{8,0},{12,4},{16,24},{20,28},{24,16},{28,20},{32,40},... | collective-permute-start | bytes 9224 | tf_op jit(solution)/shard_map/ppermute | solution.py:17
  14.5 1.2 collective-permute-done.1
  15.7 8.4 %collective-permute-start.2 = (f32[3,16,16]{2,1,0:T(8,128)S(1)}, f32[3,16,16]{2,1,0:T(8,128)S(1)}, u32[]{:S(2)}, u32[]{:S(2)}) collective-permute-start(f32[3,16,16]{2,1,0:T(8,128)S(1)} %pad_maximum_fusion.2), channel_id=1, source_target_pairs={{0,16},{4,20},{8,24},{12,28},{16,0},{20,4},{24,8},{28,12},{32,48},... | collective-permute-start | bytes 9224 | tf_op jit(solution)/shard_map/ppermute | solution.py:17
  24.2 1.1 convolution_select_fusion
  25.3 0.1 collective-permute-done.2
  25.4 3.1 %collective-permute-start.3 = (f32[3,16,16]{2,1,0:T(8,128)S(1)}, f32[3,16,16]{2,1,0:T(8,128)S(1)}, u32[]{:S(2)}, u32[]{:S(2)}) collective-permute-start(f32[3,16,16]{2,1,0:T(8,128)S(1)} %pad_maximum_fusion.3), channel_id=1, source_target_pairs={{0,32},{4,36},{8,40},{12,44},{16,48},{20,52},{24,56},{28,60},{32,0... | collective-permute-start | bytes 9224 | tf_op jit(solution)/shard_map/ppermute | solution.py:17
  28.6 1.1 multiply_reduce_fusion.1
  29.7 0.6 collective-permute-done.3
  30.3 2.9 %collective-permute-start.4 = (f32[3,16,16]{2,1,0:T(8,128)S(1)}, f32[3,16,16]{2,1,0:T(8,128)S(1)}, u32[]{:S(2)}, u32[]{:S(2)}) collective-permute-start(f32[3,16,16]{2,1,0:T(8,128)S(1)} %pad_maximum_fusion.4), channel_id=1, source_target_pairs={{0,64},{4,68},{8,72},{12,76},{16,80},{20,84},{24,88},{28,92},{32,9... | collective-permute-start | bytes 9224 | tf_op jit(solution)/shard_map/ppermute | solution.py:17
  33.3 1.1 fusion.3
  34.4 0.5 collective-permute-done.4
  34.9 3.9 %collective-permute-start.5 = (f32[3,16,16]{2,1,0:T(8,128)S(1)}, f32[3,16,16]{2,1,0:T(8,128)S(1)}, u32[]{:S(2)}, u32[]{:S(2)}) collective-permute-start(f32[3,16,16]{2,1,0:T(8,128)S(1)} %pad_maximum_fusion.5), channel_id=1, source_target_pairs={{0,128},{4,132},{8,136},{12,140},{16,144},{20,148},{24,152},{28,15... | collective-permute-start | bytes 9224 | tf_op jit(solution)/shard_map/ppermute | solution.py:17
  38.9 1.5 %collective-permute-done.5 = f32[3,16,16]{2,1,0:T(8,128)S(1)} collective-permute-done((f32[3,16,16]{2,1,0:T(8,128)S(1)}, f32[3,16,16]{2,1,0:T(8,128)S(1)}, u32[]{:S(2)}, u32[]{:S(2)}) %collective-permute-start.5) | collective-permute-done | bytes 3104 | tf_op jit(solution)/shard_map/ppermute | solution.py:17
  40.4 7.4 %collective-permute-start.6 = (f32[3,16,16]{2,1,0:T(8,128)S(1)}, f32[3,16,16]{2,1,0:T(8,128)S(1)}, u32[]{:S(2)}, u32[]{:S(2)}) collective-permute-start(f32[3,16,16]{2,1,0:T(8,128)S(1)} %pad_maximum_fusion.6), channel_id=1, source_target_pairs={{0,256},{4,260},{8,264},{12,268},{16,272},{20,276},{24,280},{28,28... | collective-permute-start | bytes 9224 | tf_op jit(solution)/shard_map/ppermute | solution.py:17
  47.8 1.3 %collective-permute-done.6 = f32[3,16,16]{2,1,0:T(8,128)S(1)} collective-permute-done((f32[3,16,16]{2,1,0:T(8,128)S(1)}, f32[3,16,16]{2,1,0:T(8,128)S(1)}, u32[]{:S(2)}, u32[]{:S(2)}) %collective-permute-start.6) | collective-permute-done | bytes 3104 | tf_op jit(solution)/shard_map/ppermute | solution.py:17
  49.1 0.2 multiply_reduce_fusion.2
  49.4 0.3 fusion.6
  49.7 0.0 copy-start.5
  49.7 0.7 copy-done.5
  50.3 1.2 convolution_select_fusion.1
  51.5 1.0 fusion.31
  52.5 0.0 copy-start.6
  52.5 0.6 fusion.32
  53.1 0.0 copy-done.6
  53.1 0.2 fusion.2
  53.4 1.0 fusion.8
  54.4 0.1 pad_maximum_fusion.7
  54.5 3.0 %collective-permute-start.7 = (f32[48]{0:T(128)S(1)}, f32[48]{0:T(128)S(1)}, u32[]{:S(2)}, u32[]{:S(2)}) collective-permute-start(f32[48]{0:T(128)S(1)} %pad_maximum_fusion.7), channel_id=1, source_target_pairs={{0,4},{4,0},{8,12},{12,8},{16,20},{20,16},{24,28},{28,24},{32,36},... | collective-permute-start | bytes 584 | tf_op jit(solution)/shard_map/ppermute | solution.py:17
  57.5 1.5 %collective-permute-done.7 = f32[48]{0:T(128)S(1)} collective-permute-done((f32[48]{0:T(128)S(1)}, f32[48]{0:T(128)S(1)}, u32[]{:S(2)}, u32[]{:S(2)}) %collective-permute-start.7) | collective-permute-done | bytes 224 | tf_op jit(solution)/shard_map/ppermute | solution.py:17
  59.0 0.1 fusion.101
  59.0 4.1 %collective-permute-start.8 = (f32[48]{0:T(128)S(1)}, f32[48]{0:T(128)S(1)}, u32[]{:S(2)}, u32[]{:S(2)}) collective-permute-start(f32[48]{0:T(128)S(1)} %fusion.101), channel_id=1, source_target_pairs={{0,8},{4,12},{8,0},{12,4},{16,24},{20,28},{24,16},{28,20},{32,40},... | collective-permute-start | bytes 584 | tf_op jit(solution)/shard_map/ppermute | solution.py:17
  63.1 1.1 collective-permute-done.8
  64.2 7.3 %collective-permute-start.9 = (f32[48]{0:T(128)S(1)}, f32[48]{0:T(128)S(1)}, u32[]{:S(2)}, u32[]{:S(2)}) collective-permute-start(f32[48]{0:T(128)S(1)} %add.294), channel_id=1, source_target_pairs={{0,16},{4,20},{8,24},{12,28},{16,0},{20,4},{24,8},{28,12},{32,48},... | collective-permute-start | bytes 584 | tf_op jit(solution)/shard_map/ppermute | solution.py:17
  71.5 0.9 collective-permute-done.9
  72.4 3.1 %collective-permute-start.10 = (f32[48]{0:T(128)S(1)}, f32[48]{0:T(128)S(1)}, u32[]{:S(2)}, u32[]{:S(2)}) collective-permute-start(f32[48]{0:T(128)S(1)} %add.295), channel_id=1, source_target_pairs={{0,32},{4,36},{8,40},{12,44},{16,48},{20,52},{24,56},{28,60},{32,0... | collective-permute-start | bytes 584 | tf_op jit(solution)/shard_map/ppermute | solution.py:17
  75.5 1.2 collective-permute-done.10
  76.7 2.9 %collective-permute-start.11 = (f32[48]{0:T(128)S(1)}, f32[48]{0:T(128)S(1)}, u32[]{:S(2)}, u32[]{:S(2)}) collective-permute-start(f32[48]{0:T(128)S(1)} %add.296), channel_id=1, source_target_pairs={{0,64},{4,68},{8,72},{12,76},{16,80},{20,84},{24,88},{28,92},{32,9... | collective-permute-start | bytes 584 | tf_op jit(solution)/shard_map/ppermute | solution.py:17
  79.6 1.4 %collective-permute-done.11 = f32[48]{0:T(128)S(1)} collective-permute-done((f32[48]{0:T(128)S(1)}, f32[48]{0:T(128)S(1)}, u32[]{:S(2)}, u32[]{:S(2)}) %collective-permute-start.11) | collective-permute-done | bytes 224 | tf_op jit(solution)/shard_map/ppermute | solution.py:17
  81.0 4.3 %collective-permute-start.12 = (f32[48]{0:T(128)S(1)}, f32[48]{0:T(128)S(1)}, u32[]{:S(2)}, u32[]{:S(2)}) collective-permute-start(f32[48]{0:T(128)S(1)} %add.297), channel_id=1, source_target_pairs={{0,128},{4,132},{8,136},{12,140},{16,144},{20,148},{24,152},{28,15... | collective-permute-start | bytes 584 | tf_op jit(solution)/shard_map/ppermute | solution.py:17
  85.3 0.9 collective-permute-done.12
  86.2 7.4 %collective-permute-start.13 = (f32[48]{0:T(128)S(1)}, f32[48]{0:T(128)S(1)}, u32[]{:S(2)}, u32[]{:S(2)}) collective-permute-start(f32[48]{0:T(128)S(1)} %add.298), channel_id=1, source_target_pairs={{0,256},{4,260},{8,264},{12,268},{16,272},{20,276},{24,280},{28,28... | collective-permute-start | bytes 584 | tf_op jit(solution)/shard_map/ppermute | solution.py:17
  93.6 0.9 collective-permute-done.13
  94.5 19.8 %collective-permute-start.14 = (f32[32]{0:T(128)S(1)}, f32[32]{0:T(128)S(1)}, u32[]{:S(2)}, u32[]{:S(2)}) collective-permute-start(f32[32]{0:T(128)S(1)} %bitcast.264), channel_id=1, source_target_pairs={{0,1},{1,0},{2,3},{3,2},{4,5},{5,4},{6,7},{7,6},{8,9},{9,8},{10,11... | collective-permute-start | bytes 392 | tf_op jit(solution)/shard_map/ppermute | solution.py:17
  114.3 0.8 collective-permute-done.14
  115.1 2.8 %collective-permute-start.15 = (f32[32]{0:T(128)S(1)}, f32[32]{0:T(128)S(1)}, u32[]{:S(2)}, u32[]{:S(2)}) collective-permute-start(f32[32]{0:T(128)S(1)} %slice_add_fusion), channel_id=1, source_target_pairs={{0,2},{1,3},{2,0},{3,1},{4,6},{5,7},{6,4},{7,5},{8,10},{9,11},{10,... | collective-permute-start | bytes 392 | tf_op jit(solution)/shard_map/ppermute | solution.py:17
  117.9 0.6 slice_multiply_fusion.2
  118.5 2.4 %collective-permute-done.15 = f32[32]{0:T(128)S(1)} collective-permute-done((f32[32]{0:T(128)S(1)}, f32[32]{0:T(128)S(1)}, u32[]{:S(2)}, u32[]{:S(2)}) %collective-permute-start.15) | collective-permute-done | bytes 160 | tf_op jit(solution)/shard_map/ppermute | solution.py:17
  120.9 0.6 slice_multiply_fusion
  (29 shorter events, 0.2 us)
Async XLA Ops:
  0.6 0.7 copy-start.4
  0.6 0.7 copy-start
  0.7 0.7 copy-start.1
  1.6 0.7 copy-start.2
  1.6 0.7 copy-start.3
  2.6 6.0 %collective-permute-start = (f32[3,16,16]{2,1,0:T(8,128)S(1)}, f32[3,16,16]{2,1,0:T(8,128)S(1)}, u32[]{:S(2)}, u32[]{:S(2)}) collective-permute-start(f32[3,16,16]{2,1,0:T(8,128)S(1)} %pad_maximum_fusion), channel_id=1, source_target_pairs={{0,4},{4,0},{8,12},{12,8},{16,20},{20,16},{24,28},{28,24},{32,36},... | collective-permute-start | bytes 9224 | tf_op jit(solution)/shard_map/ppermute | solution.py:17
  8.7 7.0 %collective-permute-start.1 = (f32[3,16,16]{2,1,0:T(8,128)S(1)}, f32[3,16,16]{2,1,0:T(8,128)S(1)}, u32[]{:S(2)}, u32[]{:S(2)}) collective-permute-start(f32[3,16,16]{2,1,0:T(8,128)S(1)} %pad_maximum_fusion.1), channel_id=1, source_target_pairs={{0,8},{4,12},{8,0},{12,4},{16,24},{20,28},{24,16},{28,20},{32,40},... | collective-permute-start | bytes 9224 | tf_op jit(solution)/shard_map/ppermute | solution.py:17
  15.7 9.7 %collective-permute-start.2 = (f32[3,16,16]{2,1,0:T(8,128)S(1)}, f32[3,16,16]{2,1,0:T(8,128)S(1)}, u32[]{:S(2)}, u32[]{:S(2)}) collective-permute-start(f32[3,16,16]{2,1,0:T(8,128)S(1)} %pad_maximum_fusion.2), channel_id=1, source_target_pairs={{0,16},{4,20},{8,24},{12,28},{16,0},{20,4},{24,8},{28,12},{32,48},... | collective-permute-start | bytes 9224 | tf_op jit(solution)/shard_map/ppermute | solution.py:17
  25.4 4.9 %collective-permute-start.3 = (f32[3,16,16]{2,1,0:T(8,128)S(1)}, f32[3,16,16]{2,1,0:T(8,128)S(1)}, u32[]{:S(2)}, u32[]{:S(2)}) collective-permute-start(f32[3,16,16]{2,1,0:T(8,128)S(1)} %pad_maximum_fusion.3), channel_id=1, source_target_pairs={{0,32},{4,36},{8,40},{12,44},{16,48},{20,52},{24,56},{28,60},{32,0... | collective-permute-start | bytes 9224 | tf_op jit(solution)/shard_map/ppermute | solution.py:17
  30.3 4.6 %collective-permute-start.4 = (f32[3,16,16]{2,1,0:T(8,128)S(1)}, f32[3,16,16]{2,1,0:T(8,128)S(1)}, u32[]{:S(2)}, u32[]{:S(2)}) collective-permute-start(f32[3,16,16]{2,1,0:T(8,128)S(1)} %pad_maximum_fusion.4), channel_id=1, source_target_pairs={{0,64},{4,68},{8,72},{12,76},{16,80},{20,84},{24,88},{28,92},{32,9... | collective-permute-start | bytes 9224 | tf_op jit(solution)/shard_map/ppermute | solution.py:17
  34.9 5.5 %collective-permute-start.5 = (f32[3,16,16]{2,1,0:T(8,128)S(1)}, f32[3,16,16]{2,1,0:T(8,128)S(1)}, u32[]{:S(2)}, u32[]{:S(2)}) collective-permute-start(f32[3,16,16]{2,1,0:T(8,128)S(1)} %pad_maximum_fusion.5), channel_id=1, source_target_pairs={{0,128},{4,132},{8,136},{12,140},{16,144},{20,148},{24,152},{28,15... | collective-permute-start | bytes 9224 | tf_op jit(solution)/shard_map/ppermute | solution.py:17
  40.4 8.7 %collective-permute-start.6 = (f32[3,16,16]{2,1,0:T(8,128)S(1)}, f32[3,16,16]{2,1,0:T(8,128)S(1)}, u32[]{:S(2)}, u32[]{:S(2)}) collective-permute-start(f32[3,16,16]{2,1,0:T(8,128)S(1)} %pad_maximum_fusion.6), channel_id=1, source_target_pairs={{0,256},{4,260},{8,264},{12,268},{16,272},{20,276},{24,280},{28,28... | collective-permute-start | bytes 9224 | tf_op jit(solution)/shard_map/ppermute | solution.py:17
  49.7 0.7 copy-start.5
  52.5 0.7 copy-start.6
  54.5 4.5 %collective-permute-start.7 = (f32[48]{0:T(128)S(1)}, f32[48]{0:T(128)S(1)}, u32[]{:S(2)}, u32[]{:S(2)}) collective-permute-start(f32[48]{0:T(128)S(1)} %pad_maximum_fusion.7), channel_id=1, source_target_pairs={{0,4},{4,0},{8,12},{12,8},{16,20},{20,16},{24,28},{28,24},{32,36},... | collective-permute-start | bytes 584 | tf_op jit(solution)/shard_map/ppermute | solution.py:17
  59.0 5.2 %collective-permute-start.8 = (f32[48]{0:T(128)S(1)}, f32[48]{0:T(128)S(1)}, u32[]{:S(2)}, u32[]{:S(2)}) collective-permute-start(f32[48]{0:T(128)S(1)} %fusion.101), channel_id=1, source_target_pairs={{0,8},{4,12},{8,0},{12,4},{16,24},{20,28},{24,16},{28,20},{32,40},... | collective-permute-start | bytes 584 | tf_op jit(solution)/shard_map/ppermute | solution.py:17
  64.2 8.2 %collective-permute-start.9 = (f32[48]{0:T(128)S(1)}, f32[48]{0:T(128)S(1)}, u32[]{:S(2)}, u32[]{:S(2)}) collective-permute-start(f32[48]{0:T(128)S(1)} %add.294), channel_id=1, source_target_pairs={{0,16},{4,20},{8,24},{12,28},{16,0},{20,4},{24,8},{28,12},{32,48},... | collective-permute-start | bytes 584 | tf_op jit(solution)/shard_map/ppermute | solution.py:17
  72.4 4.3 %collective-permute-start.10 = (f32[48]{0:T(128)S(1)}, f32[48]{0:T(128)S(1)}, u32[]{:S(2)}, u32[]{:S(2)}) collective-permute-start(f32[48]{0:T(128)S(1)} %add.295), channel_id=1, source_target_pairs={{0,32},{4,36},{8,40},{12,44},{16,48},{20,52},{24,56},{28,60},{32,0... | collective-permute-start | bytes 584 | tf_op jit(solution)/shard_map/ppermute | solution.py:17
  76.7 4.3 %collective-permute-start.11 = (f32[48]{0:T(128)S(1)}, f32[48]{0:T(128)S(1)}, u32[]{:S(2)}, u32[]{:S(2)}) collective-permute-start(f32[48]{0:T(128)S(1)} %add.296), channel_id=1, source_target_pairs={{0,64},{4,68},{8,72},{12,76},{16,80},{20,84},{24,88},{28,92},{32,9... | collective-permute-start | bytes 584 | tf_op jit(solution)/shard_map/ppermute | solution.py:17
  81.0 5.2 %collective-permute-start.12 = (f32[48]{0:T(128)S(1)}, f32[48]{0:T(128)S(1)}, u32[]{:S(2)}, u32[]{:S(2)}) collective-permute-start(f32[48]{0:T(128)S(1)} %add.297), channel_id=1, source_target_pairs={{0,128},{4,132},{8,136},{12,140},{16,144},{20,148},{24,152},{28,15... | collective-permute-start | bytes 584 | tf_op jit(solution)/shard_map/ppermute | solution.py:17
  86.2 8.3 %collective-permute-start.13 = (f32[48]{0:T(128)S(1)}, f32[48]{0:T(128)S(1)}, u32[]{:S(2)}, u32[]{:S(2)}) collective-permute-start(f32[48]{0:T(128)S(1)} %add.298), channel_id=1, source_target_pairs={{0,256},{4,260},{8,264},{12,268},{16,272},{20,276},{24,280},{28,28... | collective-permute-start | bytes 584 | tf_op jit(solution)/shard_map/ppermute | solution.py:17
  94.5 20.6 %collective-permute-start.14 = (f32[32]{0:T(128)S(1)}, f32[32]{0:T(128)S(1)}, u32[]{:S(2)}, u32[]{:S(2)}) collective-permute-start(f32[32]{0:T(128)S(1)} %bitcast.264), channel_id=1, source_target_pairs={{0,1},{1,0},{2,3},{3,2},{4,5},{5,4},{6,7},{7,6},{8,9},{9,8},{10,11... | collective-permute-start | bytes 392 | tf_op jit(solution)/shard_map/ppermute | solution.py:17
  115.1 5.8 %collective-permute-start.15 = (f32[32]{0:T(128)S(1)}, f32[32]{0:T(128)S(1)}, u32[]{:S(2)}, u32[]{:S(2)}) collective-permute-start(f32[32]{0:T(128)S(1)} %slice_add_fusion), channel_id=1, source_target_pairs={{0,2},{1,3},{2,0},{3,1},{4,6},{5,7},{6,4},{7,5},{8,10},{9,11},{10,... | collective-permute-start | bytes 392 | tf_op jit(solution)/shard_map/ppermute | solution.py:17

commit v2 on v1

v2 whole, which is shorter than its diff:
```python
import functools
import math

import jax
import jax.numpy as jnp
from jax import lax
from jax.experimental import pallas as pl
from jax.experimental.pallas import tpu as pltpu
from jax.sharding import PartitionSpec as P

HIGH_PREC = lax.Precision.HIGHEST


def mm(pattern, left_op, right_op):
    return jnp.einsum(pattern, left_op, right_op, precision=HIGH_PREC)


STATE_SLABS = 7


def partner_of(index, bit):
    size = 1 << bit
    upper = (index // size) % 2
    return index + size - 2 * size * upper


def combine_kernel(seq_bits, ch_bits, state_ref, coef_ref, agg_ref, edge_ref,
                   send_buf, recv_buf, ch_send, ch_recv, send_sem, recv_sem, ch_send_sem, ch_recv_sem):
    seq_index = lax.axis_index("seq")
    ch_index = lax.axis_index("ch")
    barrier = pltpu.get_barrier_semaphore()
    for bit in range(seq_bits):
        pl.semaphore_signal(barrier, inc=1, device_id=(partner_of(seq_index, bit), ch_index),
                            device_id_type=pl.DeviceIdType.MESH)
    for bit in range(ch_bits):
        pl.semaphore_signal(barrier, inc=1, device_id=(seq_index, partner_of(ch_index, bit)),
                            device_id_type=pl.DeviceIdType.MESH)
    pl.semaphore_wait(barrier, seq_bits + ch_bits)

    mine = [state_ref[i] for i in range(STATE_SLABS)]
    rows = lax.broadcasted_iota(jnp.int32, mine[0].shape, 0)
    pre = jnp.zeros_like(mine[0])
    post = jnp.zeros_like(mine[0])
    for bit in range(seq_bits):
        for i in range(STATE_SLABS):
            send_buf[bit, i] = mine[i]
        copy = pltpu.make_async_remote_copy(
            src_ref=send_buf.at[bit],
            dst_ref=recv_buf.at[bit],
            send_sem=send_sem.at[bit],
            recv_sem=recv_sem.at[bit],
            device_id=(partner_of(seq_index, bit), ch_index),
            device_id_type=pl.DeviceIdType.MESH,
        )
        copy.start()
        copy.wait()
        other = [recv_buf[bit, i] for i in range(STATE_SLABS)]
        coef = coef_ref[bit]
        pick = coef[0:1] > 0.5
        whole, whole_len, whole_q = coef[1:2], coef[2:3], coef[3:4]
        lag, lead, inv_m = coef[4:5], coef[5:6], coef[6:7]
        lo = [jnp.where(pick, o, m) for o, m in zip(other, mine)]
        hi = [jnp.where(pick, m, o) for o, m in zip(other, mine)]
        pre = pre + lag * other[0]
        post = post + lead * other[2]
        cross_res = jnp.sum(lo[0] * hi[3], axis=0, keepdims=True)
        cross_mem = jnp.sum(lo[0] * hi[4] + lo[1] * hi[3] * inv_m, axis=0, keepdims=True)
        mine = [
            whole * lo[0] + hi[0],
            whole * lo[1] + whole_len * lo[0] + hi[1],
            lo[2] + whole * hi[2],
            lo[3] + whole * hi[3],
            lo[4] + whole * hi[4] + whole_q * hi[3],
            lo[5] + hi[5] + jnp.where(rows == 0, cross_res, jnp.where(rows == 1, cross_mem, 0.0)),
            lo[6] + hi[6],
        ]
    sums = mine[5]
    for bit in range(ch_bits):
        ch_send[bit] = sums
        copy = pltpu.make_async_remote_copy(
            src_ref=ch_send.at[bit],
            dst_ref=ch_recv.at[bit],
            send_sem=ch_send_sem.at[bit],
            recv_sem=ch_recv_sem.at[bit],
            device_id=(seq_index, partner_of(ch_index, bit)),
            device_id_type=pl.DeviceIdType.MESH,
        )
        copy.start()
        copy.wait()
        sums = sums + ch_recv[bit]
    agg_ref[0] = sums
    agg_ref[1] = mine[6]
    edge_ref[0] = pre
    edge_ref[1] = post


def combine_states(state, inv_m, block_len):
    seq_index = lax.axis_index("seq")
    seq_bits = lax.axis_size("seq").bit_length() - 1
    ch_bits = lax.axis_size("ch").bit_length() - 1
    coefs = []
    for bit in range(seq_bits):
        size = 1 << bit
        upper = ((seq_index // size) % 2).astype(jnp.float32)
        rank = (seq_index % size).astype(jnp.float32)
        whole = jnp.exp(-float(size * block_len) * inv_m)
        lag = upper * jnp.exp(-(rank * block_len) * inv_m)
        lead = (1.0 - upper) * jnp.exp(-((size - 1 - rank) * block_len) * inv_m)
        rows = [
            jnp.broadcast_to(upper, inv_m.shape),
            whole,
            whole * float(size * block_len),
            whole * float(size * block_len) * inv_m,
            lag,
            lead,
            inv_m,
            jnp.zeros_like(inv_m),
        ]
        coefs.append(jnp.stack(rows))
    coef = jnp.stack(coefs)
    slab = state.shape[1:]
    vmem = pl.BlockSpec(memory_space=pltpu.VMEM)
    return pl.pallas_call(
        functools.partial(combine_kernel, seq_bits, ch_bits),
        out_shape=(
            jax.ShapeDtypeStruct((2,) + slab, jnp.float32),
            jax.ShapeDtypeStruct((2,) + slab, jnp.float32),
        ),
        in_specs=[vmem, vmem],
        out_specs=(vmem, vmem),
        scratch_shapes=[
            pltpu.VMEM((seq_bits, STATE_SLABS) + slab, jnp.float32),
            pltpu.VMEM((seq_bits, STATE_SLABS) + slab, jnp.float32),
            pltpu.VMEM((ch_bits,) + slab, jnp.float32),
            pltpu.VMEM((ch_bits,) + slab, jnp.float32),
            pltpu.SemaphoreType.DMA((seq_bits,)),
            pltpu.SemaphoreType.DMA((seq_bits,)),
            pltpu.SemaphoreType.DMA((ch_bits,)),
            pltpu.SemaphoreType.DMA((ch_bits,)),
        ],
        compiler_params=pltpu.CompilerParams(collective_id=0, has_side_effects=True),
    )(state, coef)


def per_device(signal_x, gate_q, gate_k, skip_gain, residue, memory, cotangent):
    channels, block_len = signal_x.shape
    seq_total = lax.axis_size("seq") * block_len
    all_channels = channels * lax.axis_size("ch")
    inv_m = 1.0 / memory
    gain = jnp.sqrt(2.0 / memory)
    amp = residue * gain
    offs = jnp.arange(block_len, dtype=jnp.float32)[:, None]
    e_down = jnp.exp(-offs * inv_m)
    e_up = jnp.exp(offs * inv_m)
    e_tail = jnp.exp(-(block_len - 1 - offs) * inv_m)
    e_next = jnp.exp(-(offs + 1) * inv_m)
    e_in = jnp.exp(-(block_len - offs) * inv_m)
    lower = offs >= offs.T
    toeplitz = jnp.where(lower, mm("tn,sn->ts", e_down * amp, e_up), 0.0)

    x_float = signal_x.astype(jnp.float32)
    q_float = gate_q.astype(jnp.float32)
    k_float = gate_k.astype(jnp.float32)
    d_float = cotangent.astype(jnp.float32)
    values = x_float * k_float
    grad_mixed = d_float * q_float

    conv_local = mm("cs,ts->ct", values, toeplitz)
    corr_local = mm("ct,ts->cs", grad_mixed, toeplitz)
    fwd = mm("cs,sn->cn", values, e_tail)
    fwd_m = mm("cs,sn->cn", values, e_tail * (block_len - 1 - offs))
    bwd = mm("ct,tn->cn", grad_mixed, e_down)
    fold = mm("ct,tn->cn", grad_mixed, e_next)
    fold_m = mm("ct,tn->cn", grad_mixed, e_next * (offs + 1) * inv_m)
    pair = jnp.where(lower, mm("ct,cs->ts", grad_mixed, values), 0.0)
    near = mm("ts,sn->tn", pair, e_up)
    near_m = mm("ts,sn->tn", pair, e_up * offs * inv_m)
    local_res = jnp.sum(e_down * near, axis=0)
    local_mem = jnp.sum(e_down * ((offs * inv_m - 0.5) * near - near_m), axis=0)

    rows = lax.broadcasted_iota(jnp.int32, fwd.shape, 0)
    sums = jnp.where(rows == 0, local_res[None, :], jnp.where(rows == 1, local_mem[None, :], 0.0))
    part_skip = jnp.sum(grad_mixed * values, axis=1)
    state = jnp.stack([fwd, fwd_m, bwd, fold, fold_m - 0.5 * fold, sums, jnp.broadcast_to(part_skip[:, None], fwd.shape)])
    agg, edge = combine_states(state, inv_m, block_len)
    pre, post = edge[0], edge[1]

    conv_out = conv_local + mm("cn,tn->ct", pre, e_next * amp)
    corr_out = corr_local + mm("cn,sn->cs", post, e_in * amp)

    mixed_out = conv_out + skip_gain[:, None] * values
    output = (q_float * mixed_out).astype(jnp.bfloat16)
    grad_values = skip_gain[:, None] * grad_mixed + corr_out
    grad_x = (grad_values * k_float).astype(jnp.bfloat16)
    grad_q = (d_float * mixed_out).astype(jnp.bfloat16)
    grad_k = (grad_values * x_float).astype(jnp.bfloat16)

    norm_scale = 1.0 / math.sqrt(all_channels * seq_total)
    grad_skip = agg[1][:, 0] / math.sqrt(seq_total)
    grad_residue = gain * agg[0][0] * norm_scale
    grad_memory = residue * gain * agg[0][1] * norm_scale
    return (output, grad_x, grad_q, grad_k, grad_skip, grad_residue, grad_memory)


def solution(mesh):
    return jax.shard_map(
        per_device,
        mesh=mesh,
        in_specs=(
            P("ch", "seq"),
            P("ch", "seq"),
            P("ch", "seq"),
            P("ch"),
            P(),
            P(),
            P("ch", "seq"),
        ),
        out_specs=(
            P("ch", "seq"),
            P("ch", "seq"),
            P("ch", "seq"),
            P("ch", "seq"),
            P("ch"),
            P(),
            P(),
        ),
        check_vma=False,
    )
```

time: 122 us -> 67.3 us (0.55)
  starting transfers between devices: 91 us -> 0 us
  Pallas kernels: 0 us -> 50.2 us
  waiting for transfers between devices: 17.4 us -> 0 us
  local copies, waits for them, and re-layouts: 1.9 us -> 4.02 us
    ppermute x16 -> x0, starting transfers between devices: 91 us -> none  [exchange(): return lax.ppermute(shard, axis, [(i, i ^ 1 << bit) for i in range(size)])]
    pallas_call x0 -> x1, Pallas kernels: none -> 50.2 us  [combine_states(): pl.pallas_call(functools.partial(combine_kernel, seq_bits, ch_bits), out_...]
    ppermute x16 -> x0, waiting for transfers between devices: 17.4 us -> none  [exchange(): return lax.ppermute(shard, axis, [(i, i ^ 1 << bit) for i in range(size)])]
    unnamed x14 -> x28, local copies, waits for them, and re-layouts: 1.9 us -> 3.72 us
  transfers between devices with their start and end apart: 16 -> 0, of which waited for: 16 -> 0; matrix products, arithmetic and copies ran while one was open for 3% -> 0% of each run, Pallas kernels for 0% -> 0%
where the time goes in v2:
time: 67.3 us; the launch traced here: 66.8 us
  Pallas kernels  50.2 us (75%)
  matrix products  8.94 us (13%)
  local copies, waits for them, and re-layouts  4.02 us (6%)
  other arithmetic  2.67 us (4%)
  between operations  1 us (1%)
    pallas_call x1, Pallas kernels, combine_states(): pl.pallas_call(functools.partial(combine_kernel, seq_bits, ch_bits), out_...  50.2 us
    dot_general x13, matrix products, mm(): return jnp.einsum(pattern, left_op, right_op, precision=HIGH_PREC)  8.94 us
    unnamed x28, local copies, waits for them, and re-layouts  3.72 us

profile of v2, /device:TPU:1, one launch (start us, length us, event | category | flops | bytes accessed | tf_op | source)
XLA Modules:
  0.0 66.8 jit_solution(15187714783286366793)
XLA Ops:
  0.7 0.0 copy-start.7
  0.7 0.0 copy-start.3
  0.7 0.0 copy-start.2
  0.7 0.6 copy-done.7
  1.3 0.1 copy-done.3
  1.4 0.0 copy-done.2
  1.4 0.2 fusion.8
  1.6 0.0 copy-start
  1.7 0.0 copy-start.1
  1.7 0.2 fusion.7
  1.9 0.5 copy-done
  2.4 0.0 copy-done.1
  2.4 0.2 fusion.6
  2.7 0.2 constant_dynamic-update-slice_fusion.2
  2.9 0.2 fusion.5
  3.1 1.1 %convolution_select_fusion = f32[512,512]{1,0:T(8,128)S(1)} fusion(bf16[16,512]{1,0:T(8,128)(2,1)S(1)} %copy-done.2, bf16[16,512]{1,0:T(8,128)(2,1)S(1)} %copy-done.3, bf16[16,512]{1,0:T(8,128)(2,1)S(1)} %copy-done, bf16[16,512]{1,0:T(8,128)(2,1)S(1)} %copy-done.1), kind=kOutput, calls=%fused_computation | convolution fusion | flops 50905088 | bytes 1114112 | tf_op jit(solution)/shard_map/ct,cs->ts/dot_general | solution.py:15
  4.2 1.1 %multiply_reduce_fusion.1 = (f32[16]{0:T(128)S(1)}, f32[512,16]{0,1:T(8,128)S(1)}) fusion(f32[16]{0:T(128)S(1)} %get-tuple-element.15, f32[512]{0:T(512)S(1)} %iota_negate_fusion, f32[512,512]{1,0:T(8,128)S(1)} %convolution_select_fusion), kind=kOutput, calls=%fused_computation.37 | convolution fusion | flops 50364400 | bytes 1083520 | tf_op jit(solution)/shard_map/ts,sn->tn/dot_general | solution.py:15
  5.4 1.1 %fusion.3 = f32[16]{0:T(128)S(1)} fusion(f32[512,512]{1,0:T(8,128)S(1)} %convolution_select_fusion, f32[512,16]{0,1:T(8,128)S(1)} %get-tuple-element.57, f32[16]{0:T(128)S(1)} %get-tuple-element.15, f32[512]{0:T(512)S(1)} %iota_negate_fusion), kind=kOutput, calls=%fused_computation.8 | convolution fusion | flops 50413552 | bytes 1083520 | tf_op jit(solution)/shard_map/ts,sn->tn/dot_general | solution.py:15
  6.5 0.1 constant_dynamic-update-slice_fusion.1
  6.6 0.1 multiply_reduce_fusion
  6.7 0.1 constant_dynamic-update-slice_fusion.state_ref
  6.8 0.0 copy-start.4
  6.8 0.6 copy-done.4
  7.8 0.0 copy-start.5
  7.8 0.6 copy-done.5
  8.4 50.2 %shard_map.126 = (f32[2,16,16]{2,1,0:T(8,128)}, f32[2,16,16]{2,1,0:T(8,128)}) custom-call(f32[7,16,16]{2,1,0:T(8,128)} %copy-done.4, f32[7,8,16]{2,1,0:T(8,128)} %copy-done.5), custom_call_target="tpu_custom_call" | custom-call | tf_op jit(solution)/shard_map/pallas_call | solution.py:123
  58.6 0.0 copy-start.8
  58.6 0.6 copy-done.8
  59.3 1.2 %fusion.62 = (f32[16]{0:T(128)}, f32[16]{0:T(128)S(1)}, f32[16]{0:T(128)S(1)}) fusion(f32[2,16,16]{2,1,0:T(8,128)} %get-tuple-element.10, f32[16]{0:T(128)S(1)} %copy-done.8, f32[16]{0:T(128)S(1)} %copy-done.7), kind=kLoop, calls=%fused_computation.98 | loop fusion | flops 64 | bytes 384 | tf_op jit(solution)/shard_map/mul | solution.py:201
  60.5 1.2 %convolution_select_fusion.1 = f32[512,512]{1,0:T(8,128)S(1)} fusion(f32[16]{0:T(128)S(1)} %get-tuple-element.12, f32[16]{0:T(128)S(1)} %get-tuple-element.15, f32[512]{0:T(512)S(1)} %iota_negate_fusion), kind=kOutput, calls=%fused_computation.1 | convolution fusion | flops 50880512 | bytes 1050752 | tf_op jit(solution)/shard_map/tn,sn->ts/dot_general | solution.py:15
  61.6 0.0 copy-start.9
  61.7 1.0 %fusion.30 = f32[16,512]{1,0:T(8,128)S(1)} fusion(f32[512,512]{1,0:T(8,128)S(1)} %convolution_select_fusion.1, bf16[16,512]{1,0:T(8,128)(2,1)S(1)} %copy-done.2, bf16[16,512]{1,0:T(8,128)(2,1)S(1)} %copy-done.3), kind=kOutput, calls=%fused_computation.59 | convolution fusion | flops 50356224 | bytes 1114112 | tf_op jit(solution)/shard_map/cs,ts->ct/dot_general | solution.py:15
  62.6 0.0 copy-start.10
  62.6 0.0 copy-done.9
  62.6 0.6 copy-done.10
  63.3 0.9 %fusion.12 = (bf16[16,512]{1,0:T(8,128)(2,1)}, bf16[16,512]{1,0:T(8,128)(2,1)}) fusion(bf16[16,512]{1,0:T(8,128)(2,1)S(1)} %copy-done, bf16[16,512]{1,0:T(8,128)(2,1)S(1)} %copy-done.1, bf16[16,512]{1,0:T(8,128)(2,1)S(1)} %copy-done.2, bf16[16,512]{1,0:T(8,128)(2,1)S(1)} %copy-done.3, f32[16]{0:T(128)S(1)} %copy-done.10, f32[16,512]{1,0:T(8,128)S(1)} %fusion.30, ...), kind=kOutput, calls=%fused_computation.28 | convolution fusion | flops 1687552 | bytes 142848 | tf_op jit(solution)/shard_map/cn,tn->ct/dot_general | solution.py:15
  64.1 0.6 fusion.31
  64.8 0.0 copy-start.6
  64.8 0.9 %fusion.10 = (bf16[16,512]{1,0:T(8,128)(2,1)}, bf16[16,512]{1,0:T(8,128)(2,1)}) fusion(bf16[16,512]{1,0:T(8,128)(2,1)S(1)} %copy-done.3, bf16[16,512]{1,0:T(8,128)(2,1)S(1)} %copy-done.2, f32[16,512]{1,0:T(8,128)S(1)} %fusion.31, f32[512]{0:T(512)S(1)} %subtract_negate_fusion, f32[16]{0:T(128)S(1)} %get-tuple-element.12, f32[16]{0:T(128)S(1)} %get-tuple-element.15, ...), kind=kOutput, calls=%fused_computation.26 | convolution fusion | flops 1687552 | bytes 142848 | tf_op jit(solution)/shard_map/cn,sn->cs/dot_general | solution.py:15
  65.6 0.0 copy-done.6
  65.6 0.6 fusion.55
  66.3 0.5 fusion.63
  (31 shorter events, 0.4 us)
Async XLA Ops:
  0.7 0.7 copy-start.7
  0.7 0.7 %copy-start.3 = (bf16[16,512]{1,0:T(8,128)(2,1)S(1)}, bf16[16,512]{1,0:T(8,128)(2,1)}, u32[]{:S(2)}) copy-start(bf16[16,512]{1,0:T(8,128)(2,1)} %param.7) | copy-start | bytes 49156
  0.7 0.7 %copy-start.2 = (bf16[16,512]{1,0:T(8,128)(2,1)S(1)}, bf16[16,512]{1,0:T(8,128)(2,1)}, u32[]{:S(2)}) copy-start(bf16[16,512]{1,0:T(8,128)(2,1)} %param.9) | copy-start | bytes 49156
  1.6 0.7 %copy-start = (bf16[16,512]{1,0:T(8,128)(2,1)S(1)}, bf16[16,512]{1,0:T(8,128)(2,1)}, u32[]{:S(2)}) copy-start(bf16[16,512]{1,0:T(8,128)(2,1)} %param.13) | copy-start | bytes 49156
  1.7 0.7 %copy-start.1 = (bf16[16,512]{1,0:T(8,128)(2,1)S(1)}, bf16[16,512]{1,0:T(8,128)(2,1)}, u32[]{:S(2)}) copy-start(bf16[16,512]{1,0:T(8,128)(2,1)} %param.8) | copy-start | bytes 49156
  6.8 0.6 copy-start.4
  7.8 0.6 copy-start.5
  58.6 0.7 copy-start.8
  61.6 1.0 %copy-start.9 = (f32[2,16,16]{2,1,0:T(8,128)S(1)}, f32[2,16,16]{2,1,0:T(8,128)}, u32[]{:S(2)}) copy-start(f32[2,16,16]{2,1,0:T(8,128)} %get-tuple-element.9) | copy-start | bytes 6148
  62.6 0.7 %copy-start.10 = (f32[16]{0:T(128)S(1)}, f32[16]{0:T(128)}, u32[]{:S(2)}) copy-start(f32[16]{0:T(128)} %param.10) | copy-start | bytes 196
  64.8 0.9 %copy-start.6 = (f32[2,16,16]{2,1,0:T(8,128)S(1)}, f32[2,16,16]{2,1,0:T(8,128)}, u32[]{:S(2)}) copy-start(f32[2,16,16]{2,1,0:T(8,128)} %get-tuple-element.10) | copy-start | bytes 6148

commit v3 on v1

v3 whole, which is shorter than its diff:
```python
import functools
import math

import jax
import jax.numpy as jnp
from jax import lax
from jax.experimental import pallas as pl
from jax.experimental.pallas import tpu as pltpu
from jax.sharding import PartitionSpec as P

HIGH_PREC = lax.Precision.HIGHEST


def mm(pattern, left_op, right_op):
    return jnp.einsum(pattern, left_op, right_op, precision=HIGH_PREC)


GROUP = 8
LANES = 128
SLAB_NAMES = ("fwd", "fwd_m", "bwd", "fold", "fold_v", "res", "mem", "skip")


def unpack(block, rows):
    return {name: block[i * rows:(i + 1) * rows] for i, name in enumerate(SLAB_NAMES)}


def chan_sum(value, modes):
    total = value[0:1]
    for row in range(1, value.shape[0]):
        total = total + value[row:row + 1]
    shift = LANES // 2
    while shift >= modes:
        total = total + pltpu.roll(total, shift, 1)
        shift //= 2
    return jnp.broadcast_to(total, value.shape)


def fold_items(items, coef_ref, rows, modes):
    acc = unpack(items[0], rows)
    coef = coef_ref[0]
    pre = coef[5:6] * acc["fwd"]
    post = coef[6:7] * acc["bwd"]
    for index in range(1, len(items)):
        item = unpack(items[index], rows)
        coef = coef_ref[index]
        step, step_len, lag, lag_q, inv_m = coef[0:1], coef[1:2], coef[2:3], coef[3:4], coef[4:5]
        pre = pre + coef[5:6] * item["fwd"]
        post = post + coef[6:7] * item["bwd"]
        cross_res = chan_sum(acc["fwd"] * item["fold"], modes)
        cross_mem = chan_sum(acc["fwd"] * item["fold_v"] + acc["fwd_m"] * item["fold"] * inv_m, modes)
        acc = {
            "fwd": step * acc["fwd"] + item["fwd"],
            "fwd_m": step * acc["fwd_m"] + step_len * acc["fwd"] + item["fwd_m"],
            "bwd": acc["bwd"] + lag * item["bwd"],
            "fold": acc["fold"] + lag * item["fold"],
            "fold_v": acc["fold_v"] + lag * item["fold_v"] + lag_q * item["fold"],
            "res": acc["res"] + item["res"] + cross_res,
            "mem": acc["mem"] + item["mem"] + cross_mem,
            "skip": acc["skip"] + item["skip"],
        }
    return acc, pre, post


def gather_ring(buf, send_sems, recv_sems, count, pos, device_of):
    descs = []
    for dist in range(1, count):
        desc = pltpu.make_async_remote_copy(
            src_ref=buf.at[0],
            dst_ref=buf.at[count - dist],
            send_sem=send_sems.at[dist],
            recv_sem=recv_sems.at[count - dist],
            device_id=device_of((pos + dist) % count),
            device_id_type=pl.DeviceIdType.MESH,
        )
        desc.start()
        descs.append(desc)
    for desc in descs:
        desc.wait_recv()
    for desc in descs:
        desc.wait_send()
    return [buf[(slot - pos + count) % count] for slot in range(count)]


def combine_kernel(counts, rows, modes, state_ref, coef_a, coef_b, fin_ref, out_ref,
                   buf_a, buf_b, buf_c, send_a, recv_a, send_b, recv_b, send_c, recv_c):
    count_a, count_b, count_c = counts
    seq_index = lax.axis_index("seq")
    ch_index = lax.axis_index("ch")
    pos_a = seq_index % count_a
    pos_b = seq_index // count_a

    def dev_a(other):
        return (pos_b * count_a + other, ch_index)

    def dev_b(other):
        return (other * count_a + pos_a, ch_index)

    def dev_c(other):
        return (seq_index, other)

    barrier = pltpu.get_barrier_semaphore()
    for count, pos, device_of in ((count_a, pos_a, dev_a), (count_b, pos_b, dev_b), (count_c, ch_index, dev_c)):
        for dist in range(1, count):
            pl.semaphore_signal(barrier, inc=1, device_id=device_of((pos + dist) % count),
                                device_id_type=pl.DeviceIdType.MESH)
    pl.semaphore_wait(barrier, count_a + count_b + count_c - 3)

    buf_a[0] = state_ref[...]
    items = gather_ring(buf_a, send_a, recv_a, count_a, pos_a, dev_a)
    group, pre_a, post_a = fold_items(items, coef_a, rows, modes)
    buf_b[0] = jnp.concatenate([group[name] for name in SLAB_NAMES], axis=0)
    items = gather_ring(buf_b, send_b, recv_b, count_b, pos_b, dev_b)
    total, pre_b, post_b = fold_items(items, coef_b, rows, modes)
    fin = fin_ref[...]
    pre = fin[0:1] * pre_b + pre_a
    post = fin[1:2] * post_b + post_a
    buf_c[0] = jnp.concatenate([total["res"], total["mem"]], axis=0)
    items = gather_ring(buf_c, send_c, recv_c, count_c, ch_index, dev_c)
    sums = items[0]
    for item in items[1:]:
        sums = sums + item
    out_ref[...] = jnp.concatenate([pre, post, sums, total["skip"], jnp.zeros_like(total["skip"])], axis=0)


def lanes_of(vec):
    return jnp.tile(vec, LANES // vec.shape[0])


def fold_coefs(count, size, pos, inv_m, block_len):
    def decay(blocks):
        return jnp.exp(-(blocks * block_len) * inv_m)

    step = decay(float(size))
    coefs = []
    for index in range(count):
        lag = decay(float(index * size))
        before = (index < pos).astype(jnp.float32) * decay(jnp.maximum(pos - 1 - index, 0).astype(jnp.float32) * size)
        after = (index > pos).astype(jnp.float32) * decay(jnp.maximum(index - pos - 1, 0).astype(jnp.float32) * size)
        rows = [step, step * float(size * block_len), lag, lag * float(index * size * block_len) * inv_m,
                inv_m, before, after, jnp.zeros_like(inv_m)]
        coefs.append(jnp.stack([lanes_of(r) for r in rows]))
    return jnp.stack(coefs)


def combine_states(slabs, inv_m, block_len):
    channels, modes = slabs[0].shape
    rows = channels * modes // LANES
    seq_index = lax.axis_index("seq")
    count_a = min(GROUP, lax.axis_size("seq"))
    count_b = lax.axis_size("seq") // count_a
    count_c = lax.axis_size("ch")
    pos_a = seq_index % count_a
    pos_b = seq_index // count_a
    state = jnp.concatenate([s.reshape(rows, LANES) for s in slabs], axis=0)
    coef_a = fold_coefs(count_a, 1, pos_a, inv_m, block_len)
    coef_b = fold_coefs(count_b, count_a, pos_b, inv_m, block_len)
    near = jnp.exp(-(pos_a * block_len).astype(jnp.float32) * inv_m)
    far = jnp.exp(-((count_a - 1 - pos_a) * block_len).astype(jnp.float32) * inv_m)
    fin = jnp.stack([lanes_of(near), lanes_of(far)] + [lanes_of(jnp.zeros_like(inv_m))] * 6)
    msg = (len(SLAB_NAMES) * rows, LANES)
    vmem = pl.BlockSpec(memory_space=pltpu.VMEM)
    out = pl.pallas_call(
        functools.partial(combine_kernel, (count_a, count_b, count_c), rows, modes),
        out_shape=jax.ShapeDtypeStruct((6 * rows, LANES), jnp.float32),
        in_specs=[vmem] * 4,
        out_specs=vmem,
        scratch_shapes=[
            pltpu.VMEM((count_a,) + msg, jnp.float32),
            pltpu.VMEM((count_b,) + msg, jnp.float32),
            pltpu.VMEM((count_c, 2 * rows, LANES), jnp.float32),
            pltpu.SemaphoreType.DMA((count_a,)),
            pltpu.SemaphoreType.DMA((count_a,)),
            pltpu.SemaphoreType.DMA((count_b,)),
            pltpu.SemaphoreType.DMA((count_b,)),
            pltpu.SemaphoreType.DMA((count_c,)),
            pltpu.SemaphoreType.DMA((count_c,)),
        ],
        compiler_params=pltpu.CompilerParams(collective_id=0, has_side_effects=True),
    )(state, coef_a, coef_b, fin)
    pieces = [out[i * rows:(i + 1) * rows].reshape(channels, modes) for i in range(5)]
    return pieces


def per_device(signal_x, gate_q, gate_k, skip_gain, residue, memory, cotangent):
    channels, block_len = signal_x.shape
    seq_total = lax.axis_size("seq") * block_len
    all_channels = channels * lax.axis_size("ch")
    inv_m = 1.0 / memory
    gain = jnp.sqrt(2.0 / memory)
    amp = residue * gain
    offs = jnp.arange(block_len, dtype=jnp.float32)[:, None]
    e_down = jnp.exp(-offs * inv_m)
    e_up = jnp.exp(offs * inv_m)
    e_tail = jnp.exp(-(block_len - 1 - offs) * inv_m)
    e_next = jnp.exp(-(offs + 1) * inv_m)
    e_in = jnp.exp(-(block_len - offs) * inv_m)
    lower = offs >= offs.T
    toeplitz = jnp.where(lower, mm("tn,sn->ts", e_down * amp, e_up), 0.0)

    x_float = signal_x.astype(jnp.float32)
    q_float = gate_q.astype(jnp.float32)
    k_float = gate_k.astype(jnp.float32)
    d_float = cotangent.astype(jnp.float32)
    values = x_float * k_float
    grad_mixed = d_float * q_float

    conv_local = mm("cs,ts->ct", values, toeplitz)
    corr_local = mm("ct,ts->cs", grad_mixed, toeplitz)
    fwd = mm("cs,sn->cn", values, e_tail)
    fwd_m = mm("cs,sn->cn", values, e_tail * (block_len - 1 - offs))
    bwd = mm("ct,tn->cn", grad_mixed, e_down)
    fold = mm("ct,tn->cn", grad_mixed, e_next)
    fold_m = mm("ct,tn->cn", grad_mixed, e_next * (offs + 1) * inv_m)
    pair = jnp.where(lower, mm("ct,cs->ts", grad_mixed, values), 0.0)
    near = mm("ts,sn->tn", pair, e_up)
    near_m = mm("ts,sn->tn", pair, e_up * offs * inv_m)
    local_res = jnp.sum(e_down * near, axis=0)
    local_mem = jnp.sum(e_down * ((offs * inv_m - 0.5) * near - near_m), axis=0)

    part_skip = jnp.sum(grad_mixed * values, axis=1)
    slabs = [fwd, fwd_m, bwd, fold, fold_m - 0.5 * fold]
    slabs += [jnp.broadcast_to(v, fwd.shape) for v in (local_res[None, :], local_mem[None, :], part_skip[:, None])]
    pre, post, res_sum, mem_sum, skip_sum = combine_states(slabs, inv_m, block_len)

    conv_out = conv_local + mm("cn,tn->ct", pre, e_next * amp)
    corr_out = corr_local + mm("cn,sn->cs", post, e_in * amp)

    mixed_out = conv_out + skip_gain[:, None] * values
    output = (q_float * mixed_out).astype(jnp.bfloat16)
    grad_values = skip_gain[:, None] * grad_mixed + corr_out
    grad_x = (grad_values * k_float).astype(jnp.bfloat16)
    grad_q = (d_float * mixed_out).astype(jnp.bfloat16)
    grad_k = (grad_values * x_float).astype(jnp.bfloat16)

    norm_scale = 1.0 / math.sqrt(all_channels * seq_total)
    grad_skip = skip_sum[:, 0] / math.sqrt(seq_total)
    grad_residue = gain * res_sum[0] * norm_scale
    grad_memory = residue * gain * mem_sum[0] * norm_scale
    return (output, grad_x, grad_q, grad_k, grad_skip, grad_residue, grad_memory)


def solution(mesh):
    return jax.shard_map(
        per_device,
        mesh=mesh,
        in_specs=(
            P("ch", "seq"),
            P("ch", "seq"),
            P("ch", "seq"),
            P("ch"),
            P(),
            P(),
            P("ch", "seq"),
        ),
        out_specs=(
            P("ch", "seq"),
            P("ch", "seq"),
            P("ch", "seq"),
            P("ch", "seq"),
            P("ch"),
            P(),
            P(),
        ),
        check_vma=False,
    )
```

time: 122 us -> 60.3 us (0.49)
  starting transfers between devices: 91 us -> 0 us
  Pallas kernels: 0 us -> 32.2 us
  waiting for transfers between devices: 17.4 us -> 0 us
  local copies, waits for them, and re-layouts: 1.9 us -> 15.4 us
    ppermute x16 -> x0, starting transfers between devices: 91 us -> none  [exchange(): return lax.ppermute(shard, axis, [(i, i ^ 1 << bit) for i in range(size)])]
    pallas_call x0 -> x1, Pallas kernels: none -> 32.2 us  [combine_states(): pl.pallas_call(functools.partial(combine_kernel, (count_a, count_b, count...]
    ppermute x16 -> x0, waiting for transfers between devices: 17.4 us -> none  [exchange(): return lax.ppermute(shard, axis, [(i, i ^ 1 << bit) for i in range(size)])]
    another operation x0 -> x228, local copies, waits for them, and re-layouts: none -> 9.05 us  [the longest x121 8.54 us: fold_coefs(): coefs.append(jnp.stack([lanes_of(r) for r in rows]))]
    concatenate x0 -> x1, local copies, waits for them, and re-layouts: none -> 1.22 us  [combine_states(): state = jnp.concatenate([s.reshape(rows, LANES) for s in slabs], axis=0)]
    unnamed x14 -> x41, local copies, waits for them, and re-layouts: 1.9 us -> 2.94 us
  transfers between devices with their start and end apart: 16 -> 0, of which waited for: 16 -> 0; matrix products, arithmetic and copies ran while one was open for 3% -> 0% of each run, Pallas kernels for 0% -> 0%
where the time goes in v3:
time: 60.3 us; the launch traced here: 59.9 us
  Pallas kernels  32.2 us (53%)
  local copies, waits for them, and re-layouts  15.4 us (26%)
  matrix products  8.9 us (15%)
  other arithmetic  2.04 us (3%)
  between operations  1.43 us (2%)
    pallas_call x1, Pallas kernels, combine_states(): pl.pallas_call(functools.partial(combine_kernel, (count_a, count_b, count...  32.2 us
    dot_general x13, matrix products, mm(): return jnp.einsum(pattern, left_op, right_op, precision=HIGH_PREC)  8.9 us
    another operation x121, local copies, waits for them, and re-layouts, fold_coefs(): coefs.append(jnp.stack([lanes_of(r) for r in rows]))  8.54 us
    unnamed x41, local copies, waits for them, and re-layouts  2.94 us
    concatenate x1, local copies, waits for them, and re-layouts, combine_states(): state = jnp.concatenate([s.reshape(rows, LANES) for s in slabs], axis=0)  1.22 us

profile of v3, /device:TPU:1, one launch (start us, length us, event | category | flops | bytes accessed | tf_op | source)
XLA Modules:
  0.0 59.9 jit_solution(12539248006714289331)
XLA Ops:
  0.7 0.6 %copy-done.6 = f32[16]{0:T(128)S(1)} copy-done((f32[16]{0:T(128)S(1)}, f32[16]{0:T(128)}, u32[]{:S(2)}) %copy-start.6) | copy-done | bytes 88
  1.4 0.2 fusion.20
  1.6 0.1 reshape.186
  1.7 0.2 fusion.18
  2.0 0.1 reshape.187
  2.1 0.4 copy-done
  2.5 0.2 fusion.27
  2.7 0.1 reshape.188
  2.8 0.2 fusion.17
  3.0 0.1 reshape.189
  3.1 0.2 convolution_subtract_fusion.1
  3.4 0.1 reshape.190
  3.5 1.1 %convolution_select_fusion = f32[512,512]{1,0:T(8,128)S(1)} fusion(bf16[16,512]{1,0:T(8,128)(2,1)S(1)} %copy-done.2, bf16[16,512]{1,0:T(8,128)(2,1)S(1)} %copy-done.3, bf16[16,512]{1,0:T(8,128)(2,1)S(1)} %copy-done, bf16[16,512]{1,0:T(8,128)(2,1)S(1)} %copy-done.1), kind=kOutput, calls=%fused_computation | convolution fusion | flops 50905088 | bytes 1114112 | tf_op jit(solution)/shard_map/ct,cs->ts/dot_general | solution.py:15
  4.6 1.1 %multiply_reduce_fusion.1 = (f32[16]{0:T(128)S(1)}, f32[512,16]{0,1:T(8,128)S(1)}) fusion(f32[16]{0:T(128)S(1)} %get-tuple-element.11, f32[512]{0:T(512)S(1)} %iota_negate_fusion, f32[512,512]{1,0:T(8,128)S(1)} %convolution_select_fusion), kind=kOutput, calls=%fused_computation.53 | convolution fusion | flops 50364400 | bytes 1083520 | tf_op jit(solution)/shard_map/ts,sn->tn/dot_general | solution.py:15
  5.8 1.1 %fusion.3 = f32[16]{0:T(128)S(1)} fusion(f32[512,512]{1,0:T(8,128)S(1)} %convolution_select_fusion, f32[512,16]{0,1:T(8,128)S(1)} %get-tuple-element.119, f32[16]{0:T(128)S(1)} %get-tuple-element.11, f32[512]{0:T(512)S(1)} %iota_negate_fusion), kind=kOutput, calls=%fused_computation.8 | convolution fusion | flops 50413552 | bytes 1083520 | tf_op jit(solution)/shard_map/ts,sn->tn/dot_general | solution.py:15
  7.0 0.1 multiply_reduce_fusion
  7.1 0.1 broadcast_in_dim.56
  7.3 0.1 broadcast_in_dim.58
  7.4 1.2 %concatenate.3.state_ref = f32[16,128]{1,0:T(8,128)} concatenate(f32[2,128]{1,0:T(2,128)S(1)} %reshape.186, f32[2,128]{1,0:T(2,128)S(1)} %reshape.187, f32[2,128]{1,0:T(2,128)S(1)} %reshape.188, f32[2,128]{1,0:T(2,128)S(1)} %reshape.189, f32[2,128]{1,0:T(2,128)S(1)} %reshape.190, f32[2,128]{1,0:T(2,128)S(1)} %broadcast_in_dim.26, f32[2,128]{1,0:T(2,128)S(1)} %broadcast_in_dim.55, ...), dimensions={0} | concatenate | bytes 16384 | tf_op jit(solution)/shard_map/concatenate | solution.py:154
  8.7 0.1 stack_tile.369
  8.8 0.1 stack_tile.370
  8.9 0.1 stack_tile.371
  9.0 0.1 stack_tile.372
  9.2 0.1 stack_tile.374
  9.4 0.1 stack_tile.376
  9.5 0.1 stack_tile.377
  9.7 0.1 stack_tile.379
  9.9 0.1 stack_tile.381
  10.1 0.1 stack_tile.383
  10.2 0.1 stack_tile.384
  10.3 0.1 stack_tile.385
  10.5 0.1 stack_tile.387
  10.6 0.1 stack_tile.388
  10.9 0.1 stack_tile.391
  11.0 0.1 stack_tile.392
  11.1 0.1 stack_tile.393
  11.3 0.1 stack_tile.395
  11.4 0.1 stack_tile.396
  11.7 0.1 stack_tile.399
  11.8 0.1 stack_tile.400
  11.9 0.1 stack_tile.401
  12.1 0.1 stack_tile.403
  12.2 0.1 stack_tile.404
  12.3 0.1 stack_tile.405
  12.5 0.1 stack_tile.407
  12.6 0.1 stack_tile.408
  12.8 0.1 stack_tile.410
  12.9 0.1 stack_tile.411
  13.0 0.1 stack_tile.412
  13.2 0.1 stack_tile.414
  18.5 0.7 %maximum_maximum_fusion.fin_ref = f32[8,128]{1,0:T(8,128)} fusion(f32[1,128]{1,0:T(1,128)S(1)} %stack_tile.466, f32[1,128]{1,0:T(1,128)S(1)} %stack_tile.465, f32[8]{0:T(128)S(1)} %pad.3.clone, f32[8]{0:T(128)S(1)} %pad.2.clone), kind=kLoop, calls=%fused_computation.94 | loop fusion | flops 3072 | bytes 5184 | tf_op jit(solution)/shard_map/stack | solution.py:159
  19.2 32.2 %shard_map.126 = f32[12,128]{1,0:T(8,128)} custom-call(f32[16,128]{1,0:T(8,128)} %concatenate.3.state_ref, f32[8,8,128]{2,1,0:T(8,128)} %copy-done.5, f32[16,8,128]{2,1,0:T(8,128)} %copy-done.4, f32[8,128]{1,0:T(8,128)} %maximum_maximum_fusion.fin_ref), custom_call_target="tpu_custom_call" | custom-call | tf_op jit(solution)/shard_map/pallas_call | solution.py:162
  51.4 0.8 %fusion.61 = (f32[2,128]{1,0:T(2,128)S(1)}, f32[2,128]{1,0:T(2,128)S(1)}, f32[2,128]{1,0:T(2,128)S(1)}, f32[2,128]{1,0:T(2,128)S(1)}, f32[2,128]{1,0:T(2,128)S(1)}) fusion(f32[12,128]{1,0:T(8,128)} %shard_map.126), kind=kLoop, calls=%fused_computation.207 | loop fusion | bytes 10240 | tf_op jit(solution)/shard_map/slice | solution.py:180
  52.3 0.6 copy-done.7
  52.9 0.5 fusion.56
  53.4 1.1 %convolution_select_fusion.1 = f32[512,512]{1,0:T(8,128)S(1)} fusion(f32[16]{0:T(128)S(1)} %get-tuple-element.8, f32[16]{0:T(128)S(1)} %get-tuple-element.11, f32[512]{0:T(512)S(1)} %iota_negate_fusion), kind=kOutput, calls=%fused_computation.1 | convolution fusion | flops 50880512 | bytes 1050752 | tf_op jit(solution)/shard_map/tn,sn->ts/dot_general | solution.py:15
  54.6 1.0 %fusion.28 = f32[16,512]{1,0:T(8,128)S(1)} fusion(f32[512,512]{1,0:T(8,128)S(1)} %convolution_select_fusion.1, bf16[16,512]{1,0:T(8,128)(2,1)S(1)} %copy-done.2, bf16[16,512]{1,0:T(8,128)(2,1)S(1)} %copy-done.3), kind=kOutput, calls=%fused_computation.68 | convolution fusion | flops 50356224 | bytes 1114112 | tf_op jit(solution)/shard_map/cs,ts->ct/dot_general | solution.py:15
  55.5 0.1 reshape.191
  55.6 0.6 copy-done.8
  56.2 0.9 %fusion.7 = (bf16[16,512]{1,0:T(8,128)(2,1)}, bf16[16,512]{1,0:T(8,128)(2,1)}) fusion(bf16[16,512]{1,0:T(8,128)(2,1)S(1)} %copy-done, bf16[16,512]{1,0:T(8,128)(2,1)S(1)} %copy-done.1, bf16[16,512]{1,0:T(8,128)(2,1)S(1)} %copy-done.2, bf16[16,512]{1,0:T(8,128)(2,1)S(1)} %copy-done.3, f32[16]{0:T(128)S(1)} %copy-done.8, f32[16,512]{1,0:T(8,128)S(1)} %fusion.28, ...), kind=kOutput, calls=%fused_computation.44 | convolution fusion | flops 1687552 | bytes 134336 | tf_op jit(solution)/shard_map/cn,tn->ct/dot_general | solution.py:15
  57.0 0.6 %fusion.29 = f32[16,512]{1,0:T(8,128)S(1)} fusion(f32[512,512]{1,0:T(8,128)S(1)} %convolution_select_fusion.1, bf16[16,512]{1,0:T(8,128)(2,1)S(1)} %copy-done, bf16[16,512]{1,0:T(8,128)(2,1)S(1)} %copy-done.1), kind=kOutput, calls=%fused_computation.69 | convolution fusion | flops 50356224 | bytes 1114112 | tf_op jit(solution)/shard_map/ct,ts->cs/dot_general | solution.py:15
  57.8 0.9 %fusion.5 = (bf16[16,512]{1,0:T(8,128)(2,1)}, bf16[16,512]{1,0:T(8,128)(2,1)}) fusion(bf16[16,512]{1,0:T(8,128)(2,1)S(1)} %copy-done.3, bf16[16,512]{1,0:T(8,128)(2,1)S(1)} %copy-done.2, f32[16,512]{1,0:T(8,128)S(1)} %fusion.29, f32[16,16]{1,0:T(8,128)S(1)} %reshape.192, f32[512]{0:T(512)S(1)} %subtract_negate_fusion, f32[16]{0:T(128)S(1)} %get-tuple-element.8, ...), kind=kOutput, calls=%fused_computation.42 | convolution fusion | flops 1687552 | bytes 134336 | tf_op jit(solution)/shard_map/cn,sn->cs/dot_general | solution.py:15
  58.7 0.6 copy.16
  59.4 0.5 fusion.58
  (256 shorter events, 7.5 us)
Async XLA Ops:
  0.6 0.7 %copy-start.6 = (f32[16]{0:T(128)S(1)}, f32[16]{0:T(128)}, u32[]{:S(2)}) copy-start(f32[16]{0:T(128)} %param.12) | copy-start | bytes 196
  0.7 0.7 %copy-start.2 = (bf16[16,512]{1,0:T(8,128)(2,1)S(1)}, bf16[16,512]{1,0:T(8,128)(2,1)}, u32[]{:S(2)}) copy-start(bf16[16,512]{1,0:T(8,128)(2,1)} %param.9) | copy-start | bytes 49156
  0.7 0.7 %copy-start.3 = (bf16[16,512]{1,0:T(8,128)(2,1)S(1)}, bf16[16,512]{1,0:T(8,128)(2,1)}, u32[]{:S(2)}) copy-start(bf16[16,512]{1,0:T(8,128)(2,1)} %param.7) | copy-start | bytes 49156
  1.7 0.7 %copy-start = (bf16[16,512]{1,0:T(8,128)(2,1)S(1)}, bf16[16,512]{1,0:T(8,128)(2,1)}, u32[]{:S(2)}) copy-start(bf16[16,512]{1,0:T(8,128)(2,1)} %param.13) | copy-start | bytes 49156
  1.7 0.7 %copy-start.1 = (bf16[16,512]{1,0:T(8,128)(2,1)S(1)}, bf16[16,512]{1,0:T(8,128)(2,1)}, u32[]{:S(2)}) copy-start(bf16[16,512]{1,0:T(8,128)(2,1)} %param.8) | copy-start | bytes 49156
  18.2 1.0 %copy-start.4 = (f32[16,8,128]{2,1,0:T(8,128)}, f32[16,8,128]{2,1,0:T(8,128)S(1)}, u32[]{:S(2)}) copy-start(f32[16,8,128]{2,1,0:T(8,128)S(1)} %get-tuple-element.125.coef_b) | copy-start | bytes 196612
  18.2 1.0 %copy-start.5 = (f32[8,8,128]{2,1,0:T(8,128)}, f32[8,8,128]{2,1,0:T(8,128)S(1)}, u32[]{:S(2)}) copy-start(f32[8,8,128]{2,1,0:T(8,128)S(1)} %get-tuple-element.124.coef_a) | copy-start | bytes 98308
  52.2 0.7 %copy-start.7 = (f32[16]{0:T(128)S(1)}, f32[16]{0:T(128)}, u32[]{:S(2)}) copy-start(f32[16]{0:T(128)} %param.11) | copy-start | bytes 196
  55.5 0.7 %copy-start.8 = (f32[16]{0:T(128)S(1)}, f32[16]{0:T(128)}, u32[]{:S(2)}) copy-start(f32[16]{0:T(128)} %param.10) | copy-start | bytes 196

commit v4 on v3

--- a/solution.py
+++ b/solution.py
@@ -127,19 +127,17 @@
 
 
 def fold_coefs(count, size, pos, inv_m, block_len):
-    def decay(blocks):
-        return jnp.exp(-(blocks * block_len) * inv_m)
-
-    step = decay(float(size))
-    coefs = []
-    for index in range(count):
-        lag = decay(float(index * size))
-        before = (index < pos).astype(jnp.float32) * decay(jnp.maximum(pos - 1 - index, 0).astype(jnp.float32) * size)
-        after = (index > pos).astype(jnp.float32) * decay(jnp.maximum(index - pos - 1, 0).astype(jnp.float32) * size)
-        rows = [step, step * float(size * block_len), lag, lag * float(index * size * block_len) * inv_m,
-                inv_m, before, after, jnp.zeros_like(inv_m)]
-        coefs.append(jnp.stack([lanes_of(r) for r in rows]))
-    return jnp.stack(coefs)
+    inv = lanes_of(inv_m)[None, :]
+    index = jnp.arange(count, dtype=jnp.int32)[:, None]
+    span = float(size * block_len)
+    step = jnp.broadcast_to(jnp.exp(-span * inv), (count, LANES))
+    starts = index.astype(jnp.float32) * span
+    lag = jnp.exp(-starts * inv)
+    before = jnp.where(index < pos, jnp.exp(-((pos - 1 - index).astype(jnp.float32) * span) * inv), 0.0)
+    after = jnp.where(index > pos, jnp.exp(-((index - pos - 1).astype(jnp.float32) * span) * inv), 0.0)
+    rows = [step, step * span, lag, lag * starts * inv, jnp.broadcast_to(inv, (count, LANES)), before, after,
+            jnp.zeros((count, LANES), jnp.float32)]
+    return jnp.stack(rows, axis=1)
 
 
 def combine_states(slabs, inv_m, block_len):

time: 60.3 us -> 52.8 us (0.88)
  local copies, waits for them, and re-layouts: 15.4 us -> 8.21 us
    another operation x123 -> x7, local copies, waits for them, and re-layouts: 8.54 us -> 1.48 us  [the longest x6 1.4 us: fold_coefs(): return jnp.stack(rows, axis=1)]
    unnamed x41 -> x15, local copies, waits for them, and re-layouts: 2.94 us -> 2.86 us
where the time goes in v4:
time: 52.8 us; the launch traced here: 52.4 us
  Pallas kernels  32.2 us (61%)
  matrix products  8.91 us (17%)
  local copies, waits for them, and re-layouts  8.21 us (16%)
  other arithmetic  2.22 us (4%)
  between operations  0.86 us (2%)
    pallas_call x1, Pallas kernels, combine_states(): pl.pallas_call(functools.partial(combine_kernel, (count_a, count_b, count...  32.2 us
    dot_general x13, matrix products, mm(): return jnp.einsum(pattern, left_op, right_op, precision=HIGH_PREC)  8.91 us
    unnamed x15, local copies, waits for them, and re-layouts  2.86 us
    another operation x6, local copies, waits for them, and re-layouts, fold_coefs(): return jnp.stack(rows, axis=1)  1.4 us
    concatenate x1, local copies, waits for them, and re-layouts, combine_states(): state = jnp.concatenate([s.reshape(rows, LANES) for s in slabs], axis=0)  1.22 us

profile of v4, /device:TPU:1, one launch (start us, length us, event | category | flops | bytes accessed | tf_op | source)
XLA Modules:
  0.0 52.4 jit_solution(17266593368321808573)
XLA Ops:
  0.6 0.0 copy-start.4
  0.7 0.0 copy-start.2
  0.7 0.0 copy-start.3
  0.7 0.6 %copy-done.4 = f32[16]{0:T(128)S(1)} copy-done((f32[16]{0:T(128)S(1)}, f32[16]{0:T(128)}, u32[]{:S(2)}) %copy-start.4) | copy-done | bytes 88
  1.3 0.1 copy-done.2
  1.4 0.0 copy-done.3
  1.4 0.2 fusion.20
  1.6 0.1 reshape.801
  1.7 0.0 copy-start
  1.7 0.0 copy-start.1
  1.7 0.2 fusion.18
  2.0 0.1 reshape.802
  2.1 0.4 copy-done
  2.5 0.0 copy-done.1
  2.5 0.2 fusion.27
  2.7 0.1 reshape.803
  2.8 0.2 fusion.17
  3.0 0.1 reshape.804
  3.1 0.2 convolution_subtract_fusion.1
  3.4 0.1 reshape.805
  3.5 1.1 %convolution_select_fusion = f32[512,512]{1,0:T(8,128)S(1)} fusion(bf16[16,512]{1,0:T(8,128)(2,1)S(1)} %copy-done.2, bf16[16,512]{1,0:T(8,128)(2,1)S(1)} %copy-done.3, bf16[16,512]{1,0:T(8,128)(2,1)S(1)} %copy-done, bf16[16,512]{1,0:T(8,128)(2,1)S(1)} %copy-done.1), kind=kOutput, calls=%fused_computation | convolution fusion | flops 50905088 | bytes 1114112 | tf_op jit(solution)/shard_map/ct,cs->ts/dot_general | solution.py:15
  4.6 1.1 %multiply_reduce_fusion.1 = (f32[16]{0:T(128)S(1)}, f32[512,16]{0,1:T(8,128)S(1)}) fusion(f32[16]{0:T(128)S(1)} %get-tuple-element.11, f32[512]{0:T(512)S(1)} %iota_negate_fusion, f32[512,512]{1,0:T(8,128)S(1)} %convolution_select_fusion), kind=kOutput, calls=%fused_computation.29 | convolution fusion | flops 50364400 | bytes 1083520 | tf_op jit(solution)/shard_map/ts,sn->tn/dot_general | solution.py:15
  5.7 0.1 broadcast_in_dim.95
  5.8 1.1 %fusion.3 = f32[16]{0:T(128)S(1)} fusion(f32[512,512]{1,0:T(8,128)S(1)} %convolution_select_fusion, f32[512,16]{0,1:T(8,128)S(1)} %get-tuple-element.34, f32[16]{0:T(128)S(1)} %get-tuple-element.11, f32[512]{0:T(512)S(1)} %iota_negate_fusion), kind=kOutput, calls=%fused_computation.8 | convolution fusion | flops 50413552 | bytes 1083520 | tf_op jit(solution)/shard_map/ts,sn->tn/dot_general | solution.py:15
  6.9 0.1 broadcast_in_dim.98
  7.0 0.1 multiply_reduce_fusion
  7.1 0.1 broadcast_in_dim.100
  7.2 0.1 broadcast_in_dim.101
  7.3 0.1 broadcast_in_dim.102
  7.4 1.2 %concatenate.3.state_ref = f32[16,128]{1,0:T(8,128)} concatenate(f32[2,128]{1,0:T(2,128)S(1)} %reshape.801, f32[2,128]{1,0:T(2,128)S(1)} %reshape.802, f32[2,128]{1,0:T(2,128)S(1)} %reshape.803, f32[2,128]{1,0:T(2,128)S(1)} %reshape.804, f32[2,128]{1,0:T(2,128)S(1)} %reshape.805, f32[2,128]{1,0:T(2,128)S(1)} %broadcast_in_dim.96, f32[2,128]{1,0:T(2,128)S(1)} %broadcast_in_dim.99, ...), dimensions={0} | concatenate | bytes 16384 | tf_op jit(solution)/shard_map/concatenate | solution.py:152
  8.6 0.1 broadcast_in_dim_tile.4
  8.7 0.1 mul.507
  8.8 0.1 multiply_multiply_fusion.1
  9.0 0.7 %stack.30.coef_a = f32[8,8,128]{2,1,0:T(8,128)} concatenate(f32[8,1,128]{2,1,0:T(1,128)S(1)} %stack_broadcast_in_dim.4, f32[8,1,128]{2,1,0:T(1,128)S(1)} %stack.14, f32[8,1,128]{2,1,0:T(1,128)S(1)} %get-tuple-element.24, f32[8,1,128]{2,1,0:T(1,128)S(1)} %get-tuple-element.23, f32[8,1,128]{2,1,0:T(1,128)S(1)} %mul.508, f32[8,1,128]{2,1,0:T(1,128)S(1)} %get-tuple-element.32, ...), dimensions={1} | concatenate | bytes 65536 | tf_op jit(solution)/shard_map/stack | solution.py:140
  9.7 0.1 mul.524
  9.7 0.2 multiply_multiply_fusion
  9.9 0.7 %stack.32.coef_b = f32[16,8,128]{2,1,0:T(8,128)} concatenate(f32[16,1,128]{2,1,0:T(1,128)S(1)} %stack_broadcast_in_dim.5, f32[16,1,128]{2,1,0:T(1,128)S(1)} %stack.31, f32[16,1,128]{2,1,0:T(1,128)S(1)} %get-tuple-element.17, f32[16,1,128]{2,1,0:T(1,128)S(1)} %get-tuple-element.16, f32[16,1,128]{2,1,0:T(1,128)S(1)} %mul.525, f32[16,1,128]{2,1,0:T(1,128)S(1)} %get-tuple-element.26, ...), dimensions={1} | concatenate | bytes 131072 | tf_op jit(solution)/shard_map/stack | solution.py:140
  10.7 0.1 stack_tile.7
  10.8 0.1 stack_tile.6
  10.8 0.1 pad.3.clone
  10.9 0.1 pad.2.clone
  11.0 0.7 %maximum_maximum_fusion.fin_ref = f32[8,128]{1,0:T(8,128)} fusion(f32[1,128]{1,0:T(1,128)S(1)} %stack_tile.7, f32[1,128]{1,0:T(1,128)S(1)} %stack_tile.6, f32[8]{0:T(128)S(1)} %pad.3.clone, f32[8]{0:T(128)S(1)} %pad.2.clone), kind=kLoop, calls=%fused_computation.76 | loop fusion | flops 3072 | bytes 5184 | tf_op jit(solution)/shard_map/stack | solution.py:157
  11.7 32.2 %shard_map.126 = f32[12,128]{1,0:T(8,128)} custom-call(f32[16,128]{1,0:T(8,128)} %concatenate.3.state_ref, f32[8,8,128]{2,1,0:T(8,128)} %stack.30.coef_a, f32[16,8,128]{2,1,0:T(8,128)} %stack.32.coef_b, f32[8,128]{1,0:T(8,128)} %maximum_maximum_fusion.fin_ref), custom_call_target="tpu_custom_call" | custom-call | tf_op jit(solution)/shard_map/pallas_call | solution.py:160
  43.8 0.8 %fusion.61 = (f32[2,128]{1,0:T(2,128)S(1)}, f32[2,128]{1,0:T(2,128)S(1)}, f32[2,128]{1,0:T(2,128)S(1)}, f32[2,128]{1,0:T(2,128)S(1)}, f32[2,128]{1,0:T(2,128)S(1)}) fusion(f32[12,128]{1,0:T(8,128)} %shard_map.126), kind=kLoop, calls=%fused_computation.111 | loop fusion | bytes 10240 | tf_op jit(solution)/shard_map/slice | solution.py:178
  44.7 0.0 copy-start.5
  44.7 0.1 reshape.810
  44.8 0.6 %copy-done.5 = f32[16]{0:T(128)S(1)} copy-done((f32[16]{0:T(128)S(1)}, f32[16]{0:T(128)}, u32[]{:S(2)}) %copy-start.5) | copy-done | bytes 88
  45.3 0.5 %fusion.56 = (f32[16]{0:T(128)}, f32[16]{0:T(128)S(1)}, f32[16]{0:T(128)S(1)}) fusion(f32[16,16]{1,0:T(8,128)S(1)} %reshape.810, f32[16]{0:T(128)S(1)} %copy-done.5, f32[16]{0:T(128)S(1)} %copy-done.4), kind=kLoop, calls=%fused_computation.87 | loop fusion | flops 64 | bytes 384 | tf_op jit(solution)/shard_map/mul | solution.py:236
  45.9 1.2 %convolution_select_fusion.1 = f32[512,512]{1,0:T(8,128)S(1)} fusion(f32[16]{0:T(128)S(1)} %get-tuple-element.8, f32[16]{0:T(128)S(1)} %get-tuple-element.11, f32[512]{0:T(512)S(1)} %iota_negate_fusion), kind=kOutput, calls=%fused_computation.1 | convolution fusion | flops 50880512 | bytes 1050752 | tf_op jit(solution)/shard_map/tn,sn->ts/dot_general | solution.py:15
  47.0 1.0 %fusion.28 = f32[16,512]{1,0:T(8,128)S(1)} fusion(f32[512,512]{1,0:T(8,128)S(1)} %convolution_select_fusion.1, bf16[16,512]{1,0:T(8,128)(2,1)S(1)} %copy-done.2, bf16[16,512]{1,0:T(8,128)(2,1)S(1)} %copy-done.3), kind=kOutput, calls=%fused_computation.44 | convolution fusion | flops 50356224 | bytes 1114112 | tf_op jit(solution)/shard_map/cs,ts->ct/dot_general | solution.py:15
  48.0 0.0 copy-start.6
  48.0 0.1 reshape.806
  48.1 0.6 %copy-done.6 = f32[16]{0:T(128)S(1)} copy-done((f32[16]{0:T(128)S(1)}, f32[16]{0:T(128)}, u32[]{:S(2)}) %copy-start.6) | copy-done | bytes 88
  48.7 0.9 %fusion.7 = (bf16[16,512]{1,0:T(8,128)(2,1)}, bf16[16,512]{1,0:T(8,128)(2,1)}) fusion(bf16[16,512]{1,0:T(8,128)(2,1)S(1)} %copy-done, bf16[16,512]{1,0:T(8,128)(2,1)S(1)} %copy-done.1, bf16[16,512]{1,0:T(8,128)(2,1)S(1)} %copy-done.2, bf16[16,512]{1,0:T(8,128)(2,1)S(1)} %copy-done.3, f32[16]{0:T(128)S(1)} %copy-done.6, f32[16,512]{1,0:T(8,128)S(1)} %fusion.28, ...), kind=kOutput, calls=%fused_computation.20 | convolution fusion | flops 1687552 | bytes 134336 | tf_op jit(solution)/shard_map/cn,tn->ct/dot_general | solution.py:15
  49.5 0.6 %fusion.29 = f32[16,512]{1,0:T(8,128)S(1)} fusion(f32[512,512]{1,0:T(8,128)S(1)} %convolution_select_fusion.1, bf16[16,512]{1,0:T(8,128)(2,1)S(1)} %copy-done, bf16[16,512]{1,0:T(8,128)(2,1)S(1)} %copy-done.1), kind=kOutput, calls=%fused_computation.45 | convolution fusion | flops 50356224 | bytes 1114112 | tf_op jit(solution)/shard_map/ct,ts->cs/dot_general | solution.py:15
  50.1 0.1 reshape.807
  50.2 0.9 %fusion.5 = (bf16[16,512]{1,0:T(8,128)(2,1)}, bf16[16,512]{1,0:T(8,128)(2,1)}) fusion(bf16[16,512]{1,0:T(8,128)(2,1)S(1)} %copy-done.3, bf16[16,512]{1,0:T(8,128)(2,1)S(1)} %copy-done.2, f32[16,512]{1,0:T(8,128)S(1)} %fusion.29, f32[16,16]{1,0:T(8,128)S(1)} %reshape.807, f32[512]{0:T(512)S(1)} %subtract_negate_fusion, f32[16]{0:T(128)S(1)} %get-tuple-element.8, ...), kind=kOutput, calls=%fused_computation.18 | convolution fusion | flops 1687552 | bytes 134336 | tf_op jit(solution)/shard_map/cn,sn->cs/dot_general | solution.py:15
  51.1 0.1 reshape.808
  51.2 0.6 %copy.19 = f32[16,1]{0,1:T(1,128)} copy(f32[16,1]{1,0:T(8,128)S(1)} %slice_multiply_fusion) | data formatting | bytes 128
  51.8 0.1 reshape.809
  51.8 0.5 fusion.58
  (33 shorter events, 0.2 us)
Async XLA Ops:
  0.6 0.7 %copy-start.4 = (f32[16]{0:T(128)S(1)}, f32[16]{0:T(128)}, u32[]{:S(2)}) copy-start(f32[16]{0:T(128)} %param.12) | copy-start | bytes 196
  0.7 0.7 %copy-start.2 = (bf16[16,512]{1,0:T(8,128)(2,1)S(1)}, bf16[16,512]{1,0:T(8,128)(2,1)}, u32[]{:S(2)}) copy-start(bf16[16,512]{1,0:T(8,128)(2,1)} %param.9) | copy-start | bytes 49156
  0.7 0.7 %copy-start.3 = (bf16[16,512]{1,0:T(8,128)(2,1)S(1)}, bf16[16,512]{1,0:T(8,128)(2,1)}, u32[]{:S(2)}) copy-start(bf16[16,512]{1,0:T(8,128)(2,1)} %param.7) | copy-start | bytes 49156
  1.7 0.7 %copy-start = (bf16[16,512]{1,0:T(8,128)(2,1)S(1)}, bf16[16,512]{1,0:T(8,128)(2,1)}, u32[]{:S(2)}) copy-start(bf16[16,512]{1,0:T(8,128)(2,1)} %param.13) | copy-start | bytes 49156
  1.7 0.7 %copy-start.1 = (bf16[16,512]{1,0:T(8,128)(2,1)S(1)}, bf16[16,512]{1,0:T(8,128)(2,1)}, u32[]{:S(2)}) copy-start(bf16[16,512]{1,0:T(8,128)(2,1)} %param.8) | copy-start | bytes 49156
  44.7 0.7 %copy-start.5 = (f32[16]{0:T(128)S(1)}, f32[16]{0:T(128)}, u32[]{:S(2)}) copy-start(f32[16]{0:T(128)} %param.11) | copy-start | bytes 196
  48.0 0.7 %copy-start.6 = (f32[16]{0:T(128)S(1)}, f32[16]{0:T(128)}, u32[]{:S(2)}) copy-start(f32[16]{0:T(128)} %param.10) | copy-start | bytes 196

commit v5 on v4

--- a/solution.py
+++ b/solution.py
@@ -35,17 +35,16 @@
     return jnp.broadcast_to(total, value.shape)
 
 
-def fold_items(items, coef_ref, rows, modes):
+def fold_items(items, coefs, rows, modes):
+    step, step_len, lags, lags_q, inv_m, befores, afters = coefs
     acc = unpack(items[0], rows)
-    coef = coef_ref[0]
-    pre = coef[5:6] * acc["fwd"]
-    post = coef[6:7] * acc["bwd"]
+    pre = befores[0:1] * acc["fwd"]
+    post = afters[0:1] * acc["bwd"]
     for index in range(1, len(items)):
         item = unpack(items[index], rows)
-        coef = coef_ref[index]
-        step, step_len, lag, lag_q, inv_m = coef[0:1], coef[1:2], coef[2:3], coef[3:4], coef[4:5]
-        pre = pre + coef[5:6] * item["fwd"]
-        post = post + coef[6:7] * item["bwd"]
+        lag, lag_q = lags[index:index + 1], lags_q[index:index + 1]
+        pre = pre + befores[index:index + 1] * item["fwd"]
+        post = post + afters[index:index + 1] * item["bwd"]
         cross_res = chan_sum(acc["fwd"] * item["fold"], modes)
         cross_mem = chan_sum(acc["fwd"] * item["fold_v"] + acc["fwd_m"] * item["fold"] * inv_m, modes)
         acc = {
@@ -81,9 +80,21 @@
     return [buf[(slot - pos + count) % count] for slot in range(count)]
 
 
-def combine_kernel(counts, rows, modes, state_ref, coef_a, coef_b, fin_ref, out_ref,
-                   buf_a, buf_b, buf_c, send_a, recv_a, send_b, recv_b, send_c, recv_c):
+def fold_coefs(count, size, pos, inv, block_len):
+    index = lax.broadcasted_iota(jnp.int32, (count, LANES), 0)
+    span = float(size * block_len)
+    step = jnp.exp(-span * inv)
+    starts = index.astype(jnp.float32) * span
+    lag = jnp.exp(-starts * inv)
+    before = jnp.where(index < pos, jnp.exp(-((pos - 1 - index).astype(jnp.float32) * span) * inv), 0.0)
+    after = jnp.where(index > pos, jnp.exp(-((index - pos - 1).astype(jnp.float32) * span) * inv), 0.0)
+    return step, step * span, lag, lag * starts * inv, inv, before, after
+
+
+def combine_kernel(counts, rows, modes, block_len, *refs):
     count_a, count_b, count_c = counts
+    slab_refs = refs[:len(SLAB_NAMES)]
+    inv_ref, out_ref, buf_a, buf_b, buf_c, send_a, recv_a, send_b, recv_b, send_c, recv_c = refs[len(SLAB_NAMES):]
     seq_index = lax.axis_index("seq")
     ch_index = lax.axis_index("ch")
     pos_a = seq_index % count_a
@@ -103,17 +114,23 @@
         for dist in range(1, count):
             pl.semaphore_signal(barrier, inc=1, device_id=device_of((pos + dist) % count),
                                 device_id_type=pl.DeviceIdType.MESH)
+
+    for i, ref in enumerate(slab_refs):
+        buf_a[0, i * rows:(i + 1) * rows, :] = ref[...]
+    inv = inv_ref[...][0:1]
+    coefs_a = fold_coefs(count_a, 1, pos_a, inv, block_len)
+    coefs_b = fold_coefs(count_b, count_a, pos_b, inv, block_len)
+    near = jnp.exp(-(pos_a * block_len).astype(jnp.float32) * inv)
+    far = jnp.exp(-((count_a - 1 - pos_a) * block_len).astype(jnp.float32) * inv)
     pl.semaphore_wait(barrier, count_a + count_b + count_c - 3)
 
-    buf_a[0] = state_ref[...]
     items = gather_ring(buf_a, send_a, recv_a, count_a, pos_a, dev_a)
-    group, pre_a, post_a = fold_items(items, coef_a, rows, modes)
+    group, pre_a, post_a = fold_items(items, coefs_a, rows, modes)
     buf_b[0] = jnp.concatenate([group[name] for name in SLAB_NAMES], axis=0)
     items = gather_ring(buf_b, send_b, recv_b, count_b, pos_b, dev_b)
-    total, pre_b, post_b = fold_items(items, coef_b, rows, modes)
-    fin = fin_ref[...]
-    pre = fin[0:1] * pre_b + pre_a
-    post = fin[1:2] * post_b + post_a
+    total, pre_b, post_b = fold_items(items, coefs_b, rows, modes)
+    pre = near * pre_b + pre_a
+    post = far * post_b + post_a
     buf_c[0] = jnp.concatenate([total["res"], total["mem"]], axis=0)
     items = gather_ring(buf_c, send_c, recv_c, count_c, ch_index, dev_c)
     sums = items[0]
@@ -126,41 +143,20 @@
     return jnp.tile(vec, LANES // vec.shape[0])
 
 
-def fold_coefs(count, size, pos, inv_m, block_len):
-    inv = lanes_of(inv_m)[None, :]
-    index = jnp.arange(count, dtype=jnp.int32)[:, None]
-    span = float(size * block_len)
-    step = jnp.broadcast_to(jnp.exp(-span * inv), (count, LANES))
-    starts = index.astype(jnp.float32) * span
-    lag = jnp.exp(-starts * inv)
-    before = jnp.where(index < pos, jnp.exp(-((pos - 1 - index).astype(jnp.float32) * span) * inv), 0.0)
-    after = jnp.where(index > pos, jnp.exp(-((index - pos - 1).astype(jnp.float32) * span) * inv), 0.0)
-    rows = [step, step * span, lag, lag * starts * inv, jnp.broadcast_to(inv, (count, LANES)), before, after,
-            jnp.zeros((count, LANES), jnp.float32)]
-    return jnp.stack(rows, axis=1)
-
-
 def combine_states(slabs, inv_m, block_len):
     channels, modes = slabs[0].shape
     rows = channels * modes // LANES
-    seq_index = lax.axis_index("seq")
     count_a = min(GROUP, lax.axis_size("seq"))
     count_b = lax.axis_size("seq") // count_a
     count_c = lax.axis_size("ch")
-    pos_a = seq_index % count_a
-    pos_b = seq_index // count_a
-    state = jnp.concatenate([s.reshape(rows, LANES) for s in slabs], axis=0)
-    coef_a = fold_coefs(count_a, 1, pos_a, inv_m, block_len)
-    coef_b = fold_coefs(count_b, count_a, pos_b, inv_m, block_len)
-    near = jnp.exp(-(pos_a * block_len).astype(jnp.float32) * inv_m)
-    far = jnp.exp(-((count_a - 1 - pos_a) * block_len).astype(jnp.float32) * inv_m)
-    fin = jnp.stack([lanes_of(near), lanes_of(far)] + [lanes_of(jnp.zeros_like(inv_m))] * 6)
+    packed = [s.reshape(rows, LANES) for s in slabs]
+    inv = jnp.broadcast_to(lanes_of(inv_m)[None, :], (8, LANES))
     msg = (len(SLAB_NAMES) * rows, LANES)
     vmem = pl.BlockSpec(memory_space=pltpu.VMEM)
     out = pl.pallas_call(
-        functools.partial(combine_kernel, (count_a, count_b, count_c), rows, modes),
+        functools.partial(combine_kernel, (count_a, count_b, count_c), rows, modes, block_len),
         out_shape=jax.ShapeDtypeStruct((6 * rows, LANES), jnp.float32),
-        in_specs=[vmem] * 4,
+        in_specs=[vmem] * (len(SLAB_NAMES) + 1),
         out_specs=vmem,
         scratch_shapes=[
             pltpu.VMEM((count_a,) + msg, jnp.float32),
@@ -174,7 +170,7 @@
             pltpu.SemaphoreType.DMA((count_c,)),
         ],
         compiler_params=pltpu.CompilerParams(collective_id=0, has_side_effects=True),
-    )(state, coef_a, coef_b, fin)
+    )(*packed, inv)
     pieces = [out[i * rows:(i + 1) * rows].reshape(channels, modes) for i in range(5)]
     return pieces
 

time: 52.8 us -> 53.8 us (1.019)
  local copies, waits for them, and re-layouts: 8.21 us -> 9.86 us
  other arithmetic: 2.22 us -> 1.21 us
  matrix products: 8.91 us -> 9.66 us
    reshape x5, local copies, waits for them, and re-layouts: 0.51 us -> 3.4 us  [combine_states(): packed = [s.reshape(rows, LANES) for s in slabs]]
    another operation x13 -> x0, local copies, waits for them, and re-layouts: 1.8 us -> none  [the longest x6 1.4 us: fold_coefs(): return jnp.stack(rows, axis=1)]
    broadcast_in_dim x9, local copies, waits for them, and re-layouts: 0.42 us -> 2.13 us  [per_device(): jnp.broadcast_to(v, fwd.shape)]
    concatenate x1 -> x0, local copies, waits for them, and re-layouts: 1.22 us -> none  [combine_states(): state = jnp.concatenate([s.reshape(rows, LANES) for s in slabs], axis=0)]
    dot_general x13, matrix products: 8.91 us -> 9.66 us  [mm(): return jnp.einsum(pattern, left_op, right_op, precision=HIGH_PREC)]
    another operation x1 -> x0, other arithmetic: 0.68 us -> none  [combine_states(): jnp.stack([lanes_of(near), lanes_of(far)] + [lanes_of(jnp.zeros_like(inv_...]
    broadcast_in_dim x2, local copies, waits for them, and re-layouts: 0.01 us -> 0.68 us  [combine_states(): inv = jnp.broadcast_to(lanes_of(inv_m)[None, :], (8, LANES))]
where the time goes in v5:
time: 53.8 us; the launch traced here: 53.5 us
  Pallas kernels  32 us (59%)
  local copies, waits for them, and re-layouts  9.86 us (18%)
  matrix products  9.66 us (18%)
  other arithmetic  1.21 us (2%)
  between operations  0.72 us (1%)
    pallas_call x1, Pallas kernels, combine_states(): pl.pallas_call(functools.partial(combine_kernel, (count_a, count_b, count...  32 us
    dot_general x13, matrix products, mm(): return jnp.einsum(pattern, left_op, right_op, precision=HIGH_PREC)  9.66 us
    reshape x5, local copies, waits for them, and re-layouts, combine_states(): packed = [s.reshape(rows, LANES) for s in slabs]  3.4 us
    unnamed x15, local copies, waits for them, and re-layouts  2.42 us
    broadcast_in_dim x9, local copies, waits for them, and re-layouts, per_device(): jnp.broadcast_to(v, fwd.shape)  2.13 us

profile of v5, /device:TPU:1, one launch (start us, length us, event | category | flops | bytes accessed | tf_op | source)
XLA Modules:
  0.0 53.5 jit_solution(10333557113315644413)
XLA Ops:
  0.6 0.0 copy-start.4
  0.7 0.6 %copy-done.4 = f32[16]{0:T(128)S(1)} copy-done((f32[16]{0:T(128)S(1)}, f32[16]{0:T(128)}, u32[]{:S(2)}) %copy-start.4) | copy-done | bytes 88
  1.3 0.0 copy-start.2
  1.3 0.0 copy-start.3
  1.3 1.0 %fusion.20 = f32[16,16]{1,0:T(8,128)S(1)} fusion(bf16[16,512]{1,0:T(8,128)(2,1)} %param.9, bf16[16,512]{1,0:T(8,128)(2,1)} %param.7, f32[512]{0:T(512)S(1)} %get-tuple-element.22, f32[16]{0:T(128)S(1)} %broadcast_divide_fusion), kind=kOutput, calls=%fused_computation.37 | convolution fusion | flops 1605632 | bytes 35904 | tf_op jit(solution)/shard_map/cs,sn->cn/dot_general | solution.py:15
  2.3 0.7 %reshape.89.refs_0_ = f32[2,128]{1,0:T(2,128)} reshape(f32[16,16]{1,0:T(8,128)S(1)} %fusion.20) | data formatting | bytes 2048 | tf_op jit(solution)/shard_map/reshape | solution.py:152
  3.0 0.0 copy-done.2
  3.0 0.0 copy-done.3
  3.0 0.0 copy-start
  3.0 0.0 copy-start.1
  3.0 0.2 fusion.18
  3.2 0.7 %reshape.90.refs_1_ = f32[2,128]{1,0:T(2,128)} reshape(f32[16,16]{1,0:T(8,128)S(1)} %fusion.18) | data formatting | bytes 2048 | tf_op jit(solution)/shard_map/reshape | solution.py:152
  3.9 0.0 copy-done
  3.9 0.0 copy-done.1
  3.9 0.2 fusion.27
  4.1 0.7 %reshape.91.refs_2_ = f32[2,128]{1,0:T(2,128)} reshape(f32[16,16]{1,0:T(8,128)S(1)} %fusion.27) | data formatting | bytes 2048 | tf_op jit(solution)/shard_map/reshape | solution.py:152
  4.8 0.2 fusion.17
  5.0 0.7 %reshape.92.refs_3_ = f32[2,128]{1,0:T(2,128)} reshape(f32[16,16]{1,0:T(8,128)S(1)} %fusion.17) | data formatting | bytes 2048 | tf_op jit(solution)/shard_map/reshape | solution.py:152
  5.7 0.2 convolution_subtract_fusion.1
  6.0 0.7 %reshape.93.refs_4_ = f32[2,128]{1,0:T(2,128)} reshape(f32[16,16]{1,0:T(8,128)S(1)} %convolution_subtract_fusion.1) | data formatting | bytes 2048 | tf_op jit(solution)/shard_map/reshape | solution.py:152
  6.6 1.1 %convolution_select_fusion = f32[512,512]{1,0:T(8,128)S(1)} fusion(bf16[16,512]{1,0:T(8,128)(2,1)S(1)} %copy-done.2, bf16[16,512]{1,0:T(8,128)(2,1)S(1)} %copy-done.3, bf16[16,512]{1,0:T(8,128)(2,1)S(1)} %copy-done, bf16[16,512]{1,0:T(8,128)(2,1)S(1)} %copy-done.1), kind=kOutput, calls=%fused_computation | convolution fusion | flops 50905088 | bytes 1114112 | tf_op jit(solution)/shard_map/ct,cs->ts/dot_general | solution.py:15
  7.7 1.1 %multiply_reduce_fusion.1 = (f32[16]{0:T(128)S(1)}, f32[512,16]{0,1:T(8,128)S(1)}) fusion(f32[16]{0:T(128)S(1)} %broadcast_divide_fusion, f32[512]{0:T(512)S(1)} %iota_negate_fusion, f32[512,512]{1,0:T(8,128)S(1)} %convolution_select_fusion), kind=kOutput, calls=%fused_computation.29 | convolution fusion | flops 50364400 | bytes 1083520 | tf_op jit(solution)/shard_map/ts,sn->tn/dot_general | solution.py:15
  8.9 0.1 broadcast_in_dim.29
  8.9 0.6 %broadcast_in_dim.30.refs_5_ = f32[2,128]{1,0:T(2,128)} broadcast(f32[128]{0:T(128)S(1)} %broadcast_in_dim.29), dimensions={1} | broadcast | bytes 1536 | tf_op jit(solution)/shard_map/broadcast_in_dim | solution.py:216
  9.5 1.1 %fusion.3 = f32[16]{0:T(128)S(1)} fusion(f32[512,512]{1,0:T(8,128)S(1)} %convolution_select_fusion, f32[512,16]{0,1:T(8,128)S(1)} %get-tuple-element.20, f32[16]{0:T(128)S(1)} %broadcast_divide_fusion, f32[512]{0:T(512)S(1)} %iota_negate_fusion), kind=kOutput, calls=%fused_computation.8 | convolution fusion | flops 50413552 | bytes 1083520 | tf_op jit(solution)/shard_map/ts,sn->tn/dot_general | solution.py:15
  10.7 0.1 broadcast_in_dim.61
  10.8 0.6 %broadcast_in_dim.62.refs_6_ = f32[2,128]{1,0:T(2,128)} broadcast(f32[128]{0:T(128)S(1)} %broadcast_in_dim.61), dimensions={1} | broadcast | bytes 1536 | tf_op jit(solution)/shard_map/broadcast_in_dim | solution.py:216
  11.3 0.1 multiply_reduce_fusion
  11.4 0.1 broadcast_in_dim.63
  11.5 0.1 broadcast_in_dim.64
  11.6 0.6 %broadcast_in_dim.65.refs_7_ = f32[2,128]{1,0:T(2,128)} reshape(f32[2,8,16]{2,1,0:T(8,128)S(1)} %broadcast_in_dim.64) | data formatting | bytes 2048 | tf_op jit(solution)/shard_map/broadcast_in_dim | solution.py:216
  12.2 0.1 broadcast_in_dim.66
  12.3 0.6 %broadcast_in_dim.67.refs_8_ = f32[8,128]{1,0:T(8,128)} broadcast(f32[128]{0:T(128)S(1)} %broadcast_in_dim.66), dimensions={1} | broadcast | bytes 4608 | tf_op jit(solution)/shard_map/broadcast_in_dim | solution.py:153
  12.9 32.0 %shard_map.126 = f32[12,128]{1,0:T(8,128)} custom-call(f32[2,128]{1,0:T(2,128)} %reshape.89.refs_0_, f32[2,128]{1,0:T(2,128)} %reshape.90.refs_1_, f32[2,128]{1,0:T(2,128)} %reshape.91.refs_2_, f32[2,128]{1,0:T(2,128)} %reshape.92.refs_3_, f32[2,128]{1,0:T(2,128)} %reshape.93.refs_4_, f32[2,128]{1,0:T(2,128)} %broadcast_in_dim.30.refs_5_, ...), custom_call_target="tpu_custom_call" | custom-call | tf_op jit(solution)/shard_map/pallas_call | solution.py:156
  45.0 0.8 %fusion.59 = (f32[2,128]{1,0:T(2,128)S(1)}, f32[2,128]{1,0:T(2,128)S(1)}, f32[2,128]{1,0:T(2,128)S(1)}, f32[2,128]{1,0:T(2,128)S(1)}, f32[2,128]{1,0:T(2,128)S(1)}) fusion(f32[12,128]{1,0:T(8,128)} %shard_map.126), kind=kLoop, calls=%fused_computation.84 | loop fusion | bytes 10240 | tf_op jit(solution)/shard_map/slice | solution.py:174
  45.8 0.0 copy-start.5
  45.8 0.1 reshape.98
  45.9 0.6 %copy-done.5 = f32[16]{0:T(128)S(1)} copy-done((f32[16]{0:T(128)S(1)}, f32[16]{0:T(128)}, u32[]{:S(2)}) %copy-start.5) | copy-done | bytes 88
  46.5 0.5 fusion.56
  47.0 1.2 %convolution_select_fusion.1 = f32[512,512]{1,0:T(8,128)S(1)} fusion(f32[16]{0:T(128)S(1)} %get-tuple-element.8, f32[16]{0:T(128)S(1)} %broadcast_divide_fusion, f32[512]{0:T(512)S(1)} %iota_negate_fusion), kind=kOutput, calls=%fused_computation.1 | convolution fusion | flops 50880512 | bytes 1050752 | tf_op jit(solution)/shard_map/tn,sn->ts/dot_general | solution.py:15
  48.2 1.0 %fusion.28 = f32[16,512]{1,0:T(8,128)S(1)} fusion(f32[512,512]{1,0:T(8,128)S(1)} %convolution_select_fusion.1, bf16[16,512]{1,0:T(8,128)(2,1)S(1)} %copy-done.2, bf16[16,512]{1,0:T(8,128)(2,1)S(1)} %copy-done.3), kind=kOutput, calls=%fused_computation.44 | convolution fusion | flops 50356224 | bytes 1114112 | tf_op jit(solution)/shard_map/cs,ts->ct/dot_general | solution.py:15
  49.1 0.0 copy-start.6
  49.1 0.1 reshape.94
  49.2 0.6 %copy-done.6 = f32[16]{0:T(128)S(1)} copy-done((f32[16]{0:T(128)S(1)}, f32[16]{0:T(128)}, u32[]{:S(2)}) %copy-start.6) | copy-done | bytes 88
  49.8 0.9 %fusion.7 = (bf16[16,512]{1,0:T(8,128)(2,1)}, bf16[16,512]{1,0:T(8,128)(2,1)}) fusion(bf16[16,512]{1,0:T(8,128)(2,1)S(1)} %copy-done, bf16[16,512]{1,0:T(8,128)(2,1)S(1)} %copy-done.1, bf16[16,512]{1,0:T(8,128)(2,1)S(1)} %copy-done.2, bf16[16,512]{1,0:T(8,128)(2,1)S(1)} %copy-done.3, f32[16]{0:T(128)S(1)} %copy-done.6, f32[16,512]{1,0:T(8,128)S(1)} %fusion.28, ...), kind=kOutput, calls=%fused_computation.20 | convolution fusion | flops 1687552 | bytes 134336 | tf_op jit(solution)/shard_map/cn,tn->ct/dot_general | solution.py:15
  50.7 0.6 %fusion.29 = f32[16,512]{1,0:T(8,128)S(1)} fusion(f32[512,512]{1,0:T(8,128)S(1)} %convolution_select_fusion.1, bf16[16,512]{1,0:T(8,128)(2,1)S(1)} %copy-done, bf16[16,512]{1,0:T(8,128)(2,1)S(1)} %copy-done.1), kind=kOutput, calls=%fused_computation.45 | convolution fusion | flops 50356224 | bytes 1114112 | tf_op jit(solution)/shard_map/ct,ts->cs/dot_general | solution.py:15
  51.3 0.1 reshape.95
  51.4 0.9 %fusion.5 = (bf16[16,512]{1,0:T(8,128)(2,1)}, bf16[16,512]{1,0:T(8,128)(2,1)}) fusion(bf16[16,512]{1,0:T(8,128)(2,1)S(1)} %copy-done.3, bf16[16,512]{1,0:T(8,128)(2,1)S(1)} %copy-done.2, f32[16,512]{1,0:T(8,128)S(1)} %fusion.29, f32[16,16]{1,0:T(8,128)S(1)} %reshape.95, f32[512]{0:T(512)S(1)} %subtract_negate_fusion, f32[16]{0:T(128)S(1)} %get-tuple-element.8, ...), kind=kOutput, calls=%fused_computation.18 | convolution fusion | flops 1687552 | bytes 134336 | tf_op jit(solution)/shard_map/cn,sn->cs/dot_general | solution.py:15
  52.2 0.1 reshape.96
  52.3 0.6 %copy.16 = f32[16,1]{0,1:T(1,128)} copy(f32[16,1]{1,0:T(8,128)S(1)} %slice_multiply_fusion) | data formatting | bytes 128
  52.9 0.1 reshape.97
  53.0 0.5 fusion.58
  (9 shorter events, 0.1 us)
Async XLA Ops:
  0.6 0.7 %copy-start.4 = (f32[16]{0:T(128)S(1)}, f32[16]{0:T(128)}, u32[]{:S(2)}) copy-start(f32[16]{0:T(128)} %param.12) | copy-start | bytes 196
  1.3 1.7 %copy-start.2 = (bf16[16,512]{1,0:T(8,128)(2,1)S(1)}, bf16[16,512]{1,0:T(8,128)(2,1)}, u32[]{:S(2)}) copy-start(bf16[16,512]{1,0:T(8,128)(2,1)} %param.9) | copy-start | bytes 49156
  1.3 1.7 %copy-start.3 = (bf16[16,512]{1,0:T(8,128)(2,1)S(1)}, bf16[16,512]{1,0:T(8,128)(2,1)}, u32[]{:S(2)}) copy-start(bf16[16,512]{1,0:T(8,128)(2,1)} %param.7) | copy-start | bytes 49156
  3.0 0.9 %copy-start = (bf16[16,512]{1,0:T(8,128)(2,1)S(1)}, bf16[16,512]{1,0:T(8,128)(2,1)}, u32[]{:S(2)}) copy-start(bf16[16,512]{1,0:T(8,128)(2,1)} %param.13) | copy-start | bytes 49156
  3.0 0.9 %copy-start.1 = (bf16[16,512]{1,0:T(8,128)(2,1)S(1)}, bf16[16,512]{1,0:T(8,128)(2,1)}, u32[]{:S(2)}) copy-start(bf16[16,512]{1,0:T(8,128)(2,1)} %param.8) | copy-start | bytes 49156
  45.8 0.7 %copy-start.5 = (f32[16]{0:T(128)S(1)}, f32[16]{0:T(128)}, u32[]{:S(2)}) copy-start(f32[16]{0:T(128)} %param.11) | copy-start | bytes 196
  49.1 0.7 %copy-start.6 = (f32[16]{0:T(128)S(1)}, f32[16]{0:T(128)}, u32[]{:S(2)}) copy-start(f32[16]{0:T(128)} %param.10) | copy-start | bytes 196

commit v6 on v5

v6 whole, which is shorter than its diff:
```python
import functools
import math

import jax
import jax.numpy as jnp
from jax import lax
from jax.experimental import pallas as pl
from jax.experimental.pallas import tpu as pltpu
from jax.sharding import PartitionSpec as P

HIGH_PREC = lax.Precision.HIGHEST


def mm(pattern, left_op, right_op):
    return jnp.einsum(pattern, left_op, right_op, precision=HIGH_PREC)


GROUP = 8
LANES = 128
SLABS = 8


def row_sum(value):
    return jnp.sum(value, axis=0, keepdims=True)


def slab_coefs(count, size, pos, inv, block_len, modes):
    lane = lax.broadcasted_iota(jnp.int32, (count, LANES), 1) // modes
    index = lax.broadcasted_iota(jnp.int32, (count, LANES), 0)
    span = float(size * block_len)
    step = jnp.exp(-span * inv)
    starts = index.astype(jnp.float32) * span
    lag = jnp.exp(-starts * inv)
    before = jnp.where(index < pos, jnp.exp(-((pos - 1 - index).astype(jnp.float32) * span) * inv), 0.0)
    after = jnp.where(index > pos, jnp.exp(-((index - pos - 1).astype(jnp.float32) * span) * inv), 0.0)
    keep = jnp.where(lane <= 1, step, 1.0)[0:1]
    carry = jnp.where(lane == 1, step * span, 0.0)[0:1]
    take = jnp.where((lane >= 2) & (lane <= 4), lag, 1.0)
    shift = jnp.where(lane == 4, lag * starts * inv, 0.0)
    edge = jnp.where(lane == 0, before, jnp.where(lane == 2, after, 0.0))
    return keep, carry, take, shift, edge


def fold_items(items, coefs, inv, modes):
    keep, carry, take, shift, edge_c = coefs
    lane = lax.broadcasted_iota(jnp.int32, (1, LANES), 1) // modes
    acc = items[0]
    edge = edge_c[0:1] * acc
    for index in range(1, len(items)):
        item = items[index]
        s1 = row_sum(pltpu.roll(acc, 3 * modes, 1) * item)
        s2 = row_sum(pltpu.roll(acc, 4 * modes, 1) * item)
        s3 = row_sum(pltpu.roll(acc, 2 * modes, 1) * item)
        cross = jnp.where(lane == 5, pltpu.roll(s1, 2 * modes, 1), 0.0) + jnp.where(
            lane == 6, pltpu.roll(s2, 2 * modes, 1) + pltpu.roll(s3 * inv, 3 * modes, 1), 0.0)
        acc = (keep * acc + take[index:index + 1] * item + carry * pltpu.roll(acc, modes, 1)
               + shift[index:index + 1] * pltpu.roll(item, modes, 1) + cross)
        edge = edge + edge_c[index:index + 1] * item
    return acc, edge


def gather_ring(buf, send_sems, recv_sems, count, pos, device_of):
    descs = []
    for dist in range(1, count):
        desc = pltpu.make_async_remote_copy(
            src_ref=buf.at[0],
            dst_ref=buf.at[count - dist],
            send_sem=send_sems.at[dist],
            recv_sem=recv_sems.at[count - dist],
            device_id=device_of((pos + dist) % count),
            device_id_type=pl.DeviceIdType.MESH,
        )
        desc.start()
        descs.append(desc)
    for desc in descs:
        desc.wait_recv()
    for desc in descs:
        desc.wait_send()
    return [buf[(slot - pos + count) % count] for slot in range(count)]


def combine_kernel(counts, modes, block_len, state_ref, inv_ref, out_ref,
                   buf_a, buf_b, buf_c, send_a, recv_a, send_b, recv_b, send_c, recv_c):
    count_a, count_b, count_c = counts
    seq_index = lax.axis_index("seq")
    ch_index = lax.axis_index("ch")
    pos_a = seq_index % count_a
    pos_b = seq_index // count_a

    def dev_a(other):
        return (pos_b * count_a + other, ch_index)

    def dev_b(other):
        return (other * count_a + pos_a, ch_index)

    def dev_c(other):
        return (seq_index, other)

    barrier = pltpu.get_barrier_semaphore()
    for count, pos, device_of in ((count_a, pos_a, dev_a), (count_b, pos_b, dev_b), (count_c, ch_index, dev_c)):
        for dist in range(1, count):
            pl.semaphore_signal(barrier, inc=1, device_id=device_of((pos + dist) % count),
                                device_id_type=pl.DeviceIdType.MESH)

    buf_a[0] = state_ref[...]
    inv = inv_ref[...][0:1]
    coefs_a = slab_coefs(count_a, 1, pos_a, inv, block_len, modes)
    coefs_b = slab_coefs(count_b, count_a, pos_b, inv, block_len, modes)
    lane = lax.broadcasted_iota(jnp.int32, (1, LANES), 1) // modes
    near = jnp.exp(-(pos_a * block_len).astype(jnp.float32) * inv)
    far = jnp.exp(-((count_a - 1 - pos_a) * block_len).astype(jnp.float32) * inv)
    join = jnp.where(lane == 0, near, jnp.where(lane == 2, far, 0.0))
    pl.semaphore_wait(barrier, count_a + count_b + count_c - 3)

    items = gather_ring(buf_a, send_a, recv_a, count_a, pos_a, dev_a)
    group, edge_a = fold_items(items, coefs_a, inv, modes)
    buf_b[0] = group
    items = gather_ring(buf_b, send_b, recv_b, count_b, pos_b, dev_b)
    total, edge_b = fold_items(items, coefs_b, inv, modes)
    buf_c[0] = total
    items = gather_ring(buf_c, send_c, recv_c, count_c, ch_index, dev_c)
    sums = items[0]
    for item in items[1:]:
        sums = sums + item
    out_ref[0] = join * edge_b + edge_a
    out_ref[1] = total
    out_ref[2] = sums


def combine_states(state, inv_m, block_len):
    channels = state.shape[0]
    modes = inv_m.shape[0]
    count_a = min(GROUP, lax.axis_size("seq"))
    count_b = lax.axis_size("seq") // count_a
    count_c = lax.axis_size("ch")
    inv = jnp.broadcast_to(jnp.tile(inv_m, LANES // modes)[None, :], (8, LANES))
    msg = (channels, LANES)
    vmem = pl.BlockSpec(memory_space=pltpu.VMEM)
    return pl.pallas_call(
        functools.partial(combine_kernel, (count_a, count_b, count_c), modes, block_len),
        out_shape=jax.ShapeDtypeStruct((3,) + msg, jnp.float32),
        in_specs=[vmem, vmem],
        out_specs=vmem,
        scratch_shapes=[
            pltpu.VMEM((count_a,) + msg, jnp.float32),
            pltpu.VMEM((count_b,) + msg, jnp.float32),
            pltpu.VMEM((count_c,) + msg, jnp.float32),
            pltpu.SemaphoreType.DMA((count_a,)),
            pltpu.SemaphoreType.DMA((count_a,)),
            pltpu.SemaphoreType.DMA((count_b,)),
            pltpu.SemaphoreType.DMA((count_b,)),
            pltpu.SemaphoreType.DMA((count_c,)),
            pltpu.SemaphoreType.DMA((count_c,)),
        ],
        compiler_params=pltpu.CompilerParams(collective_id=0, has_side_effects=True),
    )(state, inv)


def finish_kernel(x_ref, q_ref, k_ref, d_ref, gain_ref, toep_ref, into_ref, edge_ref,
                  out_ref, gx_ref, gq_ref, gk_ref):
    x_float = x_ref[...].astype(jnp.float32)
    q_float = q_ref[...].astype(jnp.float32)
    k_float = k_ref[...].astype(jnp.float32)
    d_float = d_ref[...].astype(jnp.float32)
    values = x_float * k_float
    grad_mixed = d_float * q_float
    toep = toep_ref[...]
    edge = edge_ref[...]
    conv = lax.dot_general(values, toep, (((1,), (1,)), ((), ())), precision=HIGH_PREC,
                           preferred_element_type=jnp.float32)
    conv = conv + jnp.dot(edge, into_ref[0], precision=HIGH_PREC, preferred_element_type=jnp.float32)
    corr = jnp.dot(grad_mixed, toep, precision=HIGH_PREC, preferred_element_type=jnp.float32)
    corr = corr + jnp.dot(edge, into_ref[1], precision=HIGH_PREC, preferred_element_type=jnp.float32)
    gain = gain_ref[...]
    mixed_out = conv + gain * values
    grad_values = gain * grad_mixed + corr
    out_ref[...] = (q_float * mixed_out).astype(jnp.bfloat16)
    gx_ref[...] = (grad_values * k_float).astype(jnp.bfloat16)
    gq_ref[...] = (d_float * mixed_out).astype(jnp.bfloat16)
    gk_ref[...] = (grad_values * x_float).astype(jnp.bfloat16)


def finish(signal_x, gate_q, gate_k, cotangent, skip_gain, toeplitz, into, edge):
    vmem = pl.BlockSpec(memory_space=pltpu.VMEM)
    half = jax.ShapeDtypeStruct(signal_x.shape, jnp.bfloat16)
    return pl.pallas_call(
        finish_kernel,
        out_shape=(half, half, half, half),
        in_specs=[vmem] * 8,
        out_specs=(vmem, vmem, vmem, vmem),
    )(signal_x, gate_q, gate_k, cotangent, skip_gain[:, None], toeplitz, into, edge)


def per_device(signal_x, gate_q, gate_k, skip_gain, residue, memory, cotangent):
    channels, block_len = signal_x.shape
    modes = memory.shape[0]
    seq_total = lax.axis_size("seq") * block_len
    all_channels = channels * lax.axis_size("ch")
    inv_m = 1.0 / memory
    gain = jnp.sqrt(2.0 / memory)
    amp = residue * gain
    offs = jnp.arange(block_len, dtype=jnp.float32)[:, None]
    e_down = jnp.exp(-offs * inv_m)
    e_up = jnp.exp(offs * inv_m)
    e_tail = jnp.exp(-(block_len - 1 - offs) * inv_m)
    e_next = jnp.exp(-(offs + 1) * inv_m)
    e_in = jnp.exp(-(block_len - offs) * inv_m)
    lower = offs >= offs.T
    toeplitz = jnp.where(lower, mm("tn,sn->ts", e_down * amp, e_up), 0.0)
    pad = jnp.zeros((block_len, LANES - 5 * modes), jnp.float32)
    right_v = jnp.concatenate([e_tail, e_tail * (block_len - 1 - offs), jnp.zeros((block_len, 3 * modes)), pad], axis=1)
    right_g = jnp.concatenate([jnp.zeros((block_len, 2 * modes)), e_down, e_next,
                               e_next * ((offs + 1) * inv_m - 0.5), pad], axis=1)
    zero_rows = jnp.zeros((2 * modes, block_len), jnp.float32)
    fill = jnp.zeros((LANES - 3 * modes, block_len), jnp.float32)
    into = jnp.stack([
        jnp.concatenate([(e_next * amp).T, zero_rows, fill], axis=0),
        jnp.concatenate([zero_rows, (e_in * amp).T, fill], axis=0),
    ])

    values = signal_x.astype(jnp.float32) * gate_k.astype(jnp.float32)
    grad_mixed = cotangent.astype(jnp.float32) * gate_q.astype(jnp.float32)
    pair = jnp.where(lower, mm("ct,cs->ts", grad_mixed, values), 0.0)
    near = mm("ts,sn->tn", pair, e_up)
    near_m = mm("ts,sn->tn", pair, e_up * offs * inv_m)
    local_res = jnp.sum(e_down * near, axis=0)
    local_mem = jnp.sum(e_down * ((offs * inv_m - 0.5) * near - near_m), axis=0)
    part_skip = jnp.sum(grad_mixed * values, axis=1)
    lane = jnp.arange(LANES, dtype=jnp.int32)[None, :]
    extra = jnp.concatenate([jnp.zeros((5 * modes,)), local_res, local_mem, jnp.zeros((LANES - 7 * modes,))])
    state = mm("cs,sl->cl", values, right_v) + mm("ct,tl->cl", grad_mixed, right_g)
    state = state + jnp.where(lane >= 7 * modes, part_skip[:, None], extra[None, :])
    out = combine_states(state, inv_m, block_len)
    edge, total, sums = out[0], out[1], out[2]

    output, grad_x, grad_q, grad_k = finish(signal_x, gate_q, gate_k, cotangent, skip_gain, toeplitz, into, edge)

    norm_scale = 1.0 / math.sqrt(all_channels * seq_total)
    grad_skip = total[:, 7 * modes] / math.sqrt(seq_total)
    grad_residue = gain * sums[0, 5 * modes:6 * modes] * norm_scale
    grad_memory = residue * gain * sums[0, 6 * modes:7 * modes] * norm_scale
    return (output, grad_x, grad_q, grad_k, grad_skip, grad_residue, grad_memory)


def solution(mesh):
    return jax.shard_map(
        per_device,
        mesh=mesh,
        in_specs=(
            P("ch", "seq"),
            P("ch", "seq"),
            P("ch", "seq"),
            P("ch"),
            P(),
            P(),
            P("ch", "seq"),
        ),
        out_specs=(
            P("ch", "seq"),
            P("ch", "seq"),
            P("ch", "seq"),
            P("ch", "seq"),
            P("ch"),
            P(),
            P(),
        ),
        check_vma=False,
    )
```

time: 53.8 us -> 54.9 us (1.020)
  Pallas kernels: 32 us -> 38.6 us
  local copies, waits for them, and re-layouts: 9.86 us -> 4.49 us
  matrix products: 9.66 us -> 6.66 us
  other arithmetic: 1.21 us -> 3.93 us
    reshape x10 -> x0, local copies, waits for them, and re-layouts: 3.8 us -> none  [the longest x5 3.4 us: combine_states(): packed = [s.reshape(rows, LANES) for s in slabs]]
    pallas_call x0 -> x1, Pallas kernels: none -> 3.66 us  [finish(): pl.pallas_call(finish_kernel, out_shape=(half, half, half, half), in_spec...]
    dot_general x13 -> x6, matrix products: 9.66 us -> 6.66 us  [mm(): return jnp.einsum(pattern, left_op, right_op, precision=HIGH_PREC)]
    pallas_call x1, Pallas kernels: 32 us -> 34.9 us  [combine_states(): pl.pallas_call(functools.partial(combine_kernel, (count_a, count_b, count...]
    unnamed x15 -> x14, local copies, waits for them, and re-layouts: 2.42 us -> 0.68 us
    broadcast_in_dim x11 -> x7, local copies, waits for them, and re-layouts: 2.81 us -> 1.4 us  [the longest x2 0.68 us: combine_states(): inv = jnp.broadcast_to(jnp.tile(inv_m, LANES // modes)[None, :], (8, LANES))]
    squeeze x0 -> x1, local copies, waits for them, and re-layouts: none -> 1.34 us  [per_device(): edge, total, sums = (out[0], out[1], out[2])]
    another operation x0 -> x2, other arithmetic: none -> 0.95 us  [per_device(): jnp.stack([jnp.concatenate([(e_next * amp).T, zero_rows, fill], axis=0),...]
where the time goes in v6:
time: 54.9 us; the launch traced here: 54.5 us
  Pallas kernels  38.6 us (70%)
  matrix products  6.66 us (12%)
  local copies, waits for them, and re-layouts  4.49 us (8%)
  other arithmetic  3.93 us (7%)
  between operations  0.82 us (1%)
    pallas_call x1, Pallas kernels, combine_states(): pl.pallas_call(functools.partial(combine_kernel, (count_a, count_b, count...  34.9 us
    dot_general x6, matrix products, mm(): return jnp.einsum(pattern, left_op, right_op, precision=HIGH_PREC)  6.66 us
    pallas_call x1, Pallas kernels, finish(): pl.pallas_call(finish_kernel, out_shape=(half, half, half, half), in_spec...  3.66 us
    squeeze x1, local copies, waits for them, and re-layouts, per_device(): edge, total, sums = (out[0], out[1], out[2])  1.34 us

profile of v6, /device:TPU:1, one launch (start us, length us, event | category | flops | bytes accessed | tf_op | source)
XLA Modules:
  0.0 54.5 jit_solution(17621389430590287575)
XLA Ops:
  0.6 0.0 copy-start.5
  0.6 0.6 %copy-done.5 = f32[16]{0:T(128)S(1)} copy-done((f32[16]{0:T(128)S(1)}, f32[16]{0:T(128)}, u32[]{:S(2)}) %copy-start.5) | copy-done | bytes 88
  1.3 0.0 copy-start.2
  1.3 0.0 copy-start.3
  1.3 0.9 %multiply_reduce_fusion.1 = f32[16]{0:T(128)S(1)} fusion(bf16[16,512]{1,0:T(8,128)(2,1)} %k_ref.1, bf16[16,512]{1,0:T(8,128)(2,1)} %x_ref.1, bf16[16,512]{1,0:T(8,128)(2,1)} %q_ref.1, bf16[16,512]{1,0:T(8,128)(2,1)} %d_ref.1), kind=kLoop, calls=%fused_computation.21 | loop fusion | flops 65520 | bytes 65600 | tf_op jit(solution)/shard_map/reduce_sum | solution.py:228
  2.2 0.1 pad.6.clone
  2.3 0.0 copy-start.4
  2.3 0.0 copy-start
  2.4 0.0 copy-start.1
  2.4 0.1 broadcast_in_dim.79
  2.4 0.6 %broadcast_in_dim.80.inv_ref = f32[8,128]{1,0:T(8,128)} broadcast(f32[128]{0:T(128)S(1)} %broadcast_in_dim.79), dimensions={1} | broadcast | bytes 4608 | tf_op jit(solution)/shard_map/broadcast_in_dim | solution.py:136
  3.1 0.0 copy-done.4
  3.1 0.7 %copy.25.gain_ref = f32[16,1]{1,0:T(8,128)} copy(f32[16,1]{0,1:T(1,128)S(1)} %bitcast.26) | data formatting | bytes 128 | tf_op jit(solution)/shard_map/broadcast_in_dim | solution.py:191
  3.7 0.0 copy-done.2
  3.8 0.0 copy-done.3
  3.8 0.0 copy-done
  3.8 0.0 copy-done.1
  3.8 1.1 %convolution_select_fusion = f32[512,512]{1,0:T(8,128)S(1)} fusion(bf16[16,512]{1,0:T(8,128)(2,1)S(1)} %copy-done.2, bf16[16,512]{1,0:T(8,128)(2,1)S(1)} %copy-done, bf16[16,512]{1,0:T(8,128)(2,1)S(1)} %copy-done.1, bf16[16,512]{1,0:T(8,128)(2,1)S(1)} %copy-done.3), kind=kOutput, calls=%fused_computation | convolution fusion | flops 50905088 | bytes 1114112 | tf_op jit(solution)/shard_map/ct,cs->ts/dot_general | solution.py:15
  4.8 1.1 %multiply_reduce_fusion = (f32[16]{0:T(128)S(1)}, f32[512,16]{0,1:T(8,128)S(1)}, f32[512,16]{0,1:T(8,128)S(1)}, f32[512,16]{0,1:T(8,128)S(1)}, f32[512,16]{0,1:T...) fusion(f32[16]{0:T(128)S(1)} %broadcast_divide_fusion, f32[512]{0:T(512)S(1)} %get-tuple-element.40, ...), kind=kOutput, calls=%fused_computation.20 | convolution fusion | flops 50413552 | bytes 1255552 | tf_op jit(solution)/shard_map/ts,sn->tn/dot_general | solution.py:15
  6.0 1.1 %fusion.1 = f32[16]{0:T(128)S(1)} fusion(f32[512,512]{1,0:T(8,128)S(1)} %convolution_select_fusion, f32[512,16]{0,1:T(8,128)S(1)} %get-tuple-element.37, f32[16]{0:T(128)S(1)} %broadcast_divide_fusion, f32[512]{0:T(512)S(1)} %get-tuple-element.40), kind=kOutput, calls=%fused_computation.4 | convolution fusion | flops 50413552 | bytes 1083520 | tf_op jit(solution)/shard_map/ts,sn->tn/dot_general | solution.py:15
  7.1 0.1 fusion.31
  7.2 0.1 copy.22
  7.3 0.1 copy.21
  7.5 0.1 copy.20
  7.6 0.3 fusion.3
  8.0 0.1 copy.23
  8.1 0.1 copy.24
  8.3 0.4 concatenate.22
  8.7 0.9 %fusion.2.state_ref = f32[16,128]{1,0:T(8,128)} fusion(f32[16,128]{1,0:T(8,128)S(1)} %fusion.3, f32[512,128]{1,0:T(8,128)S(1)} %concatenate.22, bf16[16,512]{1,0:T(8,128)(2,1)S(1)} %copy-done.1, bf16[16,512]{1,0:T(8,128)(2,1)S(1)} %copy-done.3, f32[128]{0:T(128)S(1)} %get-tuple-element.32, f32[16]{0:T(128)S(1)} %multiply_reduce_fusion.1, ...), kind=kOutput, calls=%fused_computation.6 | convolution fusion | flops 12613632 | bytes 312000 | tf_op jit(solution)/shard_map/ct,tl->cl/dot_general | solution.py:15
  9.5 34.9 %shard_map.126 = f32[3,16,128]{2,1,0:T(8,128)} custom-call(f32[16,128]{1,0:T(8,128)} %fusion.2.state_ref, f32[8,128]{1,0:T(8,128)} %broadcast_in_dim.80.inv_ref), custom_call_target="tpu_custom_call" | custom-call | tf_op jit(solution)/shard_map/pallas_call | solution.py:139
  44.4 1.3 %slice_bitcast_fusion.1 = (f32[16,128]{1,0:T(8,128)S(1)}, f32[16,128]{1,0:T(8,128)S(1)}, f32[16,128]{1,0:T(8,128)}) fusion(f32[3,16,128]{2,1,0:T(8,128)} %shard_map.126), kind=kLoop, calls=%fused_computation.43 | loop fusion | bytes 49152 | tf_op jit(solution)/shard_map/squeeze | solution.py:234
  45.8 0.0 copy-start.6
  45.8 0.7 %fusion.23 = f32[16]{0:T(128)} fusion(f32[16,128]{1,0:T(8,128)S(1)} %get-tuple-element.20), kind=kLoop, calls=%fused_computation.41 | loop fusion | flops 16 | bytes 128 | tf_op jit(solution)/shard_map/div | solution.py:239
  46.5 0.0 copy-done.6
  46.5 0.6 %fusion.27 = (f32[16]{0:T(128)}, f32[16]{0:T(128)S(1)}, f32[16]{0:T(128)S(1)}) fusion(f32[16,128]{1,0:T(8,128)S(1)} %get-tuple-element.21, f32[16]{0:T(128)S(1)} %copy-done.6, f32[16]{0:T(128)S(1)} %copy-done.5), kind=kLoop, calls=%fused_computation.53 | loop fusion | flops 64 | bytes 384 | tf_op jit(solution)/shard_map/mul | solution.py:241
  47.1 0.6 %fusion.29 = f32[16]{0:T(128)} fusion(f32[16]{0:T(128)S(1)} %get-tuple-element.17, f32[16,128]{1,0:T(8,128)S(1)} %get-tuple-element.21), kind=kLoop, calls=%fused_computation.56 | loop fusion | flops 32 | bytes 192 | tf_op jit(solution)/shard_map/mul | solution.py:240
  47.6 0.1 exponential_multiply_fusion.1
  47.7 0.1 maximum_bitcast_fusion
  47.9 0.8 %pad_maximum_fusion.into_ref = f32[2,128,512]{2,1,0:T(8,128)} fusion(f32[1,128,512]{2,1,0:T(8,128)S(1)} %get-tuple-element.19, f32[1,128,512]{2,1,0:T(8,128)S(1)} %get-tuple-element.18), kind=kLoop, calls=%fused_computation.8 | loop fusion | flops 131072 | bytes 1048576 | tf_op jit(solution)/shard_map/stack | solution.py:216
  48.7 2.1 %convolution_select_fusion.1.toep_ref = f32[512,512]{1,0:T(8,128)} fusion(f32[16]{0:T(128)S(1)} %get-tuple-element.16, f32[16]{0:T(128)S(1)} %broadcast_divide_fusion, f32[512]{0:T(512)S(1)} %get-tuple-element.40), kind=kOutput, calls=%fused_computation.1 | convolution fusion | flops 50880512 | bytes 1050752 | tf_op jit(solution)/shard_map/tn,sn->ts/dot_general | solution.py:15
  50.8 3.7 %shard_map.127 = (bf16[16,512]{1,0:T(8,128)(2,1)}, bf16[16,512]{1,0:T(8,128)(2,1)}, bf16[16,512]{1,0:T(8,128)(2,1)}, bf16[16,512]{1,0:T(8,128)(2,1)}) custom-call(bf16[16,512]{1,0:T(8,128)(2,1)} %x_ref.1, bf16[16,512]{1,0:T(8,128)(2,1)} %q_ref.1, bf16[16,512]{1,0:T(8,128)(2,1)} %k_ref.1, bf16[16,512]{1,0:T(8,128)(2,1)} %d_ref.1, f32[16,1]{1,0:T(8,128)} %copy.25.gain_ref, ...), custom_call_target="tpu_custom_call" | custom-call | tf_op jit(solution)/shard_map/pallas_call | solution.py:186
  (13 shorter events, 0.1 us)
Async XLA Ops:
  0.6 0.7 %copy-start.5 = (f32[16]{0:T(128)S(1)}, f32[16]{0:T(128)}, u32[]{:S(2)}) copy-start(f32[16]{0:T(128)} %param.12) | copy-start | bytes 196
  1.3 2.5 %copy-start.2 = (bf16[16,512]{1,0:T(8,128)(2,1)S(1)}, bf16[16,512]{1,0:T(8,128)(2,1)}, u32[]{:S(2)}) copy-start(bf16[16,512]{1,0:T(8,128)(2,1)} %k_ref.1) | copy-start | bytes 49156
  1.3 2.5 %copy-start.3 = (bf16[16,512]{1,0:T(8,128)(2,1)S(1)}, bf16[16,512]{1,0:T(8,128)(2,1)}, u32[]{:S(2)}) copy-start(bf16[16,512]{1,0:T(8,128)(2,1)} %d_ref.1) | copy-start | bytes 49156
  2.3 0.7 %copy-start.4 = (f32[16]{0:T(128)S(1)}, f32[16]{0:T(128)}, u32[]{:S(2)}) copy-start(f32[16]{0:T(128)} %param.10) | copy-start | bytes 196
  2.3 1.4 %copy-start = (bf16[16,512]{1,0:T(8,128)(2,1)S(1)}, bf16[16,512]{1,0:T(8,128)(2,1)}, u32[]{:S(2)}) copy-start(bf16[16,512]{1,0:T(8,128)(2,1)} %x_ref.1) | copy-start | bytes 49156
  2.4 1.4 %copy-start.1 = (bf16[16,512]{1,0:T(8,128)(2,1)S(1)}, bf16[16,512]{1,0:T(8,128)(2,1)}, u32[]{:S(2)}) copy-start(bf16[16,512]{1,0:T(8,128)(2,1)} %q_ref.1) | copy-start | bytes 49156
  45.8 0.7 %copy-start.6 = (f32[16]{0:T(128)S(1)}, f32[16]{0:T(128)}, u32[]{:S(2)}) copy-start(f32[16]{0:T(128)} %param.11) | copy-start | bytes 196

commit v7 on v6

v7 whole, which is shorter than its diff:
```python
import functools
import math

import jax
import jax.numpy as jnp
from jax import lax
from jax.experimental import pallas as pl
from jax.experimental.pallas import tpu as pltpu
from jax.sharding import PartitionSpec as P

HIGH_PREC = lax.Precision.HIGHEST


def mm(pattern, left_op, right_op):
    return jnp.einsum(pattern, left_op, right_op, precision=HIGH_PREC)


GROUP = 8
LANES = 128
SLABS = 8


def row_sum(value):
    return jnp.sum(value, axis=0, keepdims=True)


def slab_coefs(count, size, pos, inv, block_len, modes):
    lane = lax.broadcasted_iota(jnp.int32, (count, LANES), 1) // modes
    index = lax.broadcasted_iota(jnp.int32, (count, LANES), 0)
    span = float(size * block_len)
    step = jnp.exp(-span * inv)
    starts = index.astype(jnp.float32) * span
    lag = jnp.exp(-starts * inv)
    before = jnp.where(index < pos, jnp.exp(-((pos - 1 - index).astype(jnp.float32) * span) * inv), 0.0)
    after = jnp.where(index > pos, jnp.exp(-((index - pos - 1).astype(jnp.float32) * span) * inv), 0.0)
    keep = jnp.where(lane <= 1, step, 1.0)[0:1]
    carry = jnp.where(lane == 1, step * span, 0.0)[0:1]
    take = jnp.where((lane >= 2) & (lane <= 4), lag, 1.0)
    shift = jnp.where(lane == 4, lag * starts * inv, 0.0)
    edge = jnp.where(lane == 0, before, jnp.where(lane == 2, after, 0.0))
    return keep, carry, take, shift, edge


def fold_items(items, coefs, inv, modes):
    keep, carry, take, shift, edge_c = coefs
    lane = lax.broadcasted_iota(jnp.int32, (1, LANES), 1) // modes
    acc = items[0]
    edge = edge_c[0:1] * acc
    for index in range(1, len(items)):
        item = items[index]
        s1 = row_sum(pltpu.roll(acc, 3 * modes, 1) * item)
        s2 = row_sum(pltpu.roll(acc, 4 * modes, 1) * item)
        s3 = row_sum(pltpu.roll(acc, 2 * modes, 1) * item)
        cross = jnp.where(lane == 5, pltpu.roll(s1, 2 * modes, 1), 0.0) + jnp.where(
            lane == 6, pltpu.roll(s2, 2 * modes, 1) + pltpu.roll(s3 * inv, 3 * modes, 1), 0.0)
        acc = (keep * acc + take[index:index + 1] * item + carry * pltpu.roll(acc, modes, 1)
               + shift[index:index + 1] * pltpu.roll(item, modes, 1) + cross)
        edge = edge + edge_c[index:index + 1] * item
    return acc, edge


def start_ring(buf, send_sems, recv_sems, count, pos, device_of):
    descs = []
    for dist in range(1, count):
        desc = pltpu.make_async_remote_copy(
            src_ref=buf.at[0],
            dst_ref=buf.at[count - dist],
            send_sem=send_sems.at[dist],
            recv_sem=recv_sems.at[count - dist],
            device_id=device_of((pos + dist) % count),
            device_id_type=pl.DeviceIdType.MESH,
        )
        desc.start()
        descs.append(desc)
    return descs


def finish_ring(descs, buf, count, pos):
    for desc in descs:
        desc.wait_recv()
    for desc in descs:
        desc.wait_send()
    return [buf[(slot - pos + count) % count] for slot in range(count)]


def dot_nn(left_op, right_op):
    return jnp.dot(left_op, right_op, precision=HIGH_PREC, preferred_element_type=jnp.float32)


def dot_nt(left_op, right_op):
    return lax.dot_general(left_op, right_op, (((1,), (1,)), ((), ())), precision=HIGH_PREC,
                           preferred_element_type=jnp.float32)


def dot_tn(left_op, right_op):
    return lax.dot_general(left_op, right_op, (((0,), (0,)), ((), ())), precision=HIGH_PREC,
                           preferred_element_type=jnp.float32)


def fused_kernel(counts, modes, x_ref, q_ref, k_ref, d_ref, par_ref,
                 out_ref, gx_ref, gq_ref, gk_ref, small_ref,
                 buf_a, buf_b, buf_c, send_a, recv_a, send_b, recv_b, send_c, recv_c):
    count_a, count_b, count_c = counts
    channels, block_len = x_ref.shape
    seq_index = lax.axis_index("seq")
    ch_index = lax.axis_index("ch")
    pos_a = seq_index % count_a
    pos_b = seq_index // count_a

    def dev_a(other):
        return (pos_b * count_a + other, ch_index)

    def dev_b(other):
        return (other * count_a + pos_a, ch_index)

    def dev_c(other):
        return (seq_index, other)

    barrier = pltpu.get_barrier_semaphore()
    for count, pos, device_of in ((count_a, pos_a, dev_a), (count_b, pos_b, dev_b), (count_c, ch_index, dev_c)):
        for dist in range(1, count):
            pl.semaphore_signal(barrier, inc=1, device_id=device_of((pos + dist) % count),
                                device_id_type=pl.DeviceIdType.MESH)

    par = par_ref[...]
    inv = par[0:1]
    amp = par[1:2]
    gain = par[8:8 + channels, 0:1]
    slab = lax.broadcasted_iota(jnp.int32, (1, LANES), 1) // modes
    offs = lax.broadcasted_iota(jnp.int32, (block_len, LANES), 0).astype(jnp.float32)
    back = float(block_len - 1) - offs
    e_down = jnp.exp(-offs * inv)
    e_tail = jnp.exp(-back * inv)
    e_next = jnp.exp(-(offs + 1.0) * inv)
    e_up = jnp.exp(offs * inv)
    right_v = jnp.where(slab == 0, e_tail, jnp.where(slab == 1, e_tail * back, 0.0))
    right_g = jnp.where(slab == 2, e_down, jnp.where(slab == 3, e_next, jnp.where(
        slab == 4, e_next * ((offs + 1.0) * inv - 0.5), 0.0)))
    right_r = jnp.where(slab == 5, e_up, jnp.where(slab == 6, e_up * offs * inv, 0.0))

    x_float = x_ref[...].astype(jnp.float32)
    q_float = q_ref[...].astype(jnp.float32)
    k_float = k_ref[...].astype(jnp.float32)
    d_float = d_ref[...].astype(jnp.float32)
    values = x_float * k_float
    grad_mixed = d_float * q_float
    row_t = lax.broadcasted_iota(jnp.int32, (block_len, block_len), 0)
    col_s = lax.broadcasted_iota(jnp.int32, (block_len, block_len), 1)
    lower = row_t >= col_s
    pair = jnp.where(lower, dot_tn(grad_mixed, values), 0.0)
    near = dot_nn(pair, right_r)
    terms = jnp.where(slab == 5, e_down * near, jnp.where(
        slab == 6, e_down * ((offs * inv - 0.5) * pltpu.roll(near, modes, 1) - near), 0.0))
    local = row_sum(terms)
    skip = jnp.sum(grad_mixed * values, axis=1, keepdims=True)
    state = dot_nn(values, right_v) + dot_nn(grad_mixed, right_g) + jnp.where(slab == 7, skip, local)
    buf_a[0] = state
    coefs_a = slab_coefs(count_a, 1, pos_a, inv, block_len, modes)
    coefs_b = slab_coefs(count_b, count_a, pos_b, inv, block_len, modes)
    near_w = jnp.exp(-(pos_a * block_len).astype(jnp.float32) * inv)
    far_w = jnp.exp(-((count_a - 1 - pos_a) * block_len).astype(jnp.float32) * inv)
    join = jnp.where(slab == 0, near_w, jnp.where(slab == 2, far_w, 0.0))
    pl.semaphore_wait(barrier, count_a + count_b + count_c - 3)

    descs = start_ring(buf_a, send_a, recv_a, count_a, pos_a, dev_a)
    toep = jnp.where(lower, dot_nt(jnp.where(slab == 0, e_down * amp, 0.0), jnp.where(slab == 0, e_up, 0.0)), 0.0)
    conv = dot_nt(values, toep)
    corr = dot_nn(grad_mixed, toep)
    into_f = jnp.where(slab == 0, e_next * amp, 0.0)
    into_b = jnp.where(slab == 2, jnp.exp(-(float(block_len) - offs) * inv) * amp, 0.0)
    items = finish_ring(descs, buf_a, count_a, pos_a)
    group, edge_a = fold_items(items, coefs_a, inv, modes)
    buf_b[0] = group
    descs = start_ring(buf_b, send_b, recv_b, count_b, pos_b, dev_b)
    items = finish_ring(descs, buf_b, count_b, pos_b)
    total, edge_b = fold_items(items, coefs_b, inv, modes)
    buf_c[0] = total
    descs = start_ring(buf_c, send_c, recv_c, count_c, ch_index, dev_c)
    edge = join * edge_b + edge_a
    conv = conv + dot_nt(edge, into_f)
    corr = corr + dot_nt(edge, into_b)
    mixed_out = conv + gain * values
    grad_values = gain * grad_mixed + corr
    out_ref[...] = (q_float * mixed_out).astype(jnp.bfloat16)
    gx_ref[...] = (grad_values * k_float).astype(jnp.bfloat16)
    gq_ref[...] = (d_float * mixed_out).astype(jnp.bfloat16)
    gk_ref[...] = (grad_values * x_float).astype(jnp.bfloat16)
    items = finish_ring(descs, buf_c, count_c, ch_index)
    sums = items[0]
    for item in items[1:]:
        sums = sums + item
    small_ref[0] = total
    small_ref[1] = sums


def per_device(signal_x, gate_q, gate_k, skip_gain, residue, memory, cotangent):
    channels, block_len = signal_x.shape
    modes = memory.shape[0]
    seq_total = lax.axis_size("seq") * block_len
    all_channels = channels * lax.axis_size("ch")
    count_a = min(GROUP, lax.axis_size("seq"))
    count_b = lax.axis_size("seq") // count_a
    count_c = lax.axis_size("ch")
    inv_m = 1.0 / memory
    gain = jnp.sqrt(2.0 / memory)
    amp = residue * gain
    reps = LANES // modes
    par = jnp.concatenate([
        jnp.tile(inv_m, reps)[None, :],
        jnp.tile(amp, reps)[None, :],
        jnp.zeros((6, LANES), jnp.float32),
        jnp.broadcast_to(skip_gain[:, None], (channels, LANES)),
    ], axis=0)
    msg = (channels, LANES)
    vmem = pl.BlockSpec(memory_space=pltpu.VMEM)
    half = jax.ShapeDtypeStruct(signal_x.shape, jnp.bfloat16)
    output, grad_x, grad_q, grad_k, small = pl.pallas_call(
        functools.partial(fused_kernel, (count_a, count_b, count_c), modes),
        out_shape=(half, half, half, half, jax.ShapeDtypeStruct((2,) + msg, jnp.float32)),
        in_specs=[vmem] * 5,
        out_specs=(vmem,) * 5,
        scratch_shapes=[
            pltpu.VMEM((count_a,) + msg, jnp.float32),
            pltpu.VMEM((count_b,) + msg, jnp.float32),
            pltpu.VMEM((count_c,) + msg, jnp.float32),
            pltpu.SemaphoreType.DMA((count_a,)),
            pltpu.SemaphoreType.DMA((count_a,)),
            pltpu.SemaphoreType.DMA((count_b,)),
            pltpu.SemaphoreType.DMA((count_b,)),
            pltpu.SemaphoreType.DMA((count_c,)),
            pltpu.SemaphoreType.DMA((count_c,)),
        ],
        compiler_params=pltpu.CompilerParams(collective_id=0, has_side_effects=True),
    )(signal_x, gate_q, gate_k, cotangent, par)
    total, sums = small[0], small[1]
    norm_scale = 1.0 / math.sqrt(all_channels * seq_total)
    grad_skip = total[:, 7 * modes] / math.sqrt(seq_total)
    grad_residue = gain * sums[0, 5 * modes:6 * modes] * norm_scale
    grad_memory = residue * gain * sums[0, 6 * modes:7 * modes] * norm_scale
    return (output, grad_x, grad_q, grad_k, grad_skip, grad_residue, grad_memory)


def solution(mesh):
    return jax.shard_map(
        per_device,
        mesh=mesh,
        in_specs=(
            P("ch", "seq"),
            P("ch", "seq"),
            P("ch", "seq"),
            P("ch"),
            P(),
            P(),
            P("ch", "seq"),
        ),
        out_specs=(
            P("ch", "seq"),
            P("ch", "seq"),
            P("ch", "seq"),
            P("ch", "seq"),
            P("ch"),
            P(),
            P(),
        ),
        check_vma=False,
    )
```

time: 54.9 us -> 44.6 us (0.81)
  matrix products: 6.66 us -> 0 us
  Pallas kernels: 38.6 us -> 36.3 us
  other arithmetic: 3.93 us -> 1.98 us
  local copies, waits for them, and re-layouts: 4.49 us -> 5.07 us
    dot_general x6 -> x0, matrix products: 6.66 us -> none  [mm(): return jnp.einsum(pattern, left_op, right_op, precision=HIGH_PREC)]
    unnamed x14 -> x16, local copies, waits for them, and re-layouts: 0.68 us -> 3.38 us
    pallas_call x2 -> x1, Pallas kernels: 38.6 us -> 36.3 us  [per_device(): pl.pallas_call(functools.partial(fused_kernel, (count_a, count_b, count_c...]
    broadcast_in_dim x7 -> x1, local copies, waits for them, and re-layouts: 1.4 us -> 0.01 us  [per_device(): jnp.zeros((6, LANES), jnp.float32)]
    another operation x2 -> x0, other arithmetic: 0.95 us -> none  [per_device(): jnp.stack([jnp.concatenate([(e_next * amp).T, zero_rows, fill], axis=0),...]
    reduce_sum x1 -> x0, other arithmetic: 0.92 us -> none  [per_device(): part_skip = jnp.sum(grad_mixed * values, axis=1)]
    mul x2 -> x1, other arithmetic: 0.67 us -> 0.01 us  [per_device(): amp = residue * gain]
    squeeze x1, local copies, waits for them, and re-layouts: 1.34 us -> 0.72 us  [per_device(): total, sums = (small[0], small[1])]
where the time goes in v7:
time: 44.6 us; the launch traced here: 44 us
  Pallas kernels  36.3 us (81%)
  local copies, waits for them, and re-layouts  5.07 us (11%)
  other arithmetic  1.98 us (4%)
  between operations  0.66 us (1%)
    pallas_call x1, Pallas kernels, per_device(): pl.pallas_call(functools.partial(fused_kernel, (count_a, count_b, count_c...  36.3 us
    unnamed x16, local copies, waits for them, and re-layouts  3.38 us

profile of v7, /device:TPU:1, one launch (start us, length us, event | category | flops | bytes accessed | tf_op | source)
XLA Modules:
  0.0 44.0 jit_solution(3914898430153954917)
XLA Ops:
  0.6 0.7 %pad.3.clone = f32[24]{0:T(128)S(1)} pad(f32[16]{0:T(128)} %param.10, f32[]{:T(128)} %constant.12), padding=8_0 | pad | bytes 164 | tf_op jit(solution)/shard_map/concatenate | solution.py:208
  1.4 0.0 copy-start.4
  1.4 0.0 copy-start.5
  1.4 0.1 pad.2.clone
  1.4 0.6 %copy-done.4 = f32[16]{0:T(128)S(1)} copy-done((f32[16]{0:T(128)S(1)}, f32[16]{0:T(128)}, u32[]{:S(2)}) %copy-start.4) | copy-done | bytes 88
  2.0 0.0 copy-done.5
  2.0 0.1 broadcast_in_dim_tile.6
  2.1 0.1 broadcast_in_dim_tile.7
  2.2 0.7 %maximum_maximum_fusion.par_ref = f32[24,128]{1,0:T(8,128)} fusion(f32[1,128]{1,0:T(1,128)S(1)} %broadcast_in_dim_tile.7, f32[1,128]{1,0:T(1,128)S(1)} %broadcast_in_dim_tile.6, f32[24]{0:T(128)S(1)} %pad.3.clone, f32[24]{0:T(128)S(1)} %pad.2.clone), kind=kLoop, calls=%fused_computation | loop fusion | flops 9216 | bytes 13504 | tf_op jit(solution)/shard_map/concatenate | solution.py:208
  2.9 36.3 %shard_map.126 = (bf16[16,512]{1,0:T(8,128)(2,1)}, bf16[16,512]{1,0:T(8,128)(2,1)}, bf16[16,512]{1,0:T(8,128)(2,1)}, bf16[16,512]{1,0:T(8,128)(2,1)}, f32[2,16,128]{2,1,0:T(8,128)}) custom-call(bf16[16,512]{1,0:T(8,128)(2,1)} %x_ref.1, bf16[16,512]{1,0:T(8,128)(2,1)} %q_ref.1, bf16[16,512]{1,0:T(8,128)(2,1)} %k_ref.1, bf16[16,512]{1,0:T(8,128)(2,1)} %d_ref.1, ...), custom_call_target="tpu_custom_call" | custom-call | tf_op jit(solution)/shard_map/pallas_call | solution.py:217
  39.2 0.7 %slice_bitcast_fusion = (f32[16,128]{1,0:T(8,128)S(1)}, f32[16,128]{1,0:T(8,128)S(1)}) fusion(f32[2,16,128]{2,1,0:T(8,128)} %get-tuple-element.16), kind=kLoop, calls=%fused_computation.3 | loop fusion | bytes 32768 | tf_op jit(solution)/shard_map/squeeze | solution.py:235
  39.9 0.0 copy-start.3
  39.9 0.6 %fusion.2 = (f32[16]{0:T(128)}, f32[16]{0:T(128)}) fusion(f32[16]{0:T(128)S(1)} %get-tuple-element.17, f32[16,128]{1,0:T(8,128)S(1)} %get-tuple-element.19, f32[16]{0:T(128)S(1)} %get-tuple-element.18), kind=kLoop, calls=%fused_computation.7 | loop fusion | flops 64 | bytes 384 | tf_op jit(solution)/shard_map/mul | solution.py:239
  40.5 0.7 %fusion = f32[16]{0:T(128)} fusion(f32[16,128]{1,0:T(8,128)S(1)} %get-tuple-element.20), kind=kLoop, calls=%fused_computation.2 | loop fusion | flops 16 | bytes 128 | tf_op jit(solution)/shard_map/div | solution.py:237
  41.2 0.0 copy-done.3
  41.2 0.0 copy-start.2
  41.2 0.6 %copy.18 = bf16[16,512]{1,0:T(8,128)(2,1)} copy(bf16[16,512]{1,0:T(8,128)(2,1)S(1)} %copy-done.3) | data formatting | bytes 32768
  41.8 0.1 copy-done.2
  41.9 0.0 copy-start.1
  41.9 0.6 %copy.19 = bf16[16,512]{1,0:T(8,128)(2,1)} copy(bf16[16,512]{1,0:T(8,128)(2,1)S(1)} %copy-done.2) | data formatting | bytes 32768
  42.5 0.1 copy-done.1
  42.6 0.0 copy-start
  42.6 0.6 %copy.20 = bf16[16,512]{1,0:T(8,128)(2,1)} copy(bf16[16,512]{1,0:T(8,128)(2,1)S(1)} %copy-done.1) | data formatting | bytes 32768
  43.2 0.1 copy-done
  43.4 0.6 %copy.21 = bf16[16,512]{1,0:T(8,128)(2,1)} copy(bf16[16,512]{1,0:T(8,128)(2,1)S(1)} %copy-done) | data formatting | bytes 32768
  (4 shorter events, 0.0 us)
Async XLA Ops:
  1.4 0.7 %copy-start.4 = (f32[16]{0:T(128)S(1)}, f32[16]{0:T(128)}, u32[]{:S(2)}) copy-start(f32[16]{0:T(128)} %param.11) | copy-start | bytes 196
  1.4 0.7 %copy-start.5 = (f32[16]{0:T(128)S(1)}, f32[16]{0:T(128)}, u32[]{:S(2)}) copy-start(f32[16]{0:T(128)} %param.12) | copy-start | bytes 196
  39.9 1.3 %copy-start.3 = (bf16[16,512]{1,0:T(8,128)(2,1)S(1)}, bf16[16,512]{1,0:T(8,128)(2,1)}, u32[]{:S(2)}) copy-start(bf16[16,512]{1,0:T(8,128)(2,1)} %get-tuple-element.31) | copy-start | bytes 49156
  41.2 0.7 %copy-start.2 = (bf16[16,512]{1,0:T(8,128)(2,1)S(1)}, bf16[16,512]{1,0:T(8,128)(2,1)}, u32[]{:S(2)}) copy-start(bf16[16,512]{1,0:T(8,128)(2,1)} %get-tuple-element.32) | copy-start | bytes 49156
  41.9 0.7 %copy-start.1 = (bf16[16,512]{1,0:T(8,128)(2,1)S(1)}, bf16[16,512]{1,0:T(8,128)(2,1)}, u32[]{:S(2)}) copy-start(bf16[16,512]{1,0:T(8,128)(2,1)} %get-tuple-element.33) | copy-start | bytes 49156
  42.6 0.7 %copy-start = (bf16[16,512]{1,0:T(8,128)(2,1)S(1)}, bf16[16,512]{1,0:T(8,128)(2,1)}, u32[]{:S(2)}) copy-start(bf16[16,512]{1,0:T(8,128)(2,1)} %get-tuple-element.34) | copy-start | bytes 49156

commit v8 on v7

--- a/solution.py
+++ b/solution.py
@@ -41,22 +41,43 @@
     return keep, carry, take, shift, edge
 
 
-def fold_items(items, coefs, inv, modes):
-    keep, carry, take, shift, edge_c = coefs
-    lane = lax.broadcasted_iota(jnp.int32, (1, LANES), 1) // modes
-    acc = items[0]
-    edge = edge_c[0:1] * acc
+def level_coefs(count, size, inv, block_len, modes):
+    slab = lax.broadcasted_iota(jnp.int32, (1, LANES), 1) // modes
+    levels = []
+    width = size
+    while width < count * size:
+        span = float(width * block_len)
+        step = jnp.exp(-span * inv)
+        levels.append((
+            jnp.where(slab <= 1, step, 1.0),
+            jnp.where(slab == 1, step * span, 0.0),
+            jnp.where((slab >= 2) & (slab <= 4), step, 1.0),
+            jnp.where(slab == 4, step * span * inv, 0.0),
+        ))
+        width *= 2
+    return levels
+
+
+def combine_pair(left, right, coefs, inv, modes):
+    keep, carry, take, shift = coefs
+    slab = lax.broadcasted_iota(jnp.int32, (1, LANES), 1) // modes
+    s1 = row_sum(pltpu.roll(left, 3 * modes, 1) * right)
+    s2 = row_sum(pltpu.roll(left, 4 * modes, 1) * right)
+    s3 = row_sum(pltpu.roll(left, 2 * modes, 1) * right)
+    cross = jnp.where(slab == 5, pltpu.roll(s1, 2 * modes, 1), 0.0) + jnp.where(
+        slab == 6, pltpu.roll(s2, 2 * modes, 1) + pltpu.roll(s3 * inv, 3 * modes, 1), 0.0)
+    return (keep * left + take * right + carry * pltpu.roll(left, modes, 1)
+            + shift * pltpu.roll(right, modes, 1) + cross)
+
+
+def fold_items(items, levels, edge_c, inv, modes):
+    edge = edge_c[0:1] * items[0]
     for index in range(1, len(items)):
-        item = items[index]
-        s1 = row_sum(pltpu.roll(acc, 3 * modes, 1) * item)
-        s2 = row_sum(pltpu.roll(acc, 4 * modes, 1) * item)
-        s3 = row_sum(pltpu.roll(acc, 2 * modes, 1) * item)
-        cross = jnp.where(lane == 5, pltpu.roll(s1, 2 * modes, 1), 0.0) + jnp.where(
-            lane == 6, pltpu.roll(s2, 2 * modes, 1) + pltpu.roll(s3 * inv, 3 * modes, 1), 0.0)
-        acc = (keep * acc + take[index:index + 1] * item + carry * pltpu.roll(acc, modes, 1)
-               + shift[index:index + 1] * pltpu.roll(item, modes, 1) + cross)
-        edge = edge + edge_c[index:index + 1] * item
-    return acc, edge
+        edge = edge + edge_c[index:index + 1] * items[index]
+    layer = list(items)
+    for coefs in levels:
+        layer = [combine_pair(layer[i], layer[i + 1], coefs, inv, modes) for i in range(0, len(layer), 2)]
+    return layer[0], edge
 
 
 def start_ring(buf, send_sems, recv_sems, count, pos, device_of):
@@ -155,8 +176,10 @@
     skip = jnp.sum(grad_mixed * values, axis=1, keepdims=True)
     state = dot_nn(values, right_v) + dot_nn(grad_mixed, right_g) + jnp.where(slab == 7, skip, local)
     buf_a[0] = state
-    coefs_a = slab_coefs(count_a, 1, pos_a, inv, block_len, modes)
-    coefs_b = slab_coefs(count_b, count_a, pos_b, inv, block_len, modes)
+    edge_a_c = slab_coefs(count_a, 1, pos_a, inv, block_len, modes)[4]
+    edge_b_c = slab_coefs(count_b, count_a, pos_b, inv, block_len, modes)[4]
+    levels_a = level_coefs(count_a, 1, inv, block_len, modes)
+    levels_b = level_coefs(count_b, count_a, inv, block_len, modes)
     near_w = jnp.exp(-(pos_a * block_len).astype(jnp.float32) * inv)
     far_w = jnp.exp(-((count_a - 1 - pos_a) * block_len).astype(jnp.float32) * inv)
     join = jnp.where(slab == 0, near_w, jnp.where(slab == 2, far_w, 0.0))
@@ -169,11 +192,11 @@
     into_f = jnp.where(slab == 0, e_next * amp, 0.0)
     into_b = jnp.where(slab == 2, jnp.exp(-(float(block_len) - offs) * inv) * amp, 0.0)
     items = finish_ring(descs, buf_a, count_a, pos_a)
-    group, edge_a = fold_items(items, coefs_a, inv, modes)
+    group, edge_a = fold_items(items, levels_a, edge_a_c, inv, modes)
     buf_b[0] = group
     descs = start_ring(buf_b, send_b, recv_b, count_b, pos_b, dev_b)
     items = finish_ring(descs, buf_b, count_b, pos_b)
-    total, edge_b = fold_items(items, coefs_b, inv, modes)
+    total, edge_b = fold_items(items, levels_b, edge_b_c, inv, modes)
     buf_c[0] = total
     descs = start_ring(buf_c, send_c, recv_c, count_c, ch_index, dev_c)
     edge = join * edge_b + edge_a

time: 44.6 us -> 42.6 us (0.955)
  Pallas kernels: 36.3 us -> 34.3 us
    pallas_call x1, Pallas kernels: 36.3 us -> 34.3 us  [per_device(): pl.pallas_call(functools.partial(fused_kernel, (count_a, count_b, count_c...]
where the time goes in v8:
time: 42.6 us; the launch traced here: 42 us
  Pallas kernels  34.3 us (81%)
  local copies, waits for them, and re-layouts  5.07 us (12%)
  other arithmetic  1.98 us (5%)
  between operations  0.66 us (2%)
    pallas_call x1, Pallas kernels, per_device(): pl.pallas_call(functools.partial(fused_kernel, (count_a, count_b, count_c...  34.3 us
    unnamed x16, local copies, waits for them, and re-layouts  3.38 us

profile of v8, /device:TPU:1, one launch (start us, length us, event | category | flops | bytes accessed | tf_op | source)
XLA Modules:
  0.0 42.0 jit_solution(11231339422839579452)
XLA Ops:
  0.6 0.7 %pad.3.clone = f32[24]{0:T(128)S(1)} pad(f32[16]{0:T(128)} %param.10, f32[]{:T(128)} %constant.12), padding=8_0 | pad | bytes 164 | tf_op jit(solution)/shard_map/concatenate | solution.py:231
  1.4 0.0 copy-start.4
  1.4 0.0 copy-start.5
  1.4 0.1 pad.2.clone
  1.4 0.6 %copy-done.4 = f32[16]{0:T(128)S(1)} copy-done((f32[16]{0:T(128)S(1)}, f32[16]{0:T(128)}, u32[]{:S(2)}) %copy-start.4) | copy-done | bytes 88
  2.0 0.0 copy-done.5
  2.0 0.1 broadcast_in_dim_tile.6
  2.1 0.1 broadcast_in_dim_tile.7
  2.2 0.7 %maximum_maximum_fusion.par_ref = f32[24,128]{1,0:T(8,128)} fusion(f32[1,128]{1,0:T(1,128)S(1)} %broadcast_in_dim_tile.7, f32[1,128]{1,0:T(1,128)S(1)} %broadcast_in_dim_tile.6, f32[24]{0:T(128)S(1)} %pad.3.clone, f32[24]{0:T(128)S(1)} %pad.2.clone), kind=kLoop, calls=%fused_computation | loop fusion | flops 9216 | bytes 13504 | tf_op jit(solution)/shard_map/concatenate | solution.py:231
  2.9 34.3 %shard_map.126 = (bf16[16,512]{1,0:T(8,128)(2,1)}, bf16[16,512]{1,0:T(8,128)(2,1)}, bf16[16,512]{1,0:T(8,128)(2,1)}, bf16[16,512]{1,0:T(8,128)(2,1)}, f32[2,16,128]{2,1,0:T(8,128)}) custom-call(bf16[16,512]{1,0:T(8,128)(2,1)} %x_ref.1, bf16[16,512]{1,0:T(8,128)(2,1)} %q_ref.1, bf16[16,512]{1,0:T(8,128)(2,1)} %k_ref.1, bf16[16,512]{1,0:T(8,128)(2,1)} %d_ref.1, ...), custom_call_target="tpu_custom_call" | custom-call | tf_op jit(solution)/shard_map/pallas_call | solution.py:240
  37.2 0.7 %slice_bitcast_fusion = (f32[16,128]{1,0:T(8,128)S(1)}, f32[16,128]{1,0:T(8,128)S(1)}) fusion(f32[2,16,128]{2,1,0:T(8,128)} %get-tuple-element.16), kind=kLoop, calls=%fused_computation.3 | loop fusion | bytes 32768 | tf_op jit(solution)/shard_map/squeeze | solution.py:258
  37.9 0.0 copy-start.3
  37.9 0.6 %fusion.2 = (f32[16]{0:T(128)}, f32[16]{0:T(128)}) fusion(f32[16]{0:T(128)S(1)} %get-tuple-element.17, f32[16,128]{1,0:T(8,128)S(1)} %get-tuple-element.19, f32[16]{0:T(128)S(1)} %get-tuple-element.18), kind=kLoop, calls=%fused_computation.7 | loop fusion | flops 64 | bytes 384 | tf_op jit(solution)/shard_map/mul | solution.py:262
  38.5 0.7 %fusion = f32[16]{0:T(128)} fusion(f32[16,128]{1,0:T(8,128)S(1)} %get-tuple-element.20), kind=kLoop, calls=%fused_computation.2 | loop fusion | flops 16 | bytes 128 | tf_op jit(solution)/shard_map/div | solution.py:260
  39.2 0.0 copy-done.3
  39.2 0.0 copy-start.2
  39.2 0.6 %copy.18 = bf16[16,512]{1,0:T(8,128)(2,1)} copy(bf16[16,512]{1,0:T(8,128)(2,1)S(1)} %copy-done.3) | data formatting | bytes 32768
  39.8 0.1 copy-done.2
  39.9 0.0 copy-start.1
  39.9 0.6 %copy.19 = bf16[16,512]{1,0:T(8,128)(2,1)} copy(bf16[16,512]{1,0:T(8,128)(2,1)S(1)} %copy-done.2) | data formatting | bytes 32768
  40.5 0.1 copy-done.1
  40.6 0.0 copy-start
  40.6 0.6 %copy.20 = bf16[16,512]{1,0:T(8,128)(2,1)} copy(bf16[16,512]{1,0:T(8,128)(2,1)S(1)} %copy-done.1) | data formatting | bytes 32768
  41.2 0.1 copy-done
  41.4 0.6 %copy.21 = bf16[16,512]{1,0:T(8,128)(2,1)} copy(bf16[16,512]{1,0:T(8,128)(2,1)S(1)} %copy-done) | data formatting | bytes 32768
  (4 shorter events, 0.0 us)
Async XLA Ops:
  1.4 0.7 %copy-start.4 = (f32[16]{0:T(128)S(1)}, f32[16]{0:T(128)}, u32[]{:S(2)}) copy-start(f32[16]{0:T(128)} %param.11) | copy-start | bytes 196
  1.4 0.7 %copy-start.5 = (f32[16]{0:T(128)S(1)}, f32[16]{0:T(128)}, u32[]{:S(2)}) copy-start(f32[16]{0:T(128)} %param.12) | copy-start | bytes 196
  37.9 1.3 %copy-start.3 = (bf16[16,512]{1,0:T(8,128)(2,1)S(1)}, bf16[16,512]{1,0:T(8,128)(2,1)}, u32[]{:S(2)}) copy-start(bf16[16,512]{1,0:T(8,128)(2,1)} %get-tuple-element.31) | copy-start | bytes 49156
  39.2 0.7 %copy-start.2 = (bf16[16,512]{1,0:T(8,128)(2,1)S(1)}, bf16[16,512]{1,0:T(8,128)(2,1)}, u32[]{:S(2)}) copy-start(bf16[16,512]{1,0:T(8,128)(2,1)} %get-tuple-element.32) | copy-start | bytes 49156
  39.9 0.7 %copy-start.1 = (bf16[16,512]{1,0:T(8,128)(2,1)S(1)}, bf16[16,512]{1,0:T(8,128)(2,1)}, u32[]{:S(2)}) copy-start(bf16[16,512]{1,0:T(8,128)(2,1)} %get-tuple-element.33) | copy-start | bytes 49156
  40.6 0.7 %copy-start = (bf16[16,512]{1,0:T(8,128)(2,1)S(1)}, bf16[16,512]{1,0:T(8,128)(2,1)}, u32[]{:S(2)}) copy-start(bf16[16,512]{1,0:T(8,128)(2,1)} %get-tuple-element.34) | copy-start | bytes 49156

commit v9 on v8

--- a/solution.py
+++ b/solution.py
@@ -118,7 +118,7 @@
                            preferred_element_type=jnp.float32)
 
 
-def fused_kernel(counts, modes, x_ref, q_ref, k_ref, d_ref, par_ref,
+def fused_kernel(counts, modes, x_ref, q_ref, k_ref, d_ref, mem_ref, res_ref, gain_ref,
                  out_ref, gx_ref, gq_ref, gk_ref, small_ref,
                  buf_a, buf_b, buf_c, send_a, recv_a, send_b, recv_b, send_c, recv_c):
     count_a, count_b, count_c = counts
@@ -143,11 +143,19 @@
             pl.semaphore_signal(barrier, inc=1, device_id=device_of((pos + dist) % count),
                                 device_id_type=pl.DeviceIdType.MESH)
 
-    par = par_ref[...]
-    inv = par[0:1]
-    amp = par[1:2]
-    gain = par[8:8 + channels, 0:1]
     slab = lax.broadcasted_iota(jnp.int32, (1, LANES), 1) // modes
+    mode_of = lax.broadcasted_iota(jnp.int32, (1, LANES), 1) % modes
+    mem_v = jnp.zeros((1, LANES), jnp.float32)
+    res_v = jnp.zeros((1, LANES), jnp.float32)
+    for mode in range(modes):
+        mem_v = jnp.where(mode_of == mode, mem_ref[mode], mem_v)
+        res_v = jnp.where(mode_of == mode, res_ref[mode], res_v)
+    inv = 1.0 / mem_v
+    amp = res_v * jnp.sqrt(2.0 * inv)
+    chan_of = lax.broadcasted_iota(jnp.int32, (channels, 1), 0)
+    gain = jnp.zeros((channels, 1), jnp.float32)
+    for chan in range(channels):
+        gain = jnp.where(chan_of == chan, gain_ref[chan], gain)
     offs = lax.broadcasted_iota(jnp.int32, (block_len, LANES), 0).astype(jnp.float32)
     back = float(block_len - 1) - offs
     e_down = jnp.exp(-offs * inv)
@@ -227,20 +235,13 @@
     inv_m = 1.0 / memory
     gain = jnp.sqrt(2.0 / memory)
     amp = residue * gain
-    reps = LANES // modes
-    par = jnp.concatenate([
-        jnp.tile(inv_m, reps)[None, :],
-        jnp.tile(amp, reps)[None, :],
-        jnp.zeros((6, LANES), jnp.float32),
-        jnp.broadcast_to(skip_gain[:, None], (channels, LANES)),
-    ], axis=0)
     msg = (channels, LANES)
     vmem = pl.BlockSpec(memory_space=pltpu.VMEM)
     half = jax.ShapeDtypeStruct(signal_x.shape, jnp.bfloat16)
     output, grad_x, grad_q, grad_k, small = pl.pallas_call(
         functools.partial(fused_kernel, (count_a, count_b, count_c), modes),
         out_shape=(half, half, half, half, jax.ShapeDtypeStruct((2,) + msg, jnp.float32)),
-        in_specs=[vmem] * 5,
+        in_specs=[vmem] * 4 + [pl.BlockSpec(memory_space=pltpu.SMEM)] * 3,
         out_specs=(vmem,) * 5,
         scratch_shapes=[
             pltpu.VMEM((count_a,) + msg, jnp.float32),
@@ -254,7 +255,7 @@
             pltpu.SemaphoreType.DMA((count_c,)),
         ],
         compiler_params=pltpu.CompilerParams(collective_id=0, has_side_effects=True),
-    )(signal_x, gate_q, gate_k, cotangent, par)
+    )(signal_x, gate_q, gate_k, cotangent, memory, residue, skip_gain)
     total, sums = small[0], small[1]
     norm_scale = 1.0 / math.sqrt(all_channels * seq_total)
     grad_skip = total[:, 7 * modes] / math.sqrt(seq_total)

time: 42.6 us -> 40.9 us (0.960)
  local copies, waits for them, and re-layouts: 5.07 us -> 3.52 us
    concatenate x2 -> x0, local copies, waits for them, and re-layouts: 0.8 us -> none  [per_device(): jnp.concatenate([jnp.tile(inv_m, reps)[None, :], jnp.tile(amp, reps)[None...]
    concatenate x1 -> x0, other arithmetic: 0.69 us -> none  [per_device(): jnp.concatenate([jnp.tile(inv_m, reps)[None, :], jnp.tile(amp, reps)[None...]
    unnamed x16, local copies, waits for them, and re-layouts: 3.38 us -> 2.79 us
    mul x1, other arithmetic: 0.01 us -> 0.58 us  [per_device(): grad_residue = gain * sums[0, 5 * modes:6 * modes] * norm_scale]
where the time goes in v9:
time: 40.9 us; the launch traced here: 40.4 us
  Pallas kernels  34.4 us (84%)
  local copies, waits for them, and re-layouts  3.52 us (9%)
  other arithmetic  1.86 us (5%)
  between operations  0.67 us (2%)
    pallas_call x1, Pallas kernels, per_device(): pl.pallas_call(functools.partial(fused_kernel, (count_a, count_b, count_c...  34.4 us
    unnamed x16, local copies, waits for them, and re-layouts  2.79 us

profile of v9, /device:TPU:1, one launch (start us, length us, event | category | flops | bytes accessed | tf_op | source)
XLA Modules:
  0.0 40.4 jit_solution(9688751731857933024)
XLA Ops:
  0.6 34.4 %shard_map.126 = (bf16[16,512]{1,0:T(8,128)(2,1)}, bf16[16,512]{1,0:T(8,128)(2,1)}, bf16[16,512]{1,0:T(8,128)(2,1)}, bf16[16,512]{1,0:T(8,128)(2,1)}, f32[2,16,128]{2,1,0:T(8,128)}) custom-call(bf16[16,512]{1,0:T(8,128)(2,1)} %x_ref.1, bf16[16,512]{1,0:T(8,128)(2,1)} %q_ref.1, bf16[16,512]{1,0:T(8,128)(2,1)} %k_ref.1, bf16[16,512]{1,0:T(8,128)(2,1)} %d_ref.1, ...), custom_call_target="tpu_custom_call" | custom-call | tf_op jit(solution)/shard_map/pallas_call | solution.py:241
  35.0 0.0 copy-start.4
  35.0 0.0 copy-start.5
  35.0 0.7 %slice_bitcast_fusion = (f32[16,128]{1,0:T(8,128)S(1)}, f32[16,128]{1,0:T(8,128)S(1)}) fusion(f32[2,16,128]{2,1,0:T(8,128)} %get-tuple-element.16), kind=kLoop, calls=%fused_computation.2 | loop fusion | bytes 32768 | tf_op jit(solution)/shard_map/squeeze | solution.py:259
  35.7 0.0 copy-start.3
  35.8 0.7 %fusion = f32[16]{0:T(128)} fusion(f32[16,128]{1,0:T(8,128)S(1)} %get-tuple-element.20), kind=kLoop, calls=%fused_computation.1 | loop fusion | flops 16 | bytes 128 | tf_op jit(solution)/shard_map/div | solution.py:261
  36.4 0.0 copy-done.4
  36.4 0.0 copy-done.5
  36.5 0.6 %fusion.2 = (f32[16]{0:T(128)}, f32[16]{0:T(128)S(1)}) fusion(f32[16,128]{1,0:T(8,128)S(1)} %get-tuple-element.19, f32[16]{0:T(128)S(1)} %copy-done.5, f32[16]{0:T(128)S(1)} %copy-done.4), kind=kLoop, calls=%fused_computation.6 | loop fusion | flops 64 | bytes 320 | tf_op jit(solution)/shard_map/mul | solution.py:263
  37.0 0.6 %fusion.4 = f32[16]{0:T(128)} fusion(f32[16]{0:T(128)S(1)} %get-tuple-element.18, f32[16,128]{1,0:T(8,128)S(1)} %get-tuple-element.19), kind=kLoop, calls=%fused_computation.9 | loop fusion | flops 32 | bytes 192 | tf_op jit(solution)/shard_map/mul | solution.py:262
  37.6 0.0 copy-done.3
  37.6 0.0 copy-start.2
  37.6 0.6 %copy.18 = bf16[16,512]{1,0:T(8,128)(2,1)} copy(bf16[16,512]{1,0:T(8,128)(2,1)S(1)} %copy-done.3) | data formatting | bytes 32768
  38.2 0.1 copy-done.2
  38.3 0.0 copy-start.1
  38.3 0.6 %copy.19 = bf16[16,512]{1,0:T(8,128)(2,1)} copy(bf16[16,512]{1,0:T(8,128)(2,1)S(1)} %copy-done.2) | data formatting | bytes 32768
  39.0 0.1 copy-done.1
  39.1 0.0 copy-start
  39.1 0.6 %copy.20 = bf16[16,512]{1,0:T(8,128)(2,1)} copy(bf16[16,512]{1,0:T(8,128)(2,1)S(1)} %copy-done.1) | data formatting | bytes 32768
  39.7 0.1 copy-done
  39.8 0.6 %copy.21 = bf16[16,512]{1,0:T(8,128)(2,1)} copy(bf16[16,512]{1,0:T(8,128)(2,1)S(1)} %copy-done) | data formatting | bytes 32768
Async XLA Ops:
  35.0 1.4 %copy-start.4 = (f32[16]{0:T(128)S(1)}, f32[16]{0:T(128)}, u32[]{:S(2)}) copy-start(f32[16]{0:T(128)} %mem_ref.1) | copy-start | bytes 196
  35.0 1.4 %copy-start.5 = (f32[16]{0:T(128)S(1)}, f32[16]{0:T(128)}, u32[]{:S(2)}) copy-start(f32[16]{0:T(128)} %res_ref.1) | copy-start | bytes 196
  35.7 1.9 %copy-start.3 = (bf16[16,512]{1,0:T(8,128)(2,1)S(1)}, bf16[16,512]{1,0:T(8,128)(2,1)}, u32[]{:S(2)}) copy-start(bf16[16,512]{1,0:T(8,128)(2,1)} %get-tuple-element.28) | copy-start | bytes 49156
  37.6 0.7 %copy-start.2 = (bf16[16,512]{1,0:T(8,128)(2,1)S(1)}, bf16[16,512]{1,0:T(8,128)(2,1)}, u32[]{:S(2)}) copy-start(bf16[16,512]{1,0:T(8,128)(2,1)} %get-tuple-element.29) | copy-start | bytes 49156
  38.3 0.7 %copy-start.1 = (bf16[16,512]{1,0:T(8,128)(2,1)S(1)}, bf16[16,512]{1,0:T(8,128)(2,1)}, u32[]{:S(2)}) copy-start(bf16[16,512]{1,0:T(8,128)(2,1)} %get-tuple-element.30) | copy-start | bytes 49156
  39.1 0.7 %copy-start = (bf16[16,512]{1,0:T(8,128)(2,1)S(1)}, bf16[16,512]{1,0:T(8,128)(2,1)}, u32[]{:S(2)}) copy-start(bf16[16,512]{1,0:T(8,128)(2,1)} %get-tuple-element.31) | copy-start | bytes 49156

commit v10 on v9

--- a/solution.py
+++ b/solution.py
@@ -119,7 +119,7 @@
 
 
 def fused_kernel(counts, modes, x_ref, q_ref, k_ref, d_ref, mem_ref, res_ref, gain_ref,
-                 out_ref, gx_ref, gq_ref, gk_ref, small_ref,
+                 mix_ref, small_ref,
                  buf_a, buf_b, buf_c, send_a, recv_a, send_b, recv_b, send_c, recv_c):
     count_a, count_b, count_c = counts
     channels, block_len = x_ref.shape
@@ -212,16 +212,23 @@
     corr = corr + dot_nt(edge, into_b)
     mixed_out = conv + gain * values
     grad_values = gain * grad_mixed + corr
-    out_ref[...] = (q_float * mixed_out).astype(jnp.bfloat16)
-    gx_ref[...] = (grad_values * k_float).astype(jnp.bfloat16)
-    gq_ref[...] = (d_float * mixed_out).astype(jnp.bfloat16)
-    gk_ref[...] = (grad_values * x_float).astype(jnp.bfloat16)
+    mix_ref[0] = mixed_out
+    mix_ref[1] = grad_values
     items = finish_ring(descs, buf_c, count_c, ch_index)
     sums = items[0]
     for item in items[1:]:
         sums = sums + item
     small_ref[0] = total
     small_ref[1] = sums
+
+
+def output_kernel(x_ref, q_ref, k_ref, d_ref, mix_ref, out_ref, gx_ref, gq_ref, gk_ref):
+    mixed_out = mix_ref[0]
+    grad_values = mix_ref[1]
+    out_ref[...] = (q_ref[...].astype(jnp.float32) * mixed_out).astype(jnp.bfloat16)
+    gx_ref[...] = (grad_values * k_ref[...].astype(jnp.float32)).astype(jnp.bfloat16)
+    gq_ref[...] = (d_ref[...].astype(jnp.float32) * mixed_out).astype(jnp.bfloat16)
+    gk_ref[...] = (grad_values * x_ref[...].astype(jnp.float32)).astype(jnp.bfloat16)
 
 
 def per_device(signal_x, gate_q, gate_k, skip_gain, residue, memory, cotangent):
@@ -238,11 +245,12 @@
     msg = (channels, LANES)
     vmem = pl.BlockSpec(memory_space=pltpu.VMEM)
     half = jax.ShapeDtypeStruct(signal_x.shape, jnp.bfloat16)
-    output, grad_x, grad_q, grad_k, small = pl.pallas_call(
+    mix, small = pl.pallas_call(
         functools.partial(fused_kernel, (count_a, count_b, count_c), modes),
-        out_shape=(half, half, half, half, jax.ShapeDtypeStruct((2,) + msg, jnp.float32)),
+        out_shape=(jax.ShapeDtypeStruct((2,) + signal_x.shape, jnp.float32),
+                   jax.ShapeDtypeStruct((2,) + msg, jnp.float32)),
         in_specs=[vmem] * 4 + [pl.BlockSpec(memory_space=pltpu.SMEM)] * 3,
-        out_specs=(vmem,) * 5,
+        out_specs=(vmem,) * 2,
         scratch_shapes=[
             pltpu.VMEM((count_a,) + msg, jnp.float32),
             pltpu.VMEM((count_b,) + msg, jnp.float32),
@@ -256,6 +264,12 @@
         ],
         compiler_params=pltpu.CompilerParams(collective_id=0, has_side_effects=True),
     )(signal_x, gate_q, gate_k, cotangent, memory, residue, skip_gain)
+    output, grad_x, grad_q, grad_k = pl.pallas_call(
+        output_kernel,
+        out_shape=(half, half, half, half),
+        in_specs=[vmem] * 5,
+        out_specs=(vmem,) * 4,
+    )(signal_x, gate_q, gate_k, cotangent, mix)
     total, sums = small[0], small[1]
     norm_scale = 1.0 / math.sqrt(all_channels * seq_total)
     grad_skip = total[:, 7 * modes] / math.sqrt(seq_total)

time: 40.9 us -> 40.2 us (0.983)
  local copies, waits for them, and re-layouts: 3.52 us -> 1.39 us
  Pallas kernels: 34.4 us -> 35.9 us
    unnamed x16 -> x4, local copies, waits for them, and re-layouts: 2.79 us -> 0.67 us
    pallas_call x0 -> x1, Pallas kernels: none -> 1.54 us  [per_device(): pl.pallas_call(output_kernel, out_shape=(half, half, half, half), in_spec...]
where the time goes in v10:
time: 40.2 us; the launch traced here: 39.8 us
  Pallas kernels  35.9 us (89%)
  other arithmetic  1.86 us (5%)
  local copies, waits for them, and re-layouts  1.39 us (3%)
  between operations  0.64 us (2%)
    pallas_call x1, Pallas kernels, per_device(): pl.pallas_call(functools.partial(fused_kernel, (count_a, count_b, count_c...  34.4 us
    pallas_call x1, Pallas kernels, per_device(): pl.pallas_call(output_kernel, out_shape=(half, half, half, half), in_spec...  1.54 us

profile of v10, /device:TPU:1, one launch (start us, length us, event | category | flops | bytes accessed | tf_op | source)
XLA Modules:
  0.0 39.8 jit_solution(17091131972598519562)
XLA Ops:
  0.6 34.4 %shard_map.126 = (f32[2,16,512]{2,1,0:T(8,128)}, f32[2,16,128]{2,1,0:T(8,128)}) custom-call(bf16[16,512]{1,0:T(8,128)(2,1)} %x_ref.3, bf16[16,512]{1,0:T(8,128)(2,1)} %q_ref.3, bf16[16,512]{1,0:T(8,128)(2,1)} %k_ref.3, bf16[16,512]{1,0:T(8,128)(2,1)} %d_ref.3, f32[16]{0:T(128)} %mem_ref.1, f32[16]{0:T(128)} %res_ref.1, f32[16]{0:T(128)} %gain_ref.1), custom_call_target="tpu_custom_call" | custom-call | tf_op jit(solution)/shard_map/pallas_call | solution.py:248
  35.0 0.7 %slice_bitcast_fusion = (f32[16,128]{1,0:T(8,128)S(1)}, f32[16,128]{1,0:T(8,128)S(1)}) fusion(f32[2,16,128]{2,1,0:T(8,128)} %get-tuple-element.18), kind=kLoop, calls=%fused_computation.2 | loop fusion | bytes 32768 | tf_op jit(solution)/shard_map/squeeze | solution.py:273
  35.7 0.0 copy-start
  35.7 0.0 copy-start.1
  35.7 0.7 %copy-done = f32[16]{0:T(128)S(1)} copy-done((f32[16]{0:T(128)S(1)}, f32[16]{0:T(128)}, u32[]{:S(2)}) %copy-start) | copy-done | bytes 88
  36.4 0.0 copy-done.1
  36.4 0.6 %fusion.2 = (f32[16]{0:T(128)}, f32[16]{0:T(128)S(1)}) fusion(f32[16,128]{1,0:T(8,128)S(1)} %get-tuple-element.21, f32[16]{0:T(128)S(1)} %copy-done.1, f32[16]{0:T(128)S(1)} %copy-done), kind=kLoop, calls=%fused_computation.6 | loop fusion | flops 64 | bytes 320 | tf_op jit(solution)/shard_map/mul | solution.py:277
  37.0 0.6 %fusion.4 = f32[16]{0:T(128)} fusion(f32[16]{0:T(128)S(1)} %get-tuple-element.20, f32[16,128]{1,0:T(8,128)S(1)} %get-tuple-element.21), kind=kLoop, calls=%fused_computation.9 | loop fusion | flops 32 | bytes 192 | tf_op jit(solution)/shard_map/mul | solution.py:276
  37.5 1.5 %shard_map.127 = (bf16[16,512]{1,0:T(8,128)(2,1)}, bf16[16,512]{1,0:T(8,128)(2,1)}, bf16[16,512]{1,0:T(8,128)(2,1)}, bf16[16,512]{1,0:T(8,128)(2,1)}) custom-call(bf16[16,512]{1,0:T(8,128)(2,1)} %x_ref.3, bf16[16,512]{1,0:T(8,128)(2,1)} %q_ref.3, bf16[16,512]{1,0:T(8,128)(2,1)} %k_ref.3, bf16[16,512]{1,0:T(8,128)(2,1)} %d_ref.3, ...), custom_call_target="tpu_custom_call" | custom-call | tf_op jit(solution)/shard_map/pallas_call | solution.py:267
  39.1 0.7 %fusion = f32[16]{0:T(128)} fusion(f32[16,128]{1,0:T(8,128)S(1)} %get-tuple-element.22), kind=kLoop, calls=%fused_computation.1 | loop fusion | flops 16 | bytes 128 | tf_op jit(solution)/shard_map/div | solution.py:275
Async XLA Ops:
  35.7 0.7 %copy-start = (f32[16]{0:T(128)S(1)}, f32[16]{0:T(128)}, u32[]{:S(2)}) copy-start(f32[16]{0:T(128)} %mem_ref.1) | copy-start | bytes 196
  35.7 0.7 %copy-start.1 = (f32[16]{0:T(128)S(1)}, f32[16]{0:T(128)}, u32[]{:S(2)}) copy-start(f32[16]{0:T(128)} %res_ref.1) | copy-start | bytes 196

commit v11 on v10

--- a/solution.py
+++ b/solution.py
@@ -120,7 +120,7 @@
 
 def fused_kernel(counts, modes, x_ref, q_ref, k_ref, d_ref, mem_ref, res_ref, gain_ref,
                  mix_ref, small_ref,
-                 buf_a, buf_b, buf_c, send_a, recv_a, send_b, recv_b, send_c, recv_c):
+                 buf_a, buf_b, send_a, recv_a, send_b, recv_b):
     count_a, count_b, count_c = counts
     channels, block_len = x_ref.shape
     seq_index = lax.axis_index("seq")
@@ -132,13 +132,10 @@
         return (pos_b * count_a + other, ch_index)
 
     def dev_b(other):
-        return (other * count_a + pos_a, ch_index)
-
-    def dev_c(other):
-        return (seq_index, other)
+        return ((other // count_c) * count_a + pos_a, other % count_c)
 
     barrier = pltpu.get_barrier_semaphore()
-    for count, pos, device_of in ((count_a, pos_a, dev_a), (count_b, pos_b, dev_b), (count_c, ch_index, dev_c)):
+    for count, pos, device_of in ((count_a, pos_a, dev_a), (count_b * count_c, pos_b * count_c + ch_index, dev_b)):
         for dist in range(1, count):
             pl.semaphore_signal(barrier, inc=1, device_id=device_of((pos + dist) % count),
                                 device_id_type=pl.DeviceIdType.MESH)
@@ -191,7 +188,7 @@
     near_w = jnp.exp(-(pos_a * block_len).astype(jnp.float32) * inv)
     far_w = jnp.exp(-((count_a - 1 - pos_a) * block_len).astype(jnp.float32) * inv)
     join = jnp.where(slab == 0, near_w, jnp.where(slab == 2, far_w, 0.0))
-    pl.semaphore_wait(barrier, count_a + count_b + count_c - 3)
+    pl.semaphore_wait(barrier, count_a + count_b * count_c - 2)
 
     descs = start_ring(buf_a, send_a, recv_a, count_a, pos_a, dev_a)
     toep = jnp.where(lower, dot_nt(jnp.where(slab == 0, e_down * amp, 0.0), jnp.where(slab == 0, e_up, 0.0)), 0.0)
@@ -202,11 +199,26 @@
     items = finish_ring(descs, buf_a, count_a, pos_a)
     group, edge_a = fold_items(items, levels_a, edge_a_c, inv, modes)
     buf_b[0] = group
-    descs = start_ring(buf_b, send_b, recv_b, count_b, pos_b, dev_b)
-    items = finish_ring(descs, buf_b, count_b, pos_b)
-    total, edge_b = fold_items(items, levels_b, edge_b_c, inv, modes)
-    buf_c[0] = total
-    descs = start_ring(buf_c, send_c, recv_c, count_c, ch_index, dev_c)
+    count_bc = count_b * count_c
+    pos_bc = pos_b * count_c + ch_index
+    descs = start_ring(buf_b, send_b, recv_b, count_bc, pos_bc, dev_b)
+    for desc in descs:
+        desc.wait_recv()
+    for desc in descs:
+        desc.wait_send()
+    totals = []
+    for chan in range(count_c):
+        column = [buf_b[(group * count_c + chan - pos_bc + count_bc) % count_bc] for group in range(count_b)]
+        totals.append(fold_items(column, levels_b, edge_b_c, inv, modes)[0])
+    own = [buf_b[(group * count_c + ch_index - pos_bc + count_bc) % count_bc] for group in range(count_b)]
+    edge_b = edge_b_c[0:1] * own[0]
+    for group in range(1, count_b):
+        edge_b = edge_b + edge_b_c[group:group + 1] * own[group]
+    total = totals[0]
+    sums = totals[0]
+    for chan in range(1, count_c):
+        total = jnp.where(ch_index == chan, totals[chan], total)
+        sums = sums + totals[chan]
     edge = join * edge_b + edge_a
     conv = conv + dot_nt(edge, into_f)
     corr = corr + dot_nt(edge, into_b)
@@ -214,10 +226,6 @@
     grad_values = gain * grad_mixed + corr
     mix_ref[0] = mixed_out
     mix_ref[1] = grad_values
-    items = finish_ring(descs, buf_c, count_c, ch_index)
-    sums = items[0]
-    for item in items[1:]:
-        sums = sums + item
     small_ref[0] = total
     small_ref[1] = sums
 
@@ -253,14 +261,11 @@
         out_specs=(vmem,) * 2,
         scratch_shapes=[
             pltpu.VMEM((count_a,) + msg, jnp.float32),
-            pltpu.VMEM((count_b,) + msg, jnp.float32),
-            pltpu.VMEM((count_c,) + msg, jnp.float32),
+            pltpu.VMEM((count_b * count_c,) + msg, jnp.float32),
             pltpu.SemaphoreType.DMA((count_a,)),
             pltpu.SemaphoreType.DMA((count_a,)),
-            pltpu.SemaphoreType.DMA((count_b,)),
-            pltpu.SemaphoreType.DMA((count_b,)),
-            pltpu.SemaphoreType.DMA((count_c,)),
-            pltpu.SemaphoreType.DMA((count_c,)),
+            pltpu.SemaphoreType.DMA((count_b * count_c,)),
+            pltpu.SemaphoreType.DMA((count_b * count_c,)),
         ],
         compiler_params=pltpu.CompilerParams(collective_id=0, has_side_effects=True),
     )(signal_x, gate_q, gate_k, cotangent, memory, residue, skip_gain)

time: 40.2 us -> 48.1 us (1.20)
  Pallas kernels: 35.9 us -> 43.8 us
    pallas_call x1, Pallas kernels: 34.4 us -> 42.3 us  [per_device(): pl.pallas_call(functools.partial(fused_kernel, (count_a, count_b, count_c...]
where the time goes in v11:
time: 48.1 us; the launch traced here: 47.7 us
  Pallas kernels  43.8 us (91%)
  other arithmetic  1.86 us (4%)
  local copies, waits for them, and re-layouts  1.39 us (3%)
  between operations  0.64 us (1%)
    pallas_call x1, Pallas kernels, per_device(): pl.pallas_call(functools.partial(fused_kernel, (count_a, count_b, count_c...  42.3 us
    pallas_call x1, Pallas kernels, per_device(): pl.pallas_call(output_kernel, out_shape=(half, half, half, half), in_spec...  1.54 us

profile of v11, /device:TPU:1, one launch (start us, length us, event | category | flops | bytes accessed | tf_op | source)
XLA Modules:
  0.0 47.7 jit_solution(4617588528245027012)
XLA Ops:
  0.6 42.3 %shard_map.126 = (f32[2,16,512]{2,1,0:T(8,128)}, f32[2,16,128]{2,1,0:T(8,128)}) custom-call(bf16[16,512]{1,0:T(8,128)(2,1)} %x_ref.3, bf16[16,512]{1,0:T(8,128)(2,1)} %q_ref.3, bf16[16,512]{1,0:T(8,128)(2,1)} %k_ref.3, bf16[16,512]{1,0:T(8,128)(2,1)} %d_ref.3, f32[16]{0:T(128)} %mem_ref.1, f32[16]{0:T(128)} %res_ref.1, f32[16]{0:T(128)} %gain_ref.1), custom_call_target="tpu_custom_call" | custom-call | tf_op jit(solution)/shard_map/pallas_call | solution.py:256
  42.9 0.7 %slice_bitcast_fusion = (f32[16,128]{1,0:T(8,128)S(1)}, f32[16,128]{1,0:T(8,128)S(1)}) fusion(f32[2,16,128]{2,1,0:T(8,128)} %get-tuple-element.18), kind=kLoop, calls=%fused_computation.2 | loop fusion | bytes 32768 | tf_op jit(solution)/shard_map/squeeze | solution.py:278
  43.6 0.0 copy-start
  43.7 0.0 copy-start.1
  43.7 0.7 %copy-done = f32[16]{0:T(128)S(1)} copy-done((f32[16]{0:T(128)S(1)}, f32[16]{0:T(128)}, u32[]{:S(2)}) %copy-start) | copy-done | bytes 88
  44.3 0.0 copy-done.1
  44.3 0.6 %fusion.2 = (f32[16]{0:T(128)}, f32[16]{0:T(128)S(1)}) fusion(f32[16,128]{1,0:T(8,128)S(1)} %get-tuple-element.21, f32[16]{0:T(128)S(1)} %copy-done.1, f32[16]{0:T(128)S(1)} %copy-done), kind=kLoop, calls=%fused_computation.6 | loop fusion | flops 64 | bytes 320 | tf_op jit(solution)/shard_map/mul | solution.py:282
  44.9 0.6 %fusion.4 = f32[16]{0:T(128)} fusion(f32[16]{0:T(128)S(1)} %get-tuple-element.20, f32[16,128]{1,0:T(8,128)S(1)} %get-tuple-element.21), kind=kLoop, calls=%fused_computation.9 | loop fusion | flops 32 | bytes 192 | tf_op jit(solution)/shard_map/mul | solution.py:281
  45.5 1.5 %shard_map.127 = (bf16[16,512]{1,0:T(8,128)(2,1)}, bf16[16,512]{1,0:T(8,128)(2,1)}, bf16[16,512]{1,0:T(8,128)(2,1)}, bf16[16,512]{1,0:T(8,128)(2,1)}) custom-call(bf16[16,512]{1,0:T(8,128)(2,1)} %x_ref.3, bf16[16,512]{1,0:T(8,128)(2,1)} %q_ref.3, bf16[16,512]{1,0:T(8,128)(2,1)} %k_ref.3, bf16[16,512]{1,0:T(8,128)(2,1)} %d_ref.3, ...), custom_call_target="tpu_custom_call" | custom-call | tf_op jit(solution)/shard_map/pallas_call | solution.py:272
  47.0 0.7 %fusion = f32[16]{0:T(128)} fusion(f32[16,128]{1,0:T(8,128)S(1)} %get-tuple-element.22), kind=kLoop, calls=%fused_computation.1 | loop fusion | flops 16 | bytes 128 | tf_op jit(solution)/shard_map/div | solution.py:280
Async XLA Ops:
  43.6 0.7 %copy-start = (f32[16]{0:T(128)S(1)}, f32[16]{0:T(128)}, u32[]{:S(2)}) copy-start(f32[16]{0:T(128)} %mem_ref.1) | copy-start | bytes 196
  43.7 0.7 %copy-start.1 = (f32[16]{0:T(128)S(1)}, f32[16]{0:T(128)}, u32[]{:S(2)}) copy-start(f32[16]{0:T(128)} %res_ref.1) | copy-start | bytes 196

commit v12 on v10

--- a/solution.py
+++ b/solution.py
@@ -222,13 +222,34 @@
     small_ref[1] = sums
 
 
-def output_kernel(x_ref, q_ref, k_ref, d_ref, mix_ref, out_ref, gx_ref, gq_ref, gk_ref):
+def output_kernel(scales, x_ref, q_ref, k_ref, d_ref, mix_ref, small_ref, mem_ref, res_ref,
+                  out_ref, gx_ref, gq_ref, gk_ref, skip_ref, gres_ref, gmem_ref):
     mixed_out = mix_ref[0]
     grad_values = mix_ref[1]
     out_ref[...] = (q_ref[...].astype(jnp.float32) * mixed_out).astype(jnp.bfloat16)
     gx_ref[...] = (grad_values * k_ref[...].astype(jnp.float32)).astype(jnp.bfloat16)
     gq_ref[...] = (d_ref[...].astype(jnp.float32) * mixed_out).astype(jnp.bfloat16)
     gk_ref[...] = (grad_values * x_ref[...].astype(jnp.float32)).astype(jnp.bfloat16)
+    modes = mem_ref.shape[0]
+    channels = small_ref.shape[1]
+    norm_scale, seq_scale = scales
+    mode_of = lax.broadcasted_iota(jnp.int32, (1, LANES), 1) % modes
+    mem_v = jnp.ones((1, LANES), jnp.float32)
+    res_v = jnp.zeros((1, LANES), jnp.float32)
+    for mode in range(modes):
+        mem_v = jnp.where(mode_of == mode, mem_ref[mode], mem_v)
+        res_v = jnp.where(mode_of == mode, res_ref[mode], res_v)
+    gain = jnp.sqrt(2.0 / mem_v)
+    sums = small_ref[1][0:1]
+    grad_res = pltpu.roll(gain * sums * norm_scale, LANES - 5 * modes, 1)
+    grad_mem = pltpu.roll(res_v * gain * sums * norm_scale, LANES - 6 * modes, 1)
+    column = small_ref[0][:, 7 * modes:7 * modes + 1]
+    lane = lax.broadcasted_iota(jnp.int32, (channels, LANES), 1)
+    row = lax.broadcasted_iota(jnp.int32, (channels, LANES), 0)
+    skip = jnp.sum(jnp.where(lane == row, column, 0.0), axis=0, keepdims=True) * seq_scale
+    gres_ref[...] = grad_res[:, 0:modes]
+    gmem_ref[...] = grad_mem[:, 0:modes]
+    skip_ref[...] = skip[:, 0:channels]
 
 
 def per_device(signal_x, gate_q, gate_k, skip_gain, residue, memory, cotangent):
@@ -239,9 +260,6 @@
     count_a = min(GROUP, lax.axis_size("seq"))
     count_b = lax.axis_size("seq") // count_a
     count_c = lax.axis_size("ch")
-    inv_m = 1.0 / memory
-    gain = jnp.sqrt(2.0 / memory)
-    amp = residue * gain
     msg = (channels, LANES)
     vmem = pl.BlockSpec(memory_space=pltpu.VMEM)
     half = jax.ShapeDtypeStruct(signal_x.shape, jnp.bfloat16)
@@ -264,17 +282,18 @@
         ],
         compiler_params=pltpu.CompilerParams(collective_id=0, has_side_effects=True),
     )(signal_x, gate_q, gate_k, cotangent, memory, residue, skip_gain)
-    output, grad_x, grad_q, grad_k = pl.pallas_call(
-        output_kernel,
-        out_shape=(half, half, half, half),
-        in_specs=[vmem] * 5,
-        out_specs=(vmem,) * 4,
-    )(signal_x, gate_q, gate_k, cotangent, mix)
-    total, sums = small[0], small[1]
     norm_scale = 1.0 / math.sqrt(all_channels * seq_total)
-    grad_skip = total[:, 7 * modes] / math.sqrt(seq_total)
-    grad_residue = gain * sums[0, 5 * modes:6 * modes] * norm_scale
-    grad_memory = residue * gain * sums[0, 6 * modes:7 * modes] * norm_scale
+    smem = pl.BlockSpec(memory_space=pltpu.SMEM)
+    output, grad_x, grad_q, grad_k, grad_skip, grad_residue, grad_memory = pl.pallas_call(
+        functools.partial(output_kernel, (norm_scale, 1.0 / math.sqrt(seq_total))),
+        out_shape=(half, half, half, half, jax.ShapeDtypeStruct((1, channels), jnp.float32),
+                   jax.ShapeDtypeStruct((1, modes), jnp.float32), jax.ShapeDtypeStruct((1, modes), jnp.float32)),
+        in_specs=[vmem] * 6 + [smem] * 2,
+        out_specs=(vmem,) * 7,
+    )(signal_x, gate_q, gate_k, cotangent, mix, small, memory, residue)
+    grad_skip = grad_skip.reshape(channels)
+    grad_residue = grad_residue.reshape(modes)
+    grad_memory = grad_memory.reshape(modes)
     return (output, grad_x, grad_q, grad_k, grad_skip, grad_residue, grad_memory)
 
 

time: 40.2 us -> 36.8 us (0.915)
  other arithmetic: 1.86 us -> 0 us
  local copies, waits for them, and re-layouts: 1.39 us -> 0 us
    mul x2 -> x0, other arithmetic: 1.17 us -> none  [the longest x1 0.58 us: per_device(): grad_memory = residue * gain * sums[0, 6 * modes:7 * modes] * norm_scale]
    squeeze x1 -> x0, local copies, waits for them, and re-layouts: 0.72 us -> none  [per_device(): total, sums = (small[0], small[1])]
    div x1 -> x0, other arithmetic: 0.69 us -> none  [per_device(): grad_skip = total[:, 7 * modes] / math.sqrt(seq_total)]
    unnamed x4 -> x0, local copies, waits for them, and re-layouts: 0.67 us -> none
where the time goes in v12:
time: 36.8 us; the launch traced here: 36.6 us
  Pallas kernels  35.9 us (98%)
  between operations  0.64 us (2%)
    pallas_call x1, Pallas kernels, per_device(): pl.pallas_call(functools.partial(fused_kernel, (count_a, count_b, count_c...  34.3 us
    pallas_call x1, Pallas kernels, per_device(): pl.pallas_call(functools.partial(output_kernel, (norm_scale, 1.0 / math.s...  1.58 us

profile of v12, /device:TPU:1, one launch (start us, length us, event | category | flops | bytes accessed | tf_op | source)
XLA Modules:
  0.0 36.6 jit_solution(5754359876191524353)
XLA Ops:
  0.6 34.3 %shard_map.126 = (f32[2,16,512]{2,1,0:T(8,128)}, f32[2,16,128]{2,1,0:T(8,128)}) custom-call(bf16[16,512]{1,0:T(8,128)(2,1)} %x_ref.3, bf16[16,512]{1,0:T(8,128)(2,1)} %q_ref.3, bf16[16,512]{1,0:T(8,128)(2,1)} %k_ref.3, bf16[16,512]{1,0:T(8,128)(2,1)} %d_ref.3, f32[16]{0:T(128)} %mem_ref.3, f32[16]{0:T(128)} %res_ref.3, f32[16]{0:T(128)} %gain_ref.1), custom_call_target="tpu_custom_call" | custom-call | tf_op jit(solution)/shard_map/pallas_call | solution.py:266
  35.0 1.6 %shard_map.127 = (bf16[16,512]{1,0:T(8,128)(2,1)}, bf16[16,512]{1,0:T(8,128)(2,1)}, bf16[16,512]{1,0:T(8,128)(2,1)}, bf16[16,512]{1,0:T(8,128)(2,1)}, f32[1,16]{...) custom-call(bf16[16,512]{1,0:T(8,128)(2,1)} %x_ref.3, bf16[16,512]{1,0:T(8,128)(2,1)} %q_ref.3, bf16[16,512]{1,0:T(8,128)(2,1)} %k_ref.3, ...), custom_call_target="tpu_custom_call" | custom-call | tf_op jit(solution)/shard_map/pallas_call | solution.py:287

commit v13 on v12

--- a/solution.py
+++ b/solution.py
@@ -184,6 +184,9 @@
     skip = jnp.sum(grad_mixed * values, axis=1, keepdims=True)
     state = dot_nn(values, right_v) + dot_nn(grad_mixed, right_g) + jnp.where(slab == 7, skip, local)
     buf_a[0] = state
+    pl.semaphore_wait(barrier, count_a + count_b + count_c - 3)
+
+    descs = start_ring(buf_a, send_a, recv_a, count_a, pos_a, dev_a)
     edge_a_c = slab_coefs(count_a, 1, pos_a, inv, block_len, modes)[4]
     edge_b_c = slab_coefs(count_b, count_a, pos_b, inv, block_len, modes)[4]
     levels_a = level_coefs(count_a, 1, inv, block_len, modes)
@@ -191,18 +194,15 @@
     near_w = jnp.exp(-(pos_a * block_len).astype(jnp.float32) * inv)
     far_w = jnp.exp(-((count_a - 1 - pos_a) * block_len).astype(jnp.float32) * inv)
     join = jnp.where(slab == 0, near_w, jnp.where(slab == 2, far_w, 0.0))
-    pl.semaphore_wait(barrier, count_a + count_b + count_c - 3)
-
-    descs = start_ring(buf_a, send_a, recv_a, count_a, pos_a, dev_a)
     toep = jnp.where(lower, dot_nt(jnp.where(slab == 0, e_down * amp, 0.0), jnp.where(slab == 0, e_up, 0.0)), 0.0)
-    conv = dot_nt(values, toep)
-    corr = dot_nn(grad_mixed, toep)
     into_f = jnp.where(slab == 0, e_next * amp, 0.0)
     into_b = jnp.where(slab == 2, jnp.exp(-(float(block_len) - offs) * inv) * amp, 0.0)
     items = finish_ring(descs, buf_a, count_a, pos_a)
     group, edge_a = fold_items(items, levels_a, edge_a_c, inv, modes)
     buf_b[0] = group
     descs = start_ring(buf_b, send_b, recv_b, count_b, pos_b, dev_b)
+    conv = dot_nt(values, toep)
+    corr = dot_nn(grad_mixed, toep)
     items = finish_ring(descs, buf_b, count_b, pos_b)
     total, edge_b = fold_items(items, levels_b, edge_b_c, inv, modes)
     buf_c[0] = total

time: 36.8 us -> 36.8 us (level)
  no operation moved by 1% of the time
where the time goes in v13:
time: 36.8 us; the launch traced here: 36.6 us
  Pallas kernels  35.9 us (98%)
  between operations  0.64 us (2%)
    pallas_call x1, Pallas kernels, per_device(): pl.pallas_call(functools.partial(fused_kernel, (count_a, count_b, count_c...  34.4 us
    pallas_call x1, Pallas kernels, per_device(): pl.pallas_call(functools.partial(output_kernel, (norm_scale, 1.0 / math.s...  1.58 us

profile of v13, /device:TPU:1, one launch (start us, length us, event | category | flops | bytes accessed | tf_op | source)
XLA Modules:
  0.0 36.6 jit_solution(13730505740707086164)
XLA Ops:
  0.6 34.4 %shard_map.126 = (f32[2,16,512]{2,1,0:T(8,128)}, f32[2,16,128]{2,1,0:T(8,128)}) custom-call(bf16[16,512]{1,0:T(8,128)(2,1)} %x_ref.3, bf16[16,512]{1,0:T(8,128)(2,1)} %q_ref.3, bf16[16,512]{1,0:T(8,128)(2,1)} %k_ref.3, bf16[16,512]{1,0:T(8,128)(2,1)} %d_ref.3, f32[16]{0:T(128)} %mem_ref.3, f32[16]{0:T(128)} %res_ref.3, f32[16]{0:T(128)} %gain_ref.1), custom_call_target="tpu_custom_call" | custom-call | tf_op jit(solution)/shard_map/pallas_call | solution.py:266
  35.0 1.6 %shard_map.127 = (bf16[16,512]{1,0:T(8,128)(2,1)}, bf16[16,512]{1,0:T(8,128)(2,1)}, bf16[16,512]{1,0:T(8,128)(2,1)}, bf16[16,512]{1,0:T(8,128)(2,1)}, f32[1,16]{...) custom-call(bf16[16,512]{1,0:T(8,128)(2,1)} %x_ref.3, bf16[16,512]{1,0:T(8,128)(2,1)} %q_ref.3, bf16[16,512]{1,0:T(8,128)(2,1)} %k_ref.3, ...), custom_call_target="tpu_custom_call" | custom-call | tf_op jit(solution)/shard_map/pallas_call | solution.py:287

commit v14 on v13

--- a/solution.py
+++ b/solution.py
@@ -99,8 +99,6 @@
 def finish_ring(descs, buf, count, pos):
     for desc in descs:
         desc.wait_recv()
-    for desc in descs:
-        desc.wait_send()
     return [buf[(slot - pos + count) % count] for slot in range(count)]
 
 
@@ -187,6 +185,7 @@
     pl.semaphore_wait(barrier, count_a + count_b + count_c - 3)
 
     descs = start_ring(buf_a, send_a, recv_a, count_a, pos_a, dev_a)
+    sent = list(descs)
     edge_a_c = slab_coefs(count_a, 1, pos_a, inv, block_len, modes)[4]
     edge_b_c = slab_coefs(count_b, count_a, pos_b, inv, block_len, modes)[4]
     levels_a = level_coefs(count_a, 1, inv, block_len, modes)
@@ -201,12 +200,14 @@
     group, edge_a = fold_items(items, levels_a, edge_a_c, inv, modes)
     buf_b[0] = group
     descs = start_ring(buf_b, send_b, recv_b, count_b, pos_b, dev_b)
+    sent += descs
     conv = dot_nt(values, toep)
     corr = dot_nn(grad_mixed, toep)
     items = finish_ring(descs, buf_b, count_b, pos_b)
     total, edge_b = fold_items(items, levels_b, edge_b_c, inv, modes)
     buf_c[0] = total
     descs = start_ring(buf_c, send_c, recv_c, count_c, ch_index, dev_c)
+    sent += descs
     edge = join * edge_b + edge_a
     conv = conv + dot_nt(edge, into_f)
     corr = corr + dot_nt(edge, into_b)
@@ -220,6 +221,8 @@
         sums = sums + item
     small_ref[0] = total
     small_ref[1] = sums
+    for desc in sent:
+        desc.wait_send()
 
 
 def output_kernel(scales, x_ref, q_ref, k_ref, d_ref, mix_ref, small_ref, mem_ref, res_ref,

time: 36.8 us -> 36.8 us (level)
  no operation moved by 1% of the time
where the time goes in v14:
time: 36.8 us; the launch traced here: 36.6 us
  Pallas kernels  35.9 us (98%)
  between operations  0.64 us (2%)
    pallas_call x1, Pallas kernels, per_device(): pl.pallas_call(functools.partial(fused_kernel, (count_a, count_b, count_c...  34.4 us
    pallas_call x1, Pallas kernels, per_device(): pl.pallas_call(functools.partial(output_kernel, (norm_scale, 1.0 / math.s...  1.58 us

profile of v14, /device:TPU:1, one launch (start us, length us, event | category | flops | bytes accessed | tf_op | source)
XLA Modules:
  0.0 36.6 jit_solution(18223207226851814921)
XLA Ops:
  0.6 34.4 %shard_map.126 = (f32[2,16,512]{2,1,0:T(8,128)}, f32[2,16,128]{2,1,0:T(8,128)}) custom-call(bf16[16,512]{1,0:T(8,128)(2,1)} %x_ref.3, bf16[16,512]{1,0:T(8,128)(2,1)} %q_ref.3, bf16[16,512]{1,0:T(8,128)(2,1)} %k_ref.3, bf16[16,512]{1,0:T(8,128)(2,1)} %d_ref.3, f32[16]{0:T(128)} %mem_ref.3, f32[16]{0:T(128)} %res_ref.3, f32[16]{0:T(128)} %gain_ref.1), custom_call_target="tpu_custom_call" | custom-call | tf_op jit(solution)/shard_map/pallas_call | solution.py:269
  35.0 1.6 %shard_map.127 = (bf16[16,512]{1,0:T(8,128)(2,1)}, bf16[16,512]{1,0:T(8,128)(2,1)}, bf16[16,512]{1,0:T(8,128)(2,1)}, bf16[16,512]{1,0:T(8,128)(2,1)}, f32[1,16]{...) custom-call(bf16[16,512]{1,0:T(8,128)(2,1)} %x_ref.3, bf16[16,512]{1,0:T(8,128)(2,1)} %q_ref.3, bf16[16,512]{1,0:T(8,128)(2,1)} %k_ref.3, ...), custom_call_target="tpu_custom_call" | custom-call | tf_op jit(solution)/shard_map/pallas_call | solution.py:290

commit v15 on v14

--- a/solution.py
+++ b/solution.py
@@ -82,7 +82,7 @@
 
 def start_ring(buf, send_sems, recv_sems, count, pos, device_of):
     descs = []
-    for dist in range(1, count):
+    for dist in sorted(range(1, count), key=lambda d: -min(d, count - d)):
         desc = pltpu.make_async_remote_copy(
             src_ref=buf.at[0],
             dst_ref=buf.at[count - dist],

time: 36.8 us -> 36.4 us (0.989)
  Pallas kernels: 35.9 us -> 35.5 us
    pallas_call x1, Pallas kernels: 34.4 us -> 34 us  [per_device(): pl.pallas_call(functools.partial(fused_kernel, (count_a, count_b, count_c...]
where the time goes in v15:
time: 36.4 us; the launch traced here: 36.2 us
  Pallas kernels  35.5 us (98%)
  between operations  0.64 us (2%)
    pallas_call x1, Pallas kernels, per_device(): pl.pallas_call(functools.partial(fused_kernel, (count_a, count_b, count_c...  34 us
    pallas_call x1, Pallas kernels, per_device(): pl.pallas_call(functools.partial(output_kernel, (norm_scale, 1.0 / math.s...  1.58 us

profile of v15, /device:TPU:1, one launch (start us, length us, event | category | flops | bytes accessed | tf_op | source)
XLA Modules:
  0.0 36.2 jit_solution(8029107407212516929)
XLA Ops:
  0.6 34.0 %shard_map.126 = (f32[2,16,512]{2,1,0:T(8,128)}, f32[2,16,128]{2,1,0:T(8,128)}) custom-call(bf16[16,512]{1,0:T(8,128)(2,1)} %x_ref.3, bf16[16,512]{1,0:T(8,128)(2,1)} %q_ref.3, bf16[16,512]{1,0:T(8,128)(2,1)} %k_ref.3, bf16[16,512]{1,0:T(8,128)(2,1)} %d_ref.3, f32[16]{0:T(128)} %mem_ref.3, f32[16]{0:T(128)} %res_ref.3, f32[16]{0:T(128)} %gain_ref.1), custom_call_target="tpu_custom_call" | custom-call | tf_op jit(solution)/shard_map/pallas_call | solution.py:269
  34.6 1.6 %shard_map.127 = (bf16[16,512]{1,0:T(8,128)(2,1)}, bf16[16,512]{1,0:T(8,128)(2,1)}, bf16[16,512]{1,0:T(8,128)(2,1)}, bf16[16,512]{1,0:T(8,128)(2,1)}, f32[1,16]{...) custom-call(bf16[16,512]{1,0:T(8,128)(2,1)} %x_ref.3, bf16[16,512]{1,0:T(8,128)(2,1)} %q_ref.3, bf16[16,512]{1,0:T(8,128)(2,1)} %k_ref.3, ...), custom_call_target="tpu_custom_call" | custom-call | tf_op jit(solution)/shard_map/pallas_call | solution.py:290

commit v16 on v15

--- a/solution.py
+++ b/solution.py
@@ -136,8 +136,8 @@
         return (seq_index, other)
 
     barrier = pltpu.get_barrier_semaphore()
-    for count, pos, device_of in ((count_a, pos_a, dev_a), (count_b, pos_b, dev_b), (count_c, ch_index, dev_c)):
-        for dist in range(1, count):
+    for count, pos, device_of in ((count_b, pos_b, dev_b), (count_a, pos_a, dev_a), (count_c, ch_index, dev_c)):
+        for dist in sorted(range(1, count), key=lambda d: -min(d, count - d)):
             pl.semaphore_signal(barrier, inc=1, device_id=device_of((pos + dist) % count),
                                 device_id_type=pl.DeviceIdType.MESH)
 

time: 36.4 us -> 36.5 us (level)
  no operation moved by 1% of the time
where the time goes in v16:
time: 36.5 us; the launch traced here: 36.3 us
  Pallas kernels  35.7 us (98%)
  between operations  0.64 us (2%)
    pallas_call x1, Pallas kernels, per_device(): pl.pallas_call(functools.partial(fused_kernel, (count_a, count_b, count_c...  34.1 us
    pallas_call x1, Pallas kernels, per_device(): pl.pallas_call(functools.partial(output_kernel, (norm_scale, 1.0 / math.s...  1.58 us

profile of v16, /device:TPU:1, one launch (start us, length us, event | category | flops | bytes accessed | tf_op | source)
XLA Modules:
  0.0 36.3 jit_solution(9122143769332658604)
XLA Ops:
  0.6 34.1 %shard_map.126 = (f32[2,16,512]{2,1,0:T(8,128)}, f32[2,16,128]{2,1,0:T(8,128)}) custom-call(bf16[16,512]{1,0:T(8,128)(2,1)} %x_ref.3, bf16[16,512]{1,0:T(8,128)(2,1)} %q_ref.3, bf16[16,512]{1,0:T(8,128)(2,1)} %k_ref.3, bf16[16,512]{1,0:T(8,128)(2,1)} %d_ref.3, f32[16]{0:T(128)} %mem_ref.3, f32[16]{0:T(128)} %res_ref.3, f32[16]{0:T(128)} %gain_ref.1), custom_call_target="tpu_custom_call" | custom-call | tf_op jit(solution)/shard_map/pallas_call | solution.py:269
  34.7 1.6 %shard_map.127 = (bf16[16,512]{1,0:T(8,128)(2,1)}, bf16[16,512]{1,0:T(8,128)(2,1)}, bf16[16,512]{1,0:T(8,128)(2,1)}, bf16[16,512]{1,0:T(8,128)(2,1)}, f32[1,16]{...) custom-call(bf16[16,512]{1,0:T(8,128)(2,1)} %x_ref.3, bf16[16,512]{1,0:T(8,128)(2,1)} %q_ref.3, bf16[16,512]{1,0:T(8,128)(2,1)} %k_ref.3, ...), custom_call_target="tpu_custom_call" | custom-call | tf_op jit(solution)/shard_map/pallas_call | solution.py:290

commit v17 on v15

--- a/solution.py
+++ b/solution.py
@@ -118,7 +118,7 @@
 
 def fused_kernel(counts, modes, x_ref, q_ref, k_ref, d_ref, mem_ref, res_ref, gain_ref,
                  mix_ref, small_ref,
-                 buf_a, buf_b, buf_c, send_a, recv_a, send_b, recv_b, send_c, recv_c):
+                 buf_a, buf_b, buf_d, buf_c, send_a, recv_a, send_b, recv_b, send_d, recv_d, send_c, recv_c):
     count_a, count_b, count_c = counts
     channels, block_len = x_ref.shape
     seq_index = lax.axis_index("seq")
@@ -129,14 +129,22 @@
     def dev_a(other):
         return (pos_b * count_a + other, ch_index)
 
+    count_d = count_b // 2
+    pos_x = pos_b % 2
+    pos_y = pos_b // 2
+
     def dev_b(other):
-        return (other * count_a + pos_a, ch_index)
+        return ((pos_y * 2 + other) * count_a + pos_a, ch_index)
+
+    def dev_d(other):
+        return ((other * 2 + pos_x) * count_a + pos_a, ch_index)
 
     def dev_c(other):
         return (seq_index, other)
 
     barrier = pltpu.get_barrier_semaphore()
-    for count, pos, device_of in ((count_a, pos_a, dev_a), (count_b, pos_b, dev_b), (count_c, ch_index, dev_c)):
+    for count, pos, device_of in ((count_a, pos_a, dev_a), (2, pos_x, dev_b), (count_d, pos_y, dev_d),
+                                  (count_c, ch_index, dev_c)):
         for dist in range(1, count):
             pl.semaphore_signal(barrier, inc=1, device_id=device_of((pos + dist) % count),
                                 device_id_type=pl.DeviceIdType.MESH)
@@ -182,14 +190,19 @@
     skip = jnp.sum(grad_mixed * values, axis=1, keepdims=True)
     state = dot_nn(values, right_v) + dot_nn(grad_mixed, right_g) + jnp.where(slab == 7, skip, local)
     buf_a[0] = state
-    pl.semaphore_wait(barrier, count_a + count_b + count_c - 3)
+    pl.semaphore_wait(barrier, count_a + 2 + count_d + count_c - 4)
 
     descs = start_ring(buf_a, send_a, recv_a, count_a, pos_a, dev_a)
     sent = list(descs)
     edge_a_c = slab_coefs(count_a, 1, pos_a, inv, block_len, modes)[4]
-    edge_b_c = slab_coefs(count_b, count_a, pos_b, inv, block_len, modes)[4]
+    edge_b_c = slab_coefs(2, count_a, pos_x, inv, block_len, modes)[4]
+    edge_d_c = slab_coefs(count_d, 2 * count_a, pos_y, inv, block_len, modes)[4]
     levels_a = level_coefs(count_a, 1, inv, block_len, modes)
-    levels_b = level_coefs(count_b, count_a, inv, block_len, modes)
+    levels_b = level_coefs(2, count_a, inv, block_len, modes)
+    levels_d = level_coefs(count_d, 2 * count_a, inv, block_len, modes)
+    near_x = jnp.exp(-(pos_x * count_a * block_len).astype(jnp.float32) * inv)
+    far_x = jnp.exp(-((1 - pos_x) * count_a * block_len).astype(jnp.float32) * inv)
+    join_x = jnp.where(slab == 0, near_x, jnp.where(slab == 2, far_x, 0.0))
     near_w = jnp.exp(-(pos_a * block_len).astype(jnp.float32) * inv)
     far_w = jnp.exp(-((count_a - 1 - pos_a) * block_len).astype(jnp.float32) * inv)
     join = jnp.where(slab == 0, near_w, jnp.where(slab == 2, far_w, 0.0))
@@ -199,12 +212,18 @@
     items = finish_ring(descs, buf_a, count_a, pos_a)
     group, edge_a = fold_items(items, levels_a, edge_a_c, inv, modes)
     buf_b[0] = group
-    descs = start_ring(buf_b, send_b, recv_b, count_b, pos_b, dev_b)
+    descs = start_ring(buf_b, send_b, recv_b, 2, pos_x, dev_b)
     sent += descs
     conv = dot_nt(values, toep)
+    items = finish_ring(descs, buf_b, 2, pos_x)
+    pair_sum, edge_x = fold_items(items, levels_b, edge_b_c, inv, modes)
+    buf_d[0] = pair_sum
+    descs = start_ring(buf_d, send_d, recv_d, count_d, pos_y, dev_d)
+    sent += descs
     corr = dot_nn(grad_mixed, toep)
-    items = finish_ring(descs, buf_b, count_b, pos_b)
-    total, edge_b = fold_items(items, levels_b, edge_b_c, inv, modes)
+    items = finish_ring(descs, buf_d, count_d, pos_y)
+    total, edge_y = fold_items(items, levels_d, edge_d_c, inv, modes)
+    edge_b = join_x * edge_y + edge_x
     buf_c[0] = total
     descs = start_ring(buf_c, send_c, recv_c, count_c, ch_index, dev_c)
     sent += descs
@@ -274,12 +293,15 @@
         out_specs=(vmem,) * 2,
         scratch_shapes=[
             pltpu.VMEM((count_a,) + msg, jnp.float32),
-            pltpu.VMEM((count_b,) + msg, jnp.float32),
+            pltpu.VMEM((2,) + msg, jnp.float32),
+            pltpu.VMEM((count_b // 2,) + msg, jnp.float32),
             pltpu.VMEM((count_c,) + msg, jnp.float32),
             pltpu.SemaphoreType.DMA((count_a,)),
             pltpu.SemaphoreType.DMA((count_a,)),
-            pltpu.SemaphoreType.DMA((count_b,)),
-            pltpu.SemaphoreType.DMA((count_b,)),
+            pltpu.SemaphoreType.DMA((2,)),
+            pltpu.SemaphoreType.DMA((2,)),
+            pltpu.SemaphoreType.DMA((count_b // 2,)),
+            pltpu.SemaphoreType.DMA((count_b // 2,)),
             pltpu.SemaphoreType.DMA((count_c,)),
             pltpu.SemaphoreType.DMA((count_c,)),
         ],

time: 36.4 us -> 38.5 us (1.058)
  Pallas kernels: 35.5 us -> 37.6 us
    pallas_call x1, Pallas kernels: 34 us -> 36 us  [per_device(): pl.pallas_call(functools.partial(fused_kernel, (count_a, count_b, count_c...]
where the time goes in v17:
time: 38.5 us; the launch traced here: 38.2 us
  Pallas kernels  37.6 us (98%)
  between operations  0.64 us (2%)
    pallas_call x1, Pallas kernels, per_device(): pl.pallas_call(functools.partial(fused_kernel, (count_a, count_b, count_c...  36 us
    pallas_call x1, Pallas kernels, per_device(): pl.pallas_call(functools.partial(output_kernel, (norm_scale, 1.0 / math.s...  1.58 us

profile of v17, /device:TPU:1, one launch (start us, length us, event | category | flops | bytes accessed | tf_op | source)
XLA Modules:
  0.0 38.2 jit_solution(6269491543901595744)
XLA Ops:
  0.6 36.0 %shard_map.126 = (f32[2,16,512]{2,1,0:T(8,128)}, f32[2,16,128]{2,1,0:T(8,128)}) custom-call(bf16[16,512]{1,0:T(8,128)(2,1)} %x_ref.3, bf16[16,512]{1,0:T(8,128)(2,1)} %q_ref.3, bf16[16,512]{1,0:T(8,128)(2,1)} %k_ref.3, bf16[16,512]{1,0:T(8,128)(2,1)} %d_ref.3, f32[16]{0:T(128)} %mem_ref.3, f32[16]{0:T(128)} %res_ref.3, f32[16]{0:T(128)} %gain_ref.1), custom_call_target="tpu_custom_call" | custom-call | tf_op jit(solution)/shard_map/pallas_call | solution.py:288
  36.7 1.6 %shard_map.127 = (bf16[16,512]{1,0:T(8,128)(2,1)}, bf16[16,512]{1,0:T(8,128)(2,1)}, bf16[16,512]{1,0:T(8,128)(2,1)}, bf16[16,512]{1,0:T(8,128)(2,1)}, f32[1,16]{...) custom-call(bf16[16,512]{1,0:T(8,128)(2,1)} %x_ref.3, bf16[16,512]{1,0:T(8,128)(2,1)} %q_ref.3, bf16[16,512]{1,0:T(8,128)(2,1)} %k_ref.3, ...), custom_call_target="tpu_custom_call" | custom-call | tf_op jit(solution)/shard_map/pallas_call | solution.py:312

commit v18 on v15

--- a/solution.py
+++ b/solution.py
@@ -15,7 +15,7 @@
     return jnp.einsum(pattern, left_op, right_op, precision=HIGH_PREC)
 
 
-GROUP = 8
+GROUP = 16
 LANES = 128
 SLABS = 8
 

time: 36.4 us -> 37.8 us (1.038)
  Pallas kernels: 35.5 us -> 36.9 us
    pallas_call x1, Pallas kernels: 34 us -> 35.3 us  [per_device(): pl.pallas_call(functools.partial(fused_kernel, (count_a, count_b, count_c...]
where the time goes in v18:
time: 37.8 us; the launch traced here: 37.5 us
  Pallas kernels  36.9 us (98%)
  between operations  0.64 us (2%)
    pallas_call x1, Pallas kernels, per_device(): pl.pallas_call(functools.partial(fused_kernel, (count_a, count_b, count_c...  35.3 us
    pallas_call x1, Pallas kernels, per_device(): pl.pallas_call(functools.partial(output_kernel, (norm_scale, 1.0 / math.s...  1.58 us

profile of v18, /device:TPU:1, one launch (start us, length us, event | category | flops | bytes accessed | tf_op | source)
XLA Modules:
  0.0 37.5 jit_solution(9599843905329124913)
XLA Ops:
  0.6 35.3 %shard_map.126 = (f32[2,16,512]{2,1,0:T(8,128)}, f32[2,16,128]{2,1,0:T(8,128)}) custom-call(bf16[16,512]{1,0:T(8,128)(2,1)} %x_ref.3, bf16[16,512]{1,0:T(8,128)(2,1)} %q_ref.3, bf16[16,512]{1,0:T(8,128)(2,1)} %k_ref.3, bf16[16,512]{1,0:T(8,128)(2,1)} %d_ref.3, f32[16]{0:T(128)} %mem_ref.3, f32[16]{0:T(128)} %res_ref.3, f32[16]{0:T(128)} %gain_ref.1), custom_call_target="tpu_custom_call" | custom-call | tf_op jit(solution)/shard_map/pallas_call | solution.py:269
  35.9 1.6 %shard_map.127 = (bf16[16,512]{1,0:T(8,128)(2,1)}, bf16[16,512]{1,0:T(8,128)(2,1)}, bf16[16,512]{1,0:T(8,128)(2,1)}, bf16[16,512]{1,0:T(8,128)(2,1)}, f32[1,16]{...) custom-call(bf16[16,512]{1,0:T(8,128)(2,1)} %x_ref.3, bf16[16,512]{1,0:T(8,128)(2,1)} %q_ref.3, bf16[16,512]{1,0:T(8,128)(2,1)} %k_ref.3, ...), custom_call_target="tpu_custom_call" | custom-call | tf_op jit(solution)/shard_map/pallas_call | solution.py:290
